TPU v7x, 128 devices: a whole 4x4x4 slice. The times are simulated.
128 devices in a mesh: tm: 8 (over x, core), ctx: 16 (over y, z).
Axes of the slice: x: 4, y: 4, z: 4, core: 2. Of those that a mesh axis runs over, the one named last changes fastest.
Arguments:
- iterate: float32 [8, 2688, 1536], P('tm', 'ctx'), may hold values from -6 to 6
- anchor: float32 [2688, 1536], P('ctx'), may hold values from -6 to 6
- frame_index: int32 [2688], P('ctx'), may hold values from 0 to 15, never falling along the last dimension, each value on 1 to 336 neighbouring positions
- noise_steps: int32 [8, 16], P('tm'), may hold values from 0 to 11
- qkv_weight: bfloat16 [1536, 4608], replicated, may hold values from -0.15625 to 0.15625
- out_weight: bfloat16 [1536, 1536], replicated, may hold values from -0.15625 to 0.15625
- mod_weight: bfloat16 [256, 4608], replicated, may hold values from -0.375 to 0.375
Outputs:
- updated: float32 [8, 2688, 1536], P('tm', 'ctx')
Inputs may be any that keep to these rules, and one draw needn't show every extreme that they name: `frame_index`: frame numbers never fall along the sequence; each of the 16 frames holds 1 to 336 tokens.
All inputs are finite; a program needn't handle non-finite values.
Results may differ from a plain program's by a relative error of at most 0.00051.
Values may be sent and summed in bfloat16 or wider, within the bound.
No kernel may reach another device: no remote copies, remote signals or barrier semaphores. Data moves between devices by JAX's collectives and lax.ppermute only.
A program may use at most 192 MiB of HBM per device.

v0:
```python
import functools
import math

import jax
import jax.numpy as jnp
from jax import lax
from jax.experimental import pallas as pl
from jax.experimental.pallas import tpu as pltpu
from jax.sharding import PartitionSpec as P


HD = 128
NSCHED = 12
NF = 16
D = 1536
ROWS = 168
PACK = 176
WIDE = 384
PAIR = 2 * ROWS
PAIRPACK = PAIR + 8
QROWS = 4 * ROWS
HALF = D // 2
BIG = 131072.0
AXES = ("tm", "ctx")

shift_factor = 5.0
norm_eps = 1e-06
F32 = jnp.float32
BF16 = jnp.bfloat16
VM = pl.BlockSpec(memory_space=pltpu.VMEM)
SM = pl.BlockSpec(memory_space=pltpu.SMEM)
ANY = pl.BlockSpec(memory_space=pl.ANY)
HBM = pl.BlockSpec(memory_space=pltpu.HBM)


def shaped(*shape, kind=F32):
    return jax.ShapeDtypeStruct(shape, kind)


def call(kernel, args, specs, outs, cost, scratch=(), mib=24, out_specs=None):
    flops, moved, exps = cost
    return run_kernel(kernel, args, specs, outs, flops, moved, exps, scratch, mib, out_specs)


def run_kernel(kernel, args, specs, outs, flops, moved, exps, scratch, mib, out_specs):
    return pl.pallas_call(
        kernel,
        in_specs=specs,
        out_specs=[VM] * len(outs) if out_specs is None else out_specs,
        out_shape=outs,
        scratch_shapes=list(scratch),
        compiler_params=pltpu.CompilerParams(vmem_limit_bytes=mib << 20),
        cost_estimate=pl.CostEstimate(flops=flops, bytes_accessed=moved, transcendentals=exps),
    )(*args)


def place_of(x, c, y, z):
    return ((x % 4) * 2 + c % 2) * 16 + (y % 4) * 4 + z % 4


def pairs(move):
    found = []
    for x in range(4):
        for c in range(2):
            for y in range(4):
                for z in range(4):
                    to = move(x, c, y, z)
                    if to is not None:
                        found.append((place_of(x, c, y, z), place_of(*to)))
    return found


def along(ring, step):
    def move(x, c, y, z):
        if (c == 0) == (ring == "a"):
            return (x, c, y + step, z)
        return (x, c, y, z + step)

    return pairs(move)


def send(value, route):
    return lax.ppermute(value, AXES, route)


def noise_level(level_index):
    fraction = level_index / NSCHED
    return shift_factor * fraction / (1.0 + (shift_factor - 1.0) * fraction)


def frame_features(steps_row):
    level_float = steps_row.astype(F32)
    upper = noise_level(level_float + 1.0)
    lower = noise_level(level_float)
    half_freq = 128
    rates = jnp.exp(-math.log(10000.0) * jnp.arange(half_freq, dtype=F32) / half_freq)
    angles = (1000.0 * upper)[:, None] * rates[None, :]
    features = jnp.concatenate([jnp.cos(angles), jnp.sin(angles)], axis=1).astype(BF16)
    return features, upper - lower


def split3(value):
    high = value.astype(BF16)
    rest = value - high.astype(F32)
    mid = rest.astype(BF16)
    low = (rest - mid.astype(F32)).astype(BF16)
    return jnp.concatenate([high, mid, low], axis=0)


def ones_by_frame(frame_row, rows):
    level = lax.broadcasted_iota(jnp.int32, (128, 256), 0)
    here = jnp.broadcast_to(frame_row, (128, 256))
    hit = jnp.where(jnp.logical_and(level % NF == here, level < rows), 1.0, 0.0)
    return hit.T[:ROWS]


def pick_rows(ones, table):
    return jnp.dot(ones[:, : 3 * NF], split3(table), preferred_element_type=F32)


def norm_kernel(latent_hbm, frame_ref, feat_ref, mod_hbm, out_ref, lat_ref, mod_ref, picked_ref, sems):
    copies = [
        pltpu.make_async_copy(mod_hbm.at[:, pl.ds(i * D, D)], mod_ref.at[i], sems.at[i])
        for i in range(2)
    ]
    copies.append(pltpu.make_async_copy(latent_hbm, lat_ref, sems.at[2]))
    for one in copies:
        one.start()
    ones = ones_by_frame(frame_ref[...], 3 * NF).astype(BF16)
    for half in range(2):
        copies[half].wait()
        table = jnp.dot(feat_ref[...], mod_ref[half], preferred_element_type=F32)
        picked_ref[:, pl.ds(half * D, D)] = pick_rows(ones, table)
    copies[2].wait()

    def block(i, carry):
        rows = pl.ds(pl.multiple_of(i * 24, 8), 24)
        latent = lat_ref[rows, :]
        center = latent - jnp.mean(latent, axis=-1, keepdims=True)
        spread = jnp.mean(center * center, axis=-1, keepdims=True)
        normal = center * lax.rsqrt(spread + norm_eps)
        out = normal * (1.0 + picked_ref[rows, D:]) + picked_ref[rows, :D]
        out_ref[rows, :] = out.astype(BF16)
        return carry

    lax.fori_loop(0, ROWS // 24, block, 0)
    out_ref[ROWS:, :] = jnp.zeros((PACK - ROWS, D), BF16)
    out_ref[ROWS:, :256] = jnp.broadcast_to(frame_ref[...], (8, 256)).astype(F32).astype(BF16)


def normed_pack(latent, frame_row, features, mod_weight):
    return call(
        norm_kernel,
        (latent, frame_row, features, mod_weight),
        [HBM, VM, VM, HBM],
        [shaped(PACK, D, kind=BF16)],
        (30000000, 4000000, 0),
        [
            pltpu.VMEM((ROWS, D), F32),
            pltpu.VMEM((2, 256, D), BF16),
            pltpu.VMEM((ROWS, 2 * D), F32),
            pltpu.SemaphoreType.DMA((3,)),
        ],
        mib=24,
    )[0]


def side_kernel(
    where_ref,
    after_hbm,
    latent_hbm,
    frame_ref,
    gap_ref,
    feat_ref,
    mod_hbm,
    qkv_hbm,
    keep_ref,
    give_ref,
    gate_ref,
    w_ref,
    lat_ref,
    mod_ref,
    sems,
):
    place, core = where_ref[0], where_ref[1]
    copies = [
        pltpu.make_async_copy(mod_hbm.at[:, pl.ds(2 * D, D)], mod_ref, sems.at[0]),
        pltpu.make_async_copy(latent_hbm, lat_ref, sems.at[1]),
    ]
    for i in range(3):
        cols = pl.ds(pl.multiple_of(i * D + place * WIDE, 128), WIDE)
        copies.append(
            pltpu.make_async_copy(
                qkv_hbm.at[:, cols], w_ref.at[:, pl.ds(i * WIDE, WIDE)], sems.at[2 + i]
            )
        )
    for one in copies:
        one.start()
    ones = ones_by_frame(frame_ref[...], 3 * NF)
    gap = jnp.sum(ones[:, :NF] * gap_ref[:, :NF], axis=1, keepdims=True)
    copies[0].wait()
    table = jnp.dot(feat_ref[...], mod_ref[...], preferred_element_type=F32)
    gate_ref[...] = -gap * pick_rows(ones.astype(BF16), table)
    copies[1].wait()
    mine = pl.ds(pl.multiple_of(core * HALF, 128), HALF)
    other = pl.ds(pl.multiple_of((1 - core) * HALF, 128), HALF)
    keep_ref[...] = -gap * lat_ref[:, mine]
    give_ref[...] = -gap * lat_ref[:, other]
    for one in copies[2:]:
        one.wait()


def side_terms(where, after, latent, frame_row, gap, features, mod_weight, qkv_weight):
    return call(
        side_kernel,
        (where, after, latent, frame_row, gap, features, mod_weight, qkv_weight),
        [SM, ANY, HBM, VM, VM, VM, HBM, HBM],
        [
            shaped(ROWS, HALF),
            shaped(ROWS, HALF),
            shaped(ROWS, D),
            shaped(D, 3 * WIDE, kind=BF16),
        ],
        (30000000, 6000000, 0),
        [
            pltpu.VMEM((ROWS, D), F32),
            pltpu.VMEM((256, D), BF16),
            pltpu.SemaphoreType.DMA((5,)),
        ],
        mib=24,
    )


def head_normed(one):
    mean = jnp.mean(one * one, axis=-1, keepdims=True)
    return (one * lax.rsqrt(mean + norm_eps)).astype(BF16)


def qkv_kernel(n_after, *refs):
    n0, n1, w_ref, q_ref, kv_ref, tok_ref = refs[n_after:]
    tok_ref[:ROWS, :] = n0[:ROWS, :]
    tok_ref[ROWS:, :] = n1[:ROWS, :]
    tokens = tok_ref[...]
    for h in range(3):
        cols = pl.ds(h * WIDE, WIDE)
        got = jnp.dot(tokens, w_ref[:, cols], preferred_element_type=F32)
        if h == 2:
            kv_ref[:PAIR, WIDE:] = got.astype(BF16)
            continue
        target = q_ref if h == 0 else kv_ref
        for i in range(3):
            part = pl.ds(i * HD, HD)
            target[:PAIR, part] = head_normed(got[:, i * HD : (i + 1) * HD])
    kv_ref[PAIR:, :256] = n0[ROWS:, :256]
    kv_ref[PAIR:, 256:512] = n1[ROWS:, :256]
    kv_ref[PAIR:, 512:] = jnp.zeros((8, 256), BF16)


def project(n0, n1, weight, after=()):
    return call(
        functools.partial(qkv_kernel, len(after)),
        (*after, n0, n1, weight),
        [ANY] * len(after) + [VM] * 3,
        [shaped(PAIR, WIDE, kind=BF16), shaped(PAIRPACK, 2 * WIDE, kind=BF16)],
        (2 * PAIR * D * 3 * WIDE, 5000000, 0),
        [pltpu.VMEM((PAIR, D), BF16)],
    )


def lanes_to_rows(pack_ref, put, make):
    for i in range(2):
        here = pack_ref[PAIR : PAIR + 1, i * 256 : (i + 1) * 256].astype(F32)
        level = lax.broadcasted_iota(jnp.int32, (HD, 256), 0).astype(F32)
        put(i, make(level, here).T[:ROWS].astype(BF16))


def attend_kernel(n_after, n_kv, first, last, row0, nrows, *refs):
    refs = list(refs)[n_after:]
    if first:
        q0, q1, kvs, rest = refs[0], refs[1], refs[2 : 2 + n_kv], refs[2 + n_kv :]
        num_ref, den_ref, qx_ref, key_ref, val_ref = rest
        for j, (q_ref, kv_ref) in enumerate(((q0, kvs[0]), (q1, kvs[1]))):
            rows = pl.ds(j * PAIR, PAIR)
            for h in range(3):
                qx_ref[rows, pl.ds(h * 256, HD)] = q_ref[:, pl.ds(h * HD, HD)]

            def put(i, block):
                at = pl.ds(j * PAIR + i * ROWS, ROWS)
                for h in range(3):
                    qx_ref[at, pl.ds(h * 256 + HD, HD)] = block

            lanes_to_rows(kv_ref, put, lambda level, here: jnp.where(level > here, -BIG, 0.0))
    else:
        qx_ref, num_in, den_in, kvs, rest = refs[0], refs[1], refs[2], refs[3 : 3 + n_kv], refs[3 + n_kv :]
        if last:
            outs, (key_ref, val_ref) = rest[:-2], rest[-2:]
        else:
            num_ref, den_ref, key_ref, val_ref = rest

    for j, kv_ref in enumerate(kvs):
        rows = pl.ds(j * PAIR, PAIR)
        for h in range(3):
            key_ref[rows, pl.ds(h * 256, HD)] = kv_ref[:PAIR, pl.ds(h * HD, HD)]
        val_ref[rows, :] = kv_ref[:PAIR, WIDE:]

        def put(i, block):
            at = pl.ds(j * PAIR + i * ROWS, ROWS)
            for h in range(3):
                key_ref[at, pl.ds(h * 256 + HD, HD)] = block

        lanes_to_rows(kv_ref, put, lambda level, here: jnp.where(level == here, 1.0, 0.0))

    scale = HD**-0.5 * math.log2(math.e)
    rows = pl.ds(row0, nrows)
    dens = []
    for h in range(3):
        cols = pl.ds(h * HD, HD)
        wide = pl.ds(h * 256, 256)
        scores = lax.dot_general(
            qx_ref[rows, wide], key_ref[:, wide], (((1,), (1,)), ((), ())),
            preferred_element_type=F32,
        )
        weights = jnp.exp2(scores * scale)
        den = jnp.sum(weights, axis=1, keepdims=True)
        num = jnp.dot(weights.astype(BF16), val_ref[:, cols], preferred_element_type=F32)
        if not first:
            num = num + num_in[rows, cols]
            den = den + den_in[rows, h : h + 1]
        if last:
            done = (num / den).astype(BF16)
            for i, out_ref in enumerate(outs):
                out_ref[:, cols] = done[i * ROWS : (i + 1) * ROWS]
        else:
            num_ref[:, cols] = num
            dens.append(den)
    if not last:
        lane = lax.broadcasted_iota(jnp.int32, (QROWS, HD), 1)
        den_ref[...] = jnp.where(lane == 0, dens[0], jnp.where(lane == 1, dens[1], dens[2]))


def attend(kvs, queries=None, state=None, last=None, after=()):
    n_kv = len(kvs)
    first = state is None
    row0, nrows = (0, QROWS) if last is None else last
    args = (list(queries) if first else list(state)) + list(kvs)
    if last is None:
        outs = [shaped(QROWS, WIDE), shaped(QROWS, HD)]
        if first:
            outs.append(shaped(QROWS, 768, kind=BF16))
    else:
        outs = [shaped(ROWS, WIDE, kind=BF16)] * (nrows // ROWS)
    got = call(
        functools.partial(attend_kernel, len(after), n_kv, first, last is not None, row0, nrows),
        list(after) + args,
        [ANY] * len(after) + [VM] * len(args),
        outs,
        (4 * nrows * PAIR * n_kv * WIDE * 2, 2000000, nrows * PAIR * 3 * n_kv),
        [
            pltpu.VMEM((n_kv * PAIR, 768), BF16),
            pltpu.VMEM((n_kv * PAIR, WIDE), BF16),
        ],
    )
    if last is not None:
        return got
    return (got[2] if first else state[0], got[0], got[1])


def out_rows(where_ref, step):
    return pl.ds(pl.multiple_of(lax.rem(where_ref[0] + step, 4) * WIDE, 128), WIDE)


def out_first_kernel(where_ref, a_ref, w_ref, part_ref):
    part_ref[...] = jnp.dot(a_ref[...], w_ref[out_rows(where_ref, 0), :], preferred_element_type=F32)


def out_first(where, piece, out_weight):
    return call(
        out_first_kernel,
        (where, piece, out_weight),
        [SM, VM, VM],
        [shaped(ROWS, D)],
        (2 * ROWS * WIDE * D, 5000000, 0),
    )[0]


def out_rest_kernel(own, where_ref, after_ref, part_ref, a1, a2, a3, w_ref, gate_ref, term_ref):
    core = where_ref[1]
    half = core if own else 1 - core
    cols = pl.ds(pl.multiple_of(half * HALF, 128), HALF)
    branch = part_ref[:, cols]
    for piece, step in ((a1, 1), (a2, 3), (a3, 2)):
        weight = w_ref[out_rows(where_ref, step), cols]
        branch = branch + jnp.dot(piece[...], weight, preferred_element_type=F32)
    term_ref[...] = gate_ref[:, cols] * branch


def out_rest(own, where, after, part, pieces, out_weight, gate):
    return call(
        functools.partial(out_rest_kernel, own),
        (where, after, part, *pieces, out_weight, gate),
        [SM, ANY] + [VM] * 6,
        [shaped(ROWS, HALF)],
        (ROWS * 3 * WIDE * D, 5000000, 0),
    )[0]


def add_kernel(a_ref, b_ref, after_ref, out_ref, wire_ref):
    total = a_ref[...] + b_ref[...].astype(F32)
    out_ref[...] = total
    wire_ref[...] = total.astype(wire_ref.dtype)


def add_up(a, b, wire, after):
    return call(
        add_kernel,
        (a, b, after),
        [VM, VM, ANY],
        [shaped(ROWS, HALF), shaped(ROWS, HALF, kind=wire)],
        (ROWS * HALF, 2000000, 0),
    )


def before_sum(where_ref, got_ref, far_ref):
    chip = where_ref[2]
    near = jnp.where(lax.rem(chip, 2) == 1, got_ref[...].astype(F32), 0.0)
    return near + jnp.where(chip >= 2, far_ref[...].astype(F32), 0.0)


def back_kernel(where_ref, after_ref, keep_ref, got_ref, far_ref, out_ref):
    extra = jnp.where(where_ref[1] == 0, keep_ref[...], 0.0)
    out_ref[...] = before_sum(where_ref, got_ref, far_ref) + extra


def back_sum(where, after, keep, got, far):
    return call(
        back_kernel,
        (where, after, keep, got, far),
        [SM, ANY] + [VM] * 3,
        [shaped(ROWS, HALF)],
        (ROWS * HALF, 2000000, 0),
    )[0]


def join_kernel(where_ref, base_ref, keep_ref, give_ref, beside_ref, got_ref, far_ref, back_ref, out_ref):
    core = where_ref[1]
    mine = pl.ds(pl.multiple_of(core * HALF, 128), HALF)
    other = pl.ds(pl.multiple_of((1 - core) * HALF, 128), HALF)
    own = before_sum(where_ref, got_ref, far_ref) + jnp.where(core == 1, beside_ref[...], 0.0)
    out_ref[:, mine] = base_ref[:, mine] + (keep_ref[...] + own)
    out_ref[:, other] = base_ref[:, other] + (give_ref[...] + back_ref[...])


def join(where, base, keep, give, beside, got, far, back):
    return call(
        join_kernel,
        (where, base, keep, give, beside, got, far, back),
        [SM] + [VM] * 7,
        [shaped(ROWS, D)],
        (ROWS * D * 2, 4000000, 0),
    )[0]


SWAP = pairs(lambda x, c, y, z: (x, 1 - c, y, z))
ROUND1 = pairs(lambda x, c, y, z: (x ^ 1, c, y, z))
ROUND2 = pairs(lambda x, c, y, z: (3 - x, c, y, z) if x < 2 else None)


def held(x):
    return pltpu.with_memory_space_constraint(x, pltpu.HBM)


def per_device(iterate, anchor, frame_index, noise_steps, qkv_weight, out_weight, mod_weight):
    qkv_weight, mod_weight = held(qkv_weight), held(mod_weight)
    tm = lax.axis_index("tm")
    ctx = lax.axis_index("ctx")
    chip, core = tm // 2, tm % 2
    place = jnp.where(core == 0, ctx // 4, ctx % 4)
    where = jnp.stack([place, core, chip]).astype(jnp.int32)
    latent = held(iterate[0])
    features, gap = frame_features(noise_steps[0])
    gap = jnp.pad(gap, (0, 128 - NF))[None, :]
    frame_row = jnp.pad(frame_index, (0, 256 - ROWS))[None, :]

    mine = normed_pack(latent, frame_row, features, mod_weight)
    from_prev = send(mine, along("a", 1))
    from_next = send(mine, along("a", -1))
    from_far = send(mine, along("a", 2))
    lat_keep, lat_give, gate, weight = side_terms(
        where, mine, latent, frame_row, gap, features, mod_weight, qkv_weight
    )
    lat_beside = send(lat_give, SWAP)

    q0, kv0 = project(mine, from_prev, weight)
    up0 = send(kv0, along("b", 1))
    down0 = send(kv0, along("b", -1))
    lat_both, lat_wire = add_up(lat_keep, lat_beside, F32, kv0)
    lat_got = send(lat_wire, ROUND1)
    q1, kv1 = project(from_next, from_far, weight, after=(kv0, lat_wire))
    down1 = send(kv1, along("b", -1))
    up1 = send(kv1, along("b", 1))
    far0 = send(up0, along("b", 1))
    state = attend([kv0, kv1], queries=(q0, q1))
    state = attend([up0, down0], state=state)
    far1 = send(down1, along("b", -1))
    _, lat_wire = add_up(lat_both, lat_got, F32, state[1])
    lat_far = send(lat_wire, ROUND2)
    state = attend([up1, down1], state=state, after=(lat_wire,))
    a1, a2, a3 = attend([far0, far1], state=state, last=(ROWS, 3 * ROWS))
    b3 = send(a3, along("a", -2))
    b1 = send(a1, along("a", -1))
    b2 = send(a2, along("a", 1))
    (a0,) = attend([far0, far1], state=state, last=(0, ROWS), after=(a1,))
    lat_sum = back_sum(where, a0, lat_keep, lat_got, lat_far)
    lat_back = send(lat_sum, SWAP)
    part = out_first(where, a0, out_weight)
    base = join(where, anchor, lat_keep, lat_give, lat_beside, lat_got, lat_far, lat_back)
    pieces = (b1, b2, b3)
    give = out_rest(False, where, base, part, pieces, out_weight, gate)
    beside = send(give, SWAP)
    keep = out_rest(True, where, give, part, pieces, out_weight, gate)
    both, wire = add_up(keep, beside, BF16, keep)
    got = send(wire, ROUND1)
    _, wire = add_up(both, got, BF16, keep)
    far = send(wire, ROUND2)
    back = send(back_sum(where, far, keep, got, far), SWAP)
    return join(where, base, keep, give, beside, got, far, back)[None]


def solution(mesh):
    placed = (P("tm", "ctx", None), P("ctx", None), P("ctx"), P("tm", None), P(), P(), P())

    return jax.shard_map(
        per_device, mesh=mesh, in_specs=placed, out_specs=P("tm", "ctx", None), check_vma=False
    )
```

profile of v0, /device:TPU:7, one launch (start us, length us, event | category | flops | bytes accessed | tf_op | source)
XLA Modules:
  0.0 99.4 jit_solution(6606328954620334124)
XLA Ops:
  1.5 3.5 %shard_map.73.after_hbm.refs_0_ = bf16[176,1536]{1,0:T(8,128)(2,1)S(1)} custom-call(f32[168,1536]{1,0:T(8,128)} %bitcast.16, s32[1,256]{1,0:T(1,128)S(1)} %bitcast.14, bf16[16,256]{1,0:T(8,128)(2,1)S(1)} %pad_maximum_fusion.feat_ref, bf16[256,4608]{1,0:T(8,128)(2,1)} %mod_hbm.3), custom_call_target="tpu_custom_call" | custom-call | flops 30000000 | bytes 4000000 | tf_op jit(solution)/shard_map/pallas_call | solution.py:46
  6.7 2.2 %collective-permute-start.3 = (bf16[176,1536]{1,0:T(8,128)(2,1)S(1)}, bf16[176,1536]{1,0:T(8,128)(2,1)S(1)}, u32[]{:S(2)}, u32[]{:S(2)}) collective-permute-start(bf16[176,1536]{1,0:T(8,128)(2,1)S(1)} %shard_map.73.after_hbm.refs_0_), channel_id=1, source_target_pairs={{0,12},{1,13},{2,14},{3,15},{4,0},{5,1},{6,2},{7,3},{8,4},{9,5},{1... | collective-permute-start | bytes 1622024 | tf_op jit(solution)/shard_map/ppermute | solution.py:83
  10.2 3.1 %shard_map.74 = (f32[168,768]{1,0:T(8,128)S(1)}, f32[168,768]{1,0:T(8,128)S(1)}, f32[168,1536]{1,0:T(8,128)S(1)}, bf16[1536,1152]{1,0:T(8,128)(2,1)S(1)}) custom-call(s32[3]{0:T(128)S(1)} %pad_add_fusion.where_ref, bf16[176,1536]{1,0:T(8,128)(2,1)S(1)} %shard_map.73.after_hbm.refs_0_, f32[168,1536]{1,0:T(8,128)} %bitcast.17, s32[1,256]{1,0:T(1,128)S(1)} %bitcast.15, ...), custom_call_target="tpu_custom_call" | custom-call | flops 30000000 | bytes 6000000 | tf_op jit(solution)/shard_map/pallas_call | solution.py:46
  15.8 1.8 %shard_map.75 = (bf16[336,384]{1,0:T(8,128)(2,1)S(1)}, bf16[344,768]{1,0:T(8,128)(2,1)S(1)}) custom-call(bf16[176,1536]{1,0:T(8,128)(2,1)S(1)} %shard_map.73.after_hbm.refs_0_, bf16[176,1536]{1,0:T(8,128)(2,1)S(1)} %collective-permute-done.1.refs_1_, bf16[1536,1152]{1,0:T(8,128)(2,1)S(1)} %get-tuple-element.31.refs_2_.refs_4_), custom_call_target="tpu_custom_call" | custom-call | flops 1189085184 | bytes 5000000 | tf_op jit(solution)/shard_map/pallas_call | solution.py:46
  17.7 3.2 %collective-permute-done.3.refs_2_ = bf16[176,1536]{1,0:T(8,128)(2,1)S(1)} collective-permute-done((bf16[176,1536]{1,0:T(8,128)(2,1)S(1)}, bf16[176,1536]{1,0:T(8,128)(2,1)S(1)}, u32[]{:S(2)}, u32[]{:S(2)}) %collective-permute-start.3) | collective-permute-done | bytes 540704 | tf_op jit(solution)/shard_map/ppermute | solution.py:83
  21.0 1.8 %collective-permute-done.4.refs_3_ = bf16[176,1536]{1,0:T(8,128)(2,1)S(1)} collective-permute-done((bf16[176,1536]{1,0:T(8,128)(2,1)S(1)}, bf16[176,1536]{1,0:T(8,128)(2,1)S(1)}, u32[]{:S(2)}, u32[]{:S(2)}) %collective-permute-start.4) | collective-permute-done | bytes 540704 | tf_op jit(solution)/shard_map/ppermute | solution.py:83
  22.8 1.8 %shard_map.77 = (bf16[336,384]{1,0:T(8,128)(2,1)S(1)}, bf16[344,768]{1,0:T(8,128)(2,1)S(1)}) custom-call(bf16[344,768]{1,0:T(8,128)(2,1)S(1)} %get-tuple-element.32.after_ref.refs_0_.refs_2_, f32[168,768]{1,0:T(8,128)S(1)} %get-tuple-element.33.refs_1_, bf16[176,1536]{1,0:T(8,128)(2,1)S(1)} %collective-permute-done.3.refs_2_, ...), custom_call_target="tpu_custom_call" | custom-call | flops 1189085184 | bytes 5000000 | tf_op jit(solution)/shard_map/pallas_call | solution.py:46
  24.6 2.5 %collective-permute-start.9 = (bf16[344,768]{1,0:T(8,128)(2,1)S(1)}, bf16[344,768]{1,0:T(8,128)(2,1)S(1)}, u32[]{:S(2)}, u32[]{:S(2)}) collective-permute-start(bf16[344,768]{1,0:T(8,128)(2,1)S(1)} %get-tuple-element.37.refs_3_), channel_id=1, source_target_pairs={{0,3},{1,0},{2,1},{3,2},{4,7},{5,4},{6,5},{7,6},{8,11},{9,8},{10,9... | collective-permute-start | bytes 1585160 | tf_op jit(solution)/shard_map/ppermute | solution.py:83
  27.1 2.7 %collective-permute-start.6 = (bf16[344,768]{1,0:T(8,128)(2,1)S(1)}, bf16[344,768]{1,0:T(8,128)(2,1)S(1)}, u32[]{:S(2)}, u32[]{:S(2)}) collective-permute-start(bf16[344,768]{1,0:T(8,128)(2,1)S(1)} %get-tuple-element.32.after_ref.refs_0_.refs_2_), channel_id=1, source_target_pairs={{0,3},{1,0},{2,1},{3,2},{4,7},{5,4},{6,5},{7,6},{8,11},{9,8},{10,9... | collective-permute-start | bytes 1585160 | tf_op jit(solution)/shard_map/ppermute | solution.py:83
  30.3 2.9 %collective-permute-done.9.refs_5_ = bf16[344,768]{1,0:T(8,128)(2,1)S(1)} collective-permute-done((bf16[344,768]{1,0:T(8,128)(2,1)S(1)}, bf16[344,768]{1,0:T(8,128)(2,1)S(1)}, u32[]{:S(2)}, u32[]{:S(2)}) %collective-permute-start.9) | collective-permute-done | bytes 528416 | tf_op jit(solution)/shard_map/ppermute | solution.py:83
  33.3 3.4 %collective-permute-start.11 = (bf16[344,768]{1,0:T(8,128)(2,1)S(1)}, bf16[344,768]{1,0:T(8,128)(2,1)S(1)}, u32[]{:S(2)}, u32[]{:S(2)}) collective-permute-start(bf16[344,768]{1,0:T(8,128)(2,1)S(1)} %collective-permute-done.9.refs_5_), channel_id=1, source_target_pairs={{0,3},{1,0},{2,1},{3,2},{4,7},{5,4},{6,5},{7,6},{8,11},{9,8},{10,9... | collective-permute-start | bytes 1585160 | tf_op jit(solution)/shard_map/ppermute | solution.py:83
  36.7 2.1 %shard_map.78 = (f32[672,384]{1,0:T(8,128)S(1)}, f32[672,128]{1,0:T(8,128)S(1)}, bf16[672,768]{1,0:T(8,128)(2,1)S(1)}) custom-call(bf16[336,384]{1,0:T(8,128)(2,1)S(1)} %get-tuple-element.35.refs_0_, bf16[336,384]{1,0:T(8,128)(2,1)S(1)} %get-tuple-element.36.refs_1_, bf16[344,768]{1,0:T(8,128)(2,1)S(1)} %get-tuple-element.32.after_ref.refs_0_.refs_2_, ...), custom_call_target="tpu_custom_call" | custom-call | flops 1387266048 | bytes 2000000 | tf_op jit(solution)/shard_map/pallas_call | solution.py:46
  39.0 3.3 %shard_map.79 = (f32[672,384]{1,0:T(8,128)S(1)}, f32[672,128]{1,0:T(8,128)S(1)}) custom-call(bf16[672,768]{1,0:T(8,128)(2,1)S(1)} %get-tuple-element.38.refs_0_.refs_1_, f32[672,384]{1,0:T(8,128)S(1)} %get-tuple-element.39.refs_1_, f32[672,128]{1,0:T(8,128)S(1)} %get-tuple-element.40.refs_2_, bf16[344,768]{1,0:T(8,128)(2,1)S(1)} %collective-permute-done.5.refs_3_, ...), custom_call_target="tpu_custom_call" | custom-call | flops 1387266048 | bytes 2000000 | tf_op jit(solution)/shard_map/pallas_call | solution.py:46
  44.4 3.3 %shard_map.81 = (f32[672,384]{1,0:T(8,128)S(1)}, f32[672,128]{1,0:T(8,128)S(1)}) custom-call(f32[168,768]{1,0:T(8,128)S(1)} %get-tuple-element.42.refs_0_, bf16[672,768]{1,0:T(8,128)(2,1)S(1)} %get-tuple-element.38.refs_0_.refs_1_, f32[672,384]{1,0:T(8,128)S(1)} %get-tuple-element.41.after_ref.refs_2_, f32[672,128]{1,0:T(8,128)S(1)} %get-tuple-element.43.refs_3_, ...), custom_call_target="tpu_custom_call" | custom-call | flops 1387266048 | bytes 2000000 | tf_op jit(solution)/shard_map/pallas_call | solution.py:46
  48.0 2.3 %shard_map.82 = (bf16[168,384]{1,0:T(8,128)(2,1)S(1)}, bf16[168,384]{1,0:T(8,128)(2,1)S(1)}, bf16[168,384]{1,0:T(8,128)(2,1)S(1)}) custom-call(bf16[672,768]{1,0:T(8,128)(2,1)S(1)} %get-tuple-element.38.refs_0_.refs_1_, f32[672,384]{1,0:T(8,128)S(1)} %get-tuple-element.44.refs_1_.refs_2_, f32[672,128]{1,0:T(8,128)S(1)} %get-tuple-element.45.refs_2_.refs_3_, ...), custom_call_target="tpu_custom_call" | custom-call | flops 1040449536 | bytes 2000000 | tf_op jit(solution)/shard_map/pallas_call | solution.py:46
  51.5 5.2 %collective-permute-done.7.far_ref = f32[168,768]{1,0:T(8,128)S(1)} collective-permute-done((f32[168,768]{1,0:T(8,128)S(1)}, f32[168,768]{1,0:T(8,128)S(1)}, u32[]{:S(2)}, u32[]{:S(2)}) %collective-permute-start.7) | collective-permute-done | bytes 516128 | tf_op jit(solution)/shard_map/ppermute | solution.py:83
  57.3 3.8 %collective-permute-start.12 = (f32[168,768]{1,0:T(8,128)S(1)}, f32[168,768]{1,0:T(8,128)S(1)}, u32[]{:S(2)}, u32[]{:S(2)}) collective-permute-start(f32[168,768]{1,0:T(8,128)S(1)} %shard_map.84), channel_id=1, source_target_pairs={{0,16},{1,17},{2,18},{3,19},{4,20},{5,21},{6,22},{7,23},{8,24},{9,... | collective-permute-start | bytes 1548296 | tf_op jit(solution)/shard_map/ppermute | solution.py:83
  61.1 2.2 %collective-permute-start.13 = (bf16[168,384]{1,0:T(8,128)(2,1)S(1)}, bf16[168,384]{1,0:T(8,128)(2,1)S(1)}, u32[]{:S(2)}, u32[]{:S(2)}) collective-permute-start(bf16[168,384]{1,0:T(8,128)(2,1)S(1)} %get-tuple-element.46.refs_0_), channel_id=1, source_target_pairs={{0,12},{1,13},{2,14},{3,15},{4,0},{5,1},{6,2},{7,3},{8,4},{9,5},{1... | collective-permute-start | bytes 387080 | tf_op jit(solution)/shard_map/ppermute | solution.py:83
  63.4 2.1 %collective-permute-start.15 = (bf16[168,384]{1,0:T(8,128)(2,1)S(1)}, bf16[168,384]{1,0:T(8,128)(2,1)S(1)}, u32[]{:S(2)}, u32[]{:S(2)}) collective-permute-start(bf16[168,384]{1,0:T(8,128)(2,1)S(1)} %get-tuple-element.48), channel_id=1, source_target_pairs={{0,8},{1,9},{2,10},{3,11},{4,12},{5,13},{6,14},{7,15},{8,0},{9,1},... | collective-permute-start | bytes 387080 | tf_op jit(solution)/shard_map/ppermute | solution.py:83
  67.4 2.7 %collective-permute-done.14.a2 = bf16[168,384]{1,0:T(8,128)(2,1)S(1)} collective-permute-done((bf16[168,384]{1,0:T(8,128)(2,1)S(1)}, bf16[168,384]{1,0:T(8,128)(2,1)S(1)}, u32[]{:S(2)}, u32[]{:S(2)}) %collective-permute-start.14) | collective-permute-done | bytes 129056 | tf_op jit(solution)/shard_map/ppermute | solution.py:83
  71.2 2.5 %collective-permute-start.16 = (f32[168,768]{1,0:T(8,128)S(1)}, f32[168,768]{1,0:T(8,128)S(1)}, u32[]{:S(2)}, u32[]{:S(2)}) collective-permute-start(f32[168,768]{1,0:T(8,128)S(1)} %shard_map.87.after_ref.give_ref), channel_id=1, source_target_pairs={{0,16},{1,17},{2,18},{3,19},{4,20},{5,21},{6,22},{7,23},{8,24},{9,... | collective-permute-start | bytes 1548296 | tf_op jit(solution)/shard_map/ppermute | solution.py:83
  75.4 7.4 %collective-permute-done.17.b_ref.got_ref = bf16[168,768]{1,0:T(8,128)(2,1)S(1)} collective-permute-done((bf16[168,768]{1,0:T(8,128)(2,1)S(1)}, bf16[168,768]{1,0:T(8,128)(2,1)S(1)}, u32[]{:S(2)}, u32[]{:S(2)}) %collective-permute-start.17) | collective-permute-done | bytes 258080 | tf_op jit(solution)/shard_map/ppermute | solution.py:83
  84.9 8.4 %collective-permute-done.18.after_ref.far_ref = bf16[168,768]{1,0:T(8,128)(2,1)S(1)} collective-permute-done((bf16[168,768]{1,0:T(8,128)(2,1)S(1)}, bf16[168,768]{1,0:T(8,128)(2,1)S(1)}, u32[]{:S(2)}, u32[]{:S(2)}) %collective-permute-start.18) | collective-permute-done | bytes 258080 | tf_op jit(solution)/shard_map/ppermute | solution.py:83
  93.9 2.2 %collective-permute-start.19 = (f32[168,768]{1,0:T(8,128)S(1)}, f32[168,768]{1,0:T(8,128)S(1)}, u32[]{:S(2)}, u32[]{:S(2)}) collective-permute-start(f32[168,768]{1,0:T(8,128)S(1)} %shard_map.91), channel_id=1, source_target_pairs={{0,16},{1,17},{2,18},{3,19},{4,20},{5,21},{6,22},{7,23},{8,24},{9,... | collective-permute-start | bytes 1548296 | tf_op jit(solution)/shard_map/ppermute | solution.py:83
  (51 shorter events, 22.7 us)
Async XLA Ops:
  5.0 10.9 %collective-permute-start.1 = (bf16[176,1536]{1,0:T(8,128)(2,1)S(1)}, bf16[176,1536]{1,0:T(8,128)(2,1)S(1)}, u32[]{:S(2)}, u32[]{:S(2)}) collective-permute-start(bf16[176,1536]{1,0:T(8,128)(2,1)S(1)} %shard_map.73.after_hbm.refs_0_), channel_id=1, source_target_pairs={{0,4},{1,5},{2,6},{3,7},{4,8},{5,9},{6,10},{7,11},{8,12},{9,13},{1... | collective-permute-start | bytes 1622024 | tf_op jit(solution)/shard_map/ppermute | solution.py:83
  6.7 14.3 %collective-permute-start.3 = (bf16[176,1536]{1,0:T(8,128)(2,1)S(1)}, bf16[176,1536]{1,0:T(8,128)(2,1)S(1)}, u32[]{:S(2)}, u32[]{:S(2)}) collective-permute-start(bf16[176,1536]{1,0:T(8,128)(2,1)S(1)} %shard_map.73.after_hbm.refs_0_), channel_id=1, source_target_pairs={{0,12},{1,13},{2,14},{3,15},{4,0},{5,1},{6,2},{7,3},{8,4},{9,5},{1... | collective-permute-start | bytes 1622024 | tf_op jit(solution)/shard_map/ppermute | solution.py:83
  8.9 13.9 %collective-permute-start.4 = (bf16[176,1536]{1,0:T(8,128)(2,1)S(1)}, bf16[176,1536]{1,0:T(8,128)(2,1)S(1)}, u32[]{:S(2)}, u32[]{:S(2)}) collective-permute-start(bf16[176,1536]{1,0:T(8,128)(2,1)S(1)} %shard_map.73.after_hbm.refs_0_), channel_id=1, source_target_pairs={{0,8},{1,9},{2,10},{3,11},{4,12},{5,13},{6,14},{7,15},{8,0},{9,1},... | collective-permute-start | bytes 1622024 | tf_op jit(solution)/shard_map/ppermute | solution.py:83
  13.3 4.3 %collective-permute-start = (f32[168,768]{1,0:T(8,128)S(1)}, f32[168,768]{1,0:T(8,128)S(1)}, u32[]{:S(2)}, u32[]{:S(2)}) collective-permute-start(f32[168,768]{1,0:T(8,128)S(1)} %get-tuple-element.30.give_ref), channel_id=1, source_target_pairs={{0,16},{1,17},{2,18},{3,19},{4,20},{5,21},{6,22},{7,23},{8,24},{9,... | collective-permute-start | bytes 1548296 | tf_op jit(solution)/shard_map/ppermute | solution.py:83
  24.6 8.7 %collective-permute-start.9 = (bf16[344,768]{1,0:T(8,128)(2,1)S(1)}, bf16[344,768]{1,0:T(8,128)(2,1)S(1)}, u32[]{:S(2)}, u32[]{:S(2)}) collective-permute-start(bf16[344,768]{1,0:T(8,128)(2,1)S(1)} %get-tuple-element.37.refs_3_), channel_id=1, source_target_pairs={{0,3},{1,0},{2,1},{3,2},{4,7},{5,4},{6,5},{7,6},{8,11},{9,8},{10,9... | collective-permute-start | bytes 1585160 | tf_op jit(solution)/shard_map/ppermute | solution.py:83
  27.1 9.6 %collective-permute-start.5 = (bf16[344,768]{1,0:T(8,128)(2,1)S(1)}, bf16[344,768]{1,0:T(8,128)(2,1)S(1)}, u32[]{:S(2)}, u32[]{:S(2)}) collective-permute-start(bf16[344,768]{1,0:T(8,128)(2,1)S(1)} %get-tuple-element.32.after_ref.refs_0_.refs_2_), channel_id=1, source_target_pairs={{0,1},{1,2},{2,3},{3,0},{4,5},{5,6},{6,7},{7,4},{8,9},{9,10},{10,1... | collective-permute-start | bytes 1585160 | tf_op jit(solution)/shard_map/ppermute | solution.py:83
  27.1 11.8 %collective-permute-start.6 = (bf16[344,768]{1,0:T(8,128)(2,1)S(1)}, bf16[344,768]{1,0:T(8,128)(2,1)S(1)}, u32[]{:S(2)}, u32[]{:S(2)}) collective-permute-start(bf16[344,768]{1,0:T(8,128)(2,1)S(1)} %get-tuple-element.32.after_ref.refs_0_.refs_2_), channel_id=1, source_target_pairs={{0,3},{1,0},{2,1},{3,2},{4,7},{5,4},{6,5},{7,6},{8,11},{9,8},{10,9... | collective-permute-start | bytes 1585160 | tf_op jit(solution)/shard_map/ppermute | solution.py:83
  29.8 12.5 %collective-permute-start.2 = (f32[168,768]{1,0:T(8,128)S(1)}, f32[168,768]{1,0:T(8,128)S(1)}, u32[]{:S(2)}, u32[]{:S(2)}) collective-permute-start(f32[168,768]{1,0:T(8,128)S(1)} %get-tuple-element.33.refs_1_), channel_id=1, source_target_pairs={{0,32},{1,33},{2,34},{3,35},{4,36},{5,37},{6,38},{7,39},{8,40},{9,... | collective-permute-start | bytes 1548296 | tf_op jit(solution)/shard_map/ppermute | solution.py:83
  30.3 14.1 %collective-permute-start.8 = (bf16[344,768]{1,0:T(8,128)(2,1)S(1)}, bf16[344,768]{1,0:T(8,128)(2,1)S(1)}, u32[]{:S(2)}, u32[]{:S(2)}) collective-permute-start(bf16[344,768]{1,0:T(8,128)(2,1)S(1)} %get-tuple-element.37.refs_3_), channel_id=1, source_target_pairs={{0,1},{1,2},{2,3},{3,0},{4,5},{5,6},{6,7},{7,4},{8,9},{9,10},{10,1... | collective-permute-start | bytes 1585160 | tf_op jit(solution)/shard_map/ppermute | solution.py:83
  33.3 14.4 %collective-permute-start.11 = (bf16[344,768]{1,0:T(8,128)(2,1)S(1)}, bf16[344,768]{1,0:T(8,128)(2,1)S(1)}, u32[]{:S(2)}, u32[]{:S(2)}) collective-permute-start(bf16[344,768]{1,0:T(8,128)(2,1)S(1)} %collective-permute-done.9.refs_5_), channel_id=1, source_target_pairs={{0,3},{1,0},{2,1},{3,2},{4,7},{5,4},{6,5},{7,6},{8,11},{9,8},{10,9... | collective-permute-start | bytes 1585160 | tf_op jit(solution)/shard_map/ppermute | solution.py:83
  36.7 11.3 %collective-permute-start.10 = (bf16[344,768]{1,0:T(8,128)(2,1)S(1)}, bf16[344,768]{1,0:T(8,128)(2,1)S(1)}, u32[]{:S(2)}, u32[]{:S(2)}) collective-permute-start(bf16[344,768]{1,0:T(8,128)(2,1)S(1)} %collective-permute-done.5.refs_3_), channel_id=1, source_target_pairs={{0,1},{1,2},{2,3},{3,0},{4,5},{5,6},{6,7},{7,4},{8,9},{9,10},{10,1... | collective-permute-start | bytes 1585160 | tf_op jit(solution)/shard_map/ppermute | solution.py:83
  43.1 13.5 %collective-permute-start.7 = (f32[168,768]{1,0:T(8,128)S(1)}, f32[168,768]{1,0:T(8,128)S(1)}, u32[]{:S(2)}, u32[]{:S(2)}) collective-permute-start(f32[168,768]{1,0:T(8,128)S(1)} %get-tuple-element.42.refs_0_), channel_id=1, source_target_pairs={{0,96},{1,97},{2,98},{3,99},{4,100},{5,101},{6,102},{7,103},{8,104... | collective-permute-start | bytes 1548296 | tf_op jit(solution)/shard_map/ppermute | solution.py:83
  44.4 21.1 %slice-start = ((s8[4718592]{0:T(1024)(128)(4,1)}), s8[4194304]{0:T(1024)(128)(4,1)S(1)}, s32[]{:S(2)}) async-start(s8[4718592]{0:T(1024)(128)(4,1)} %bitcast.12), calls=%async_computation | async-start | bytes 8388608
  48.0 17.5 %slice-start.1 = ((s8[4718592]{0:T(1024)(128)(4,1)}), s8[524288]{0:T(1024)(128)(4,1)S(1)}, s32[]{:S(2)}) async-start(s8[4718592]{0:T(1024)(128)(4,1)} %bitcast.12), calls=%async_computation.1 | async-start | bytes 1048576
  51.5 15.0 %copy-start = (f32[168,1536]{1,0:T(8,128)S(1)}, f32[168,1536]{1,0:T(8,128)}, u32[]{:S(2)}) copy-start(f32[168,1536]{1,0:T(8,128)} %base_ref.1) | copy-start | bytes 3096580
  57.3 9.1 %collective-permute-start.12 = (f32[168,768]{1,0:T(8,128)S(1)}, f32[168,768]{1,0:T(8,128)S(1)}, u32[]{:S(2)}, u32[]{:S(2)}) collective-permute-start(f32[168,768]{1,0:T(8,128)S(1)} %shard_map.84), channel_id=1, source_target_pairs={{0,16},{1,17},{2,18},{3,19},{4,20},{5,21},{6,22},{7,23},{8,24},{9,... | collective-permute-start | bytes 1548296 | tf_op jit(solution)/shard_map/ppermute | solution.py:83
  61.1 6.2 %collective-permute-start.13 = (bf16[168,384]{1,0:T(8,128)(2,1)S(1)}, bf16[168,384]{1,0:T(8,128)(2,1)S(1)}, u32[]{:S(2)}, u32[]{:S(2)}) collective-permute-start(bf16[168,384]{1,0:T(8,128)(2,1)S(1)} %get-tuple-element.46.refs_0_), channel_id=1, source_target_pairs={{0,12},{1,13},{2,14},{3,15},{4,0},{5,1},{6,2},{7,3},{8,4},{9,5},{1... | collective-permute-start | bytes 387080 | tf_op jit(solution)/shard_map/ppermute | solution.py:83
  63.4 6.7 %collective-permute-start.14 = (bf16[168,384]{1,0:T(8,128)(2,1)S(1)}, bf16[168,384]{1,0:T(8,128)(2,1)S(1)}, u32[]{:S(2)}, u32[]{:S(2)}) collective-permute-start(bf16[168,384]{1,0:T(8,128)(2,1)S(1)} %get-tuple-element.47), channel_id=1, source_target_pairs={{0,4},{1,5},{2,6},{3,7},{4,8},{5,9},{6,10},{7,11},{8,12},{9,13},{1... | collective-permute-start | bytes 387080 | tf_op jit(solution)/shard_map/ppermute | solution.py:83
  63.4 6.7 %collective-permute-start.15 = (bf16[168,384]{1,0:T(8,128)(2,1)S(1)}, bf16[168,384]{1,0:T(8,128)(2,1)S(1)}, u32[]{:S(2)}, u32[]{:S(2)}) collective-permute-start(bf16[168,384]{1,0:T(8,128)(2,1)S(1)} %get-tuple-element.48), channel_id=1, source_target_pairs={{0,8},{1,9},{2,10},{3,11},{4,12},{5,13},{6,14},{7,15},{8,0},{9,1},... | collective-permute-start | bytes 387080 | tf_op jit(solution)/shard_map/ppermute | solution.py:83
  71.2 4.0 %collective-permute-start.16 = (f32[168,768]{1,0:T(8,128)S(1)}, f32[168,768]{1,0:T(8,128)S(1)}, u32[]{:S(2)}, u32[]{:S(2)}) collective-permute-start(f32[168,768]{1,0:T(8,128)S(1)} %shard_map.87.after_ref.give_ref), channel_id=1, source_target_pairs={{0,16},{1,17},{2,18},{3,19},{4,20},{5,21},{6,22},{7,23},{8,24},{9,... | collective-permute-start | bytes 1548296 | tf_op jit(solution)/shard_map/ppermute | solution.py:83
  75.3 7.5 %collective-permute-start.17 = (bf16[168,768]{1,0:T(8,128)(2,1)S(1)}, bf16[168,768]{1,0:T(8,128)(2,1)S(1)}, u32[]{:S(2)}, u32[]{:S(2)}) collective-permute-start(bf16[168,768]{1,0:T(8,128)(2,1)S(1)} %get-tuple-element.50), channel_id=1, source_target_pairs={{0,32},{1,33},{2,34},{3,35},{4,36},{5,37},{6,38},{7,39},{8,40},{9,... | collective-permute-start | bytes 774152 | tf_op jit(solution)/shard_map/ppermute | solution.py:83
  83.6 9.6 %collective-permute-start.18 = (bf16[168,768]{1,0:T(8,128)(2,1)S(1)}, bf16[168,768]{1,0:T(8,128)(2,1)S(1)}, u32[]{:S(2)}, u32[]{:S(2)}) collective-permute-start(bf16[168,768]{1,0:T(8,128)(2,1)S(1)} %get-tuple-element.52), channel_id=1, source_target_pairs={{0,96},{1,97},{2,98},{3,99},{4,100},{5,101},{6,102},{7,103},{8,104... | collective-permute-start | bytes 774152 | tf_op jit(solution)/shard_map/ppermute | solution.py:83
  93.9 3.7 %collective-permute-start.19 = (f32[168,768]{1,0:T(8,128)S(1)}, f32[168,768]{1,0:T(8,128)S(1)}, u32[]{:S(2)}, u32[]{:S(2)}) collective-permute-start(f32[168,768]{1,0:T(8,128)S(1)} %shard_map.91), channel_id=1, source_target_pairs={{0,16},{1,17},{2,18},{3,19},{4,20},{5,21},{6,22},{7,23},{8,24},{9,... | collective-permute-start | bytes 1548296 | tf_op jit(solution)/shard_map/ppermute | solution.py:83
where the time goes:
time: 99.6 us; the launch traced here: 99.4 us
  waiting for transfers between devices  35.5 us (36%)
  Pallas kernels  31.4 us (32%)
  starting transfers between devices  30.6 us (31%)
    ppermute x20, waiting for transfers between devices, send(): return lax.ppermute(value, AXES, route)  35.5 us
    pallas_call x20, Pallas kernels, run_kernel(): pl.pallas_call(kernel, in_specs=specs, out_specs=[VM] * len(outs) if out_...  31.4 us
    ppermute x20, starting transfers between devices, send(): return lax.ppermute(value, AXES, route)  30.6 us
  transfers between devices with their start and end apart: 20, of which 12 were waited for; matrix products, arithmetic and copies ran while one was open for 0% of the time, Pallas kernels for 21%

commit v1 on v0

--- a/solution.py
+++ b/solution.py
@@ -153,81 +153,70 @@
         norm_kernel,
         (latent, frame_row, features, mod_weight),
         [HBM, VM, VM, HBM],
-        [shaped(PACK, D, kind=BF16)],
+        [shaped(PACK, D, kind=BF16), shaped(ROWS, D)],
         (30000000, 4000000, 0),
         [
-            pltpu.VMEM((ROWS, D), F32),
             pltpu.VMEM((2, 256, D), BF16),
             pltpu.VMEM((ROWS, 2 * D), F32),
             pltpu.SemaphoreType.DMA((3,)),
         ],
-        mib=24,
-    )[0]
+    )
+
+
+def frame_gap(ones, gap_ref):
+    return jnp.sum(ones[:, :NF] * gap_ref[:, :NF], axis=1, keepdims=True)
+
+
+def lat_kernel(where_ref, latent_ref, frame_ref, gap_ref, keep_ref, give_ref):
+    core = where_ref[1]
+    gap = frame_gap(ones_by_frame(frame_ref[...], NF), gap_ref)
+    mine = pl.ds(pl.multiple_of(core * HALF, 128), HALF)
+    other = pl.ds(pl.multiple_of((1 - core) * HALF, 128), HALF)
+    keep_ref[...] = -gap * latent_ref[:, mine]
+    give_ref[...] = -gap * latent_ref[:, other]
+
+
+def lat_terms(where, latent, frame_row, gap):
+    return call(
+        lat_kernel,
+        (where, latent, frame_row, gap),
+        [SM, VM, VM, VM],
+        [shaped(ROWS, HALF), shaped(ROWS, HALF)],
+        (ROWS * D, 2000000, 0),
+    )
 
 
 def side_kernel(
-    where_ref,
-    after_hbm,
-    latent_hbm,
-    frame_ref,
-    gap_ref,
-    feat_ref,
-    mod_hbm,
-    qkv_hbm,
-    keep_ref,
-    give_ref,
-    gate_ref,
-    w_ref,
-    lat_ref,
-    mod_ref,
-    sems,
+    where_ref, after_ref, frame_ref, gap_ref, feat_ref, mod_hbm, qkv_hbm, gate_ref, w_ref, mod_ref, sems
 ):
-    place, core = where_ref[0], where_ref[1]
-    copies = [
-        pltpu.make_async_copy(mod_hbm.at[:, pl.ds(2 * D, D)], mod_ref, sems.at[0]),
-        pltpu.make_async_copy(latent_hbm, lat_ref, sems.at[1]),
-    ]
+    place = where_ref[0]
+    copies = [pltpu.make_async_copy(mod_hbm.at[:, pl.ds(2 * D, D)], mod_ref, sems.at[0])]
     for i in range(3):
         cols = pl.ds(pl.multiple_of(i * D + place * WIDE, 128), WIDE)
         copies.append(
             pltpu.make_async_copy(
-                qkv_hbm.at[:, cols], w_ref.at[:, pl.ds(i * WIDE, WIDE)], sems.at[2 + i]
+                qkv_hbm.at[:, cols], w_ref.at[:, pl.ds(i * WIDE, WIDE)], sems.at[1 + i]
             )
         )
     for one in copies:
         one.start()
     ones = ones_by_frame(frame_ref[...], 3 * NF)
-    gap = jnp.sum(ones[:, :NF] * gap_ref[:, :NF], axis=1, keepdims=True)
+    gap = frame_gap(ones, gap_ref)
     copies[0].wait()
     table = jnp.dot(feat_ref[...], mod_ref[...], preferred_element_type=F32)
     gate_ref[...] = -gap * pick_rows(ones.astype(BF16), table)
-    copies[1].wait()
-    mine = pl.ds(pl.multiple_of(core * HALF, 128), HALF)
-    other = pl.ds(pl.multiple_of((1 - core) * HALF, 128), HALF)
-    keep_ref[...] = -gap * lat_ref[:, mine]
-    give_ref[...] = -gap * lat_ref[:, other]
-    for one in copies[2:]:
+    for one in copies[1:]:
         one.wait()
 
 
-def side_terms(where, after, latent, frame_row, gap, features, mod_weight, qkv_weight):
+def side_terms(where, after, frame_row, gap, features, mod_weight, qkv_weight):
     return call(
         side_kernel,
-        (where, after, latent, frame_row, gap, features, mod_weight, qkv_weight),
-        [SM, ANY, HBM, VM, VM, VM, HBM, HBM],
-        [
-            shaped(ROWS, HALF),
-            shaped(ROWS, HALF),
-            shaped(ROWS, D),
-            shaped(D, 3 * WIDE, kind=BF16),
-        ],
+        (where, after, frame_row, gap, features, mod_weight, qkv_weight),
+        [SM, ANY, VM, VM, VM, HBM, HBM],
+        [shaped(ROWS, D), shaped(D, 3 * WIDE, kind=BF16)],
         (30000000, 6000000, 0),
-        [
-            pltpu.VMEM((ROWS, D), F32),
-            pltpu.VMEM((256, D), BF16),
-            pltpu.SemaphoreType.DMA((5,)),
-        ],
-        mib=24,
+        [pltpu.VMEM((256, D), BF16), pltpu.SemaphoreType.DMA((4,))],
     )
 
 
@@ -481,27 +470,31 @@
     gap = jnp.pad(gap, (0, 128 - NF))[None, :]
     frame_row = jnp.pad(frame_index, (0, 256 - ROWS))[None, :]
 
-    mine = normed_pack(latent, frame_row, features, mod_weight)
+    tie = lax.optimization_barrier
+    mine, latent = normed_pack(latent, frame_row, features, mod_weight)
     from_prev = send(mine, along("a", 1))
     from_next = send(mine, along("a", -1))
-    from_far = send(mine, along("a", 2))
-    lat_keep, lat_give, gate, weight = side_terms(
-        where, mine, latent, frame_row, gap, features, mod_weight, qkv_weight
-    )
+    lat_keep, lat_give = lat_terms(where, latent, frame_row, gap)
     lat_beside = send(lat_give, SWAP)
-
-    q0, kv0 = project(mine, from_prev, weight)
+    gate, weight = side_terms(
+        where, lat_give, frame_row, gap, features, mod_weight, qkv_weight
+    )
+    mine_later, weight = tie((mine, weight))
+    from_far = send(mine_later, along("a", 2))
+    lat_both, lat_wire = add_up(lat_keep, lat_beside, F32, weight)
+    lat_got = send(lat_wire, ROUND1)
+
+    q0, kv0 = project(mine, from_prev, weight, after=(lat_wire,))
     up0 = send(kv0, along("b", 1))
     down0 = send(kv0, along("b", -1))
-    lat_both, lat_wire = add_up(lat_keep, lat_beside, F32, kv0)
-    lat_got = send(lat_wire, ROUND1)
-    q1, kv1 = project(from_next, from_far, weight, after=(kv0, lat_wire))
+    q1, kv1 = project(from_next, from_far, weight, after=(kv0,))
     down1 = send(kv1, along("b", -1))
     up1 = send(kv1, along("b", 1))
     far0 = send(up0, along("b", 1))
     state = attend([kv0, kv1], queries=(q0, q1))
     state = attend([up0, down0], state=state)
-    far1 = send(down1, along("b", -1))
+    down1_later, _ = tie((down1, state[1]))
+    far1 = send(down1_later, along("b", -1))
     _, lat_wire = add_up(lat_both, lat_got, F32, state[1])
     lat_far = send(lat_wire, ROUND2)
     state = attend([up1, down1], state=state, after=(lat_wire,))
@@ -510,17 +503,17 @@
     b1 = send(a1, along("a", -1))
     b2 = send(a2, along("a", 1))
     (a0,) = attend([far0, far1], state=state, last=(0, ROWS), after=(a1,))
-    lat_sum = back_sum(where, a0, lat_keep, lat_got, lat_far)
-    lat_back = send(lat_sum, SWAP)
     part = out_first(where, a0, out_weight)
-    base = join(where, anchor, lat_keep, lat_give, lat_beside, lat_got, lat_far, lat_back)
     pieces = (b1, b2, b3)
-    give = out_rest(False, where, base, part, pieces, out_weight, gate)
+    give = out_rest(False, where, part, part, pieces, out_weight, gate)
     beside = send(give, SWAP)
     keep = out_rest(True, where, give, part, pieces, out_weight, gate)
     both, wire = add_up(keep, beside, BF16, keep)
     got = send(wire, ROUND1)
-    _, wire = add_up(both, got, BF16, keep)
+    lat_sum = back_sum(where, wire, lat_keep, lat_got, lat_far)
+    lat_back = send(lat_sum, SWAP)
+    base = join(where, anchor, lat_keep, lat_give, lat_beside, lat_got, lat_far, lat_back)
+    _, wire = add_up(both, got, BF16, base)
     far = send(wire, ROUND2)
     back = send(back_sum(where, far, keep, got, far), SWAP)
     return join(where, base, keep, give, beside, got, far, back)[None]

time: 99.6 us -> 107 us (1.074)
  the two profiles are of different devices: /device:TPU:7 before, /device:TPU:15 now
where the time goes in v1:
time: 107 us; the launch traced here: 106 us
  waiting for transfers between devices  46.1 us (43%)
  Pallas kernels  31.7 us (30%)
  starting transfers between devices  26 us (24%)
    ppermute x20, waiting for transfers between devices, send(): return lax.ppermute(value, AXES, route)  46.1 us
    pallas_call x21, Pallas kernels, run_kernel(): pl.pallas_call(kernel, in_specs=specs, out_specs=[VM] * len(outs) if out_...  31.7 us
    ppermute x20, starting transfers between devices, send(): return lax.ppermute(value, AXES, route)  26 us
  transfers between devices with their start and end apart: 20, of which 11 were waited for; matrix products, arithmetic and copies ran while one was open for 0% of the time, Pallas kernels for 20%

profile of v1, /device:TPU:15, one launch (start us, length us, event | category | flops | bytes accessed | tf_op | source)
XLA Modules:
  0.0 105.7 jit_solution(13028216248370519906)
XLA Ops:
  1.5 3.4 %shard_map.73 = (bf16[176,1536]{1,0:T(8,128)(2,1)S(1)}, f32[168,1536]{1,0:T(8,128)S(1)}) custom-call(f32[168,1536]{1,0:T(8,128)} %bitcast.17, s32[1,256]{1,0:T(1,128)S(1)} %bitcast.14, bf16[16,256]{1,0:T(8,128)(2,1)S(1)} %pad_maximum_fusion.feat_ref, bf16[256,4608]{1,0:T(8,128)(2,1)} %mod_hbm.3), custom_call_target="tpu_custom_call" | custom-call | flops 30000000 | bytes 4000000 | tf_op jit(solution)/shard_map/pallas_call | solution.py:46
  5.0 1.7 %collective-permute-start.2 = (bf16[176,1536]{1,0:T(8,128)(2,1)S(1)}, bf16[176,1536]{1,0:T(8,128)(2,1)S(1)}, u32[]{:S(2)}, u32[]{:S(2)}) collective-permute-start(bf16[176,1536]{1,0:T(8,128)(2,1)S(1)} %get-tuple-element.44.refs_1_), channel_id=1, source_target_pairs={{0,4},{1,5},{2,6},{3,7},{4,8},{5,9},{6,10},{7,11},{8,12},{9,13},{1... | collective-permute-start | bytes 1622024 | tf_op jit(solution)/shard_map/ppermute | solution.py:83
  8.2 3.8 %collective-permute-start.3 = (bf16[176,1536]{1,0:T(8,128)(2,1)S(1)}, bf16[176,1536]{1,0:T(8,128)(2,1)S(1)}, u32[]{:S(2)}, u32[]{:S(2)}) collective-permute-start(bf16[176,1536]{1,0:T(8,128)(2,1)S(1)} %get-tuple-element.44.refs_1_), channel_id=1, source_target_pairs={{0,12},{1,13},{2,14},{3,15},{4,0},{5,1},{6,2},{7,3},{8,4},{9,5},{1... | collective-permute-start | bytes 1622024 | tf_op jit(solution)/shard_map/ppermute | solution.py:83
  12.0 2.8 %shard_map.75 = (f32[168,1536]{1,0:T(8,128)S(1)}, bf16[1536,1152]{1,0:T(8,128)(2,1)S(1)}) custom-call(s32[3]{0:T(128)S(1)} %pad_add_fusion.where_ref, f32[168,768]{1,0:T(8,128)S(1)} %get-tuple-element.36.after_ref.give_ref, s32[1,256]{1,0:T(1,128)S(1)} %bitcast.16, f32[1,128]{1,0:T(1,128)S(1)} %pad_bitcast_fusion.gap_ref, ...), custom_call_target="tpu_custom_call" | custom-call | flops 30000000 | bytes 6000000 | tf_op jit(solution)/shard_map/pallas_call | solution.py:46
  15.5 1.8 %shard_map.77 = (bf16[336,384]{1,0:T(8,128)(2,1)S(1)}, bf16[344,768]{1,0:T(8,128)(2,1)S(1)}) custom-call(f32[168,768]{1,0:T(8,128)S(1)} %get-tuple-element.40.refs_0_, bf16[176,1536]{1,0:T(8,128)(2,1)S(1)} %get-tuple-element.44.refs_1_, bf16[176,1536]{1,0:T(8,128)(2,1)S(1)} %collective-permute-done.2.refs_2_, ...), custom_call_target="tpu_custom_call" | custom-call | flops 1189085184 | bytes 5000000 | tf_op jit(solution)/shard_map/pallas_call | solution.py:46
  17.3 1.4 %collective-permute-start.5 = (bf16[344,768]{1,0:T(8,128)(2,1)S(1)}, bf16[344,768]{1,0:T(8,128)(2,1)S(1)}, u32[]{:S(2)}, u32[]{:S(2)}) collective-permute-start(bf16[344,768]{1,0:T(8,128)(2,1)S(1)} %get-tuple-element.43.refs_0_.refs_2_), channel_id=1, source_target_pairs={{0,1},{1,2},{2,3},{3,0},{4,5},{5,6},{6,7},{7,4},{8,9},{9,10},{10,1... | collective-permute-start | bytes 1585160 | tf_op jit(solution)/shard_map/ppermute | solution.py:83
  18.9 7.2 %collective-permute-done.3.refs_1_ = bf16[176,1536]{1,0:T(8,128)(2,1)S(1)} collective-permute-done((bf16[176,1536]{1,0:T(8,128)(2,1)S(1)}, bf16[176,1536]{1,0:T(8,128)(2,1)S(1)}, u32[]{:S(2)}, u32[]{:S(2)}) %collective-permute-start.3) | collective-permute-done | bytes 540704 | tf_op jit(solution)/shard_map/ppermute | solution.py:83
  26.1 1.8 %shard_map.78 = (bf16[336,384]{1,0:T(8,128)(2,1)S(1)}, bf16[344,768]{1,0:T(8,128)(2,1)S(1)}) custom-call(bf16[344,768]{1,0:T(8,128)(2,1)S(1)} %get-tuple-element.43.refs_0_.refs_2_, bf16[176,1536]{1,0:T(8,128)(2,1)S(1)} %collective-permute-done.3.refs_1_, bf16[176,1536]{1,0:T(8,128)(2,1)S(1)} %collective-permute-done.4.refs_2_, ...), custom_call_target="tpu_custom_call" | custom-call | flops 1189085184 | bytes 5000000 | tf_op jit(solution)/shard_map/pallas_call | solution.py:46
  28.5 1.4 %collective-permute-start.8 = (bf16[344,768]{1,0:T(8,128)(2,1)S(1)}, bf16[344,768]{1,0:T(8,128)(2,1)S(1)}, u32[]{:S(2)}, u32[]{:S(2)}) collective-permute-start(bf16[344,768]{1,0:T(8,128)(2,1)S(1)} %get-tuple-element.46.refs_3_), channel_id=1, source_target_pairs={{0,1},{1,2},{2,3},{3,0},{4,5},{5,6},{6,7},{7,4},{8,9},{9,10},{10,1... | collective-permute-start | bytes 1585160 | tf_op jit(solution)/shard_map/ppermute | solution.py:83
  29.9 2.1 %shard_map.79 = (f32[672,384]{1,0:T(8,128)S(1)}, f32[672,128]{1,0:T(8,128)S(1)}, bf16[672,768]{1,0:T(8,128)(2,1)S(1)}) custom-call(bf16[336,384]{1,0:T(8,128)(2,1)S(1)} %get-tuple-element.42.refs_0_, bf16[336,384]{1,0:T(8,128)(2,1)S(1)} %get-tuple-element.45.refs_1_, bf16[344,768]{1,0:T(8,128)(2,1)S(1)} %get-tuple-element.43.refs_0_.refs_2_, ...), custom_call_target="tpu_custom_call" | custom-call | flops 1387266048 | bytes 2000000 | tf_op jit(solution)/shard_map/pallas_call | solution.py:46
  32.0 3.3 %shard_map.80 = (f32[672,384]{1,0:T(8,128)S(1)}, f32[672,128]{1,0:T(8,128)S(1)}) custom-call(bf16[672,768]{1,0:T(8,128)(2,1)S(1)} %get-tuple-element.47.refs_0_.refs_1_, f32[672,384]{1,0:T(8,128)S(1)} %get-tuple-element.48.refs_1_, f32[672,128]{1,0:T(8,128)S(1)} %get-tuple-element.49.refs_2_, bf16[344,768]{1,0:T(8,128)(2,1)S(1)} %collective-permute-done.5.refs_3_, ...), custom_call_target="tpu_custom_call" | custom-call | flops 1387266048 | bytes 2000000 | tf_op jit(solution)/shard_map/pallas_call | solution.py:46
  38.6 3.3 %shard_map.82 = (f32[672,384]{1,0:T(8,128)S(1)}, f32[672,128]{1,0:T(8,128)S(1)}) custom-call(f32[168,768]{1,0:T(8,128)S(1)} %get-tuple-element.51.refs_0_, bf16[672,768]{1,0:T(8,128)(2,1)S(1)} %get-tuple-element.47.refs_0_.refs_1_, f32[672,384]{1,0:T(8,128)S(1)} %get-tuple-element.50.after_ref.refs_2_, f32[672,128]{1,0:T(8,128)S(1)} %get-tuple-element.52.refs_3_, ...), custom_call_target="tpu_custom_call" | custom-call | flops 1387266048 | bytes 2000000 | tf_op jit(solution)/shard_map/pallas_call | solution.py:46
  41.9 2.7 %collective-permute-done.10.refs_3_.refs_4_ = bf16[344,768]{1,0:T(8,128)(2,1)S(1)} collective-permute-done((bf16[344,768]{1,0:T(8,128)(2,1)S(1)}, bf16[344,768]{1,0:T(8,128)(2,1)S(1)}, u32[]{:S(2)}, u32[]{:S(2)}) %collective-permute-start.10) | collective-permute-done | bytes 528416 | tf_op jit(solution)/shard_map/ppermute | solution.py:83
  45.6 2.3 %shard_map.83 = (bf16[168,384]{1,0:T(8,128)(2,1)S(1)}, bf16[168,384]{1,0:T(8,128)(2,1)S(1)}, bf16[168,384]{1,0:T(8,128)(2,1)S(1)}) custom-call(bf16[672,768]{1,0:T(8,128)(2,1)S(1)} %get-tuple-element.47.refs_0_.refs_1_, f32[672,384]{1,0:T(8,128)S(1)} %get-tuple-element.53.refs_1_.refs_2_, f32[672,128]{1,0:T(8,128)S(1)} %get-tuple-element.54.refs_2_.refs_3_, ...), custom_call_target="tpu_custom_call" | custom-call | flops 1040449536 | bytes 2000000 | tf_op jit(solution)/shard_map/pallas_call | solution.py:46
  47.9 3.5 %collective-permute-start.12 = (bf16[168,384]{1,0:T(8,128)(2,1)S(1)}, bf16[168,384]{1,0:T(8,128)(2,1)S(1)}, u32[]{:S(2)}, u32[]{:S(2)}) collective-permute-start(bf16[168,384]{1,0:T(8,128)(2,1)S(1)} %get-tuple-element.56.refs_0_), channel_id=1, source_target_pairs={{0,12},{1,13},{2,14},{3,15},{4,0},{5,1},{6,2},{7,3},{8,4},{9,5},{1... | collective-permute-start | bytes 387080 | tf_op jit(solution)/shard_map/ppermute | solution.py:83
  54.8 3.0 %collective-permute-done.13.a2 = bf16[168,384]{1,0:T(8,128)(2,1)S(1)} collective-permute-done((bf16[168,384]{1,0:T(8,128)(2,1)S(1)}, bf16[168,384]{1,0:T(8,128)(2,1)S(1)}, u32[]{:S(2)}, u32[]{:S(2)}) %collective-permute-start.13) | collective-permute-done | bytes 129056 | tf_op jit(solution)/shard_map/ppermute | solution.py:83
  58.9 4.4 %collective-permute-start.15 = (f32[168,768]{1,0:T(8,128)S(1)}, f32[168,768]{1,0:T(8,128)S(1)}, u32[]{:S(2)}, u32[]{:S(2)}) collective-permute-start(f32[168,768]{1,0:T(8,128)S(1)} %shard_map.86.after_ref.give_ref), channel_id=1, source_target_pairs={{0,16},{1,17},{2,18},{3,19},{4,20},{5,21},{6,22},{7,23},{8,24},{9,... | collective-permute-start | bytes 1548296 | tf_op jit(solution)/shard_map/ppermute | solution.py:83
  65.9 13.7 %collective-permute-done.7.far_ref = f32[168,768]{1,0:T(8,128)S(1)} collective-permute-done((f32[168,768]{1,0:T(8,128)S(1)}, f32[168,768]{1,0:T(8,128)S(1)}, u32[]{:S(2)}, u32[]{:S(2)}) %collective-permute-start.7) | collective-permute-done | bytes 516128 | tf_op jit(solution)/shard_map/ppermute | solution.py:83
  81.4 1.5 %collective-permute-done.16.back_ref = f32[168,768]{1,0:T(8,128)S(1)} collective-permute-done((f32[168,768]{1,0:T(8,128)S(1)}, f32[168,768]{1,0:T(8,128)S(1)}, u32[]{:S(2)}, u32[]{:S(2)}) %collective-permute-start.16) | collective-permute-done | bytes 516128 | tf_op jit(solution)/shard_map/ppermute | solution.py:83
  83.8 5.3 %collective-permute-done.17.b_ref.got_ref = bf16[168,768]{1,0:T(8,128)(2,1)S(1)} collective-permute-done((bf16[168,768]{1,0:T(8,128)(2,1)S(1)}, bf16[168,768]{1,0:T(8,128)(2,1)S(1)}, u32[]{:S(2)}, u32[]{:S(2)}) %collective-permute-start.17) | collective-permute-done | bytes 258080 | tf_op jit(solution)/shard_map/ppermute | solution.py:83
  91.2 8.6 %collective-permute-done.18.after_ref.far_ref = bf16[168,768]{1,0:T(8,128)(2,1)S(1)} collective-permute-done((bf16[168,768]{1,0:T(8,128)(2,1)S(1)}, bf16[168,768]{1,0:T(8,128)(2,1)S(1)}, u32[]{:S(2)}, u32[]{:S(2)}) %collective-permute-start.18) | collective-permute-done | bytes 258080 | tf_op jit(solution)/shard_map/ppermute | solution.py:83
  100.5 1.9 %collective-permute-start.19 = (f32[168,768]{1,0:T(8,128)S(1)}, f32[168,768]{1,0:T(8,128)S(1)}, u32[]{:S(2)}, u32[]{:S(2)}) collective-permute-start(f32[168,768]{1,0:T(8,128)S(1)} %shard_map.92), channel_id=1, source_target_pairs={{0,16},{1,17},{2,18},{3,19},{4,20},{5,21},{6,22},{7,23},{8,24},{9,... | collective-permute-start | bytes 1548296 | tf_op jit(solution)/shard_map/ppermute | solution.py:83
  102.4 1.5 %collective-permute-done.19.back_ref = f32[168,768]{1,0:T(8,128)S(1)} collective-permute-done((f32[168,768]{1,0:T(8,128)S(1)}, f32[168,768]{1,0:T(8,128)S(1)}, u32[]{:S(2)}, u32[]{:S(2)}) %collective-permute-start.19) | collective-permute-done | bytes 516128 | tf_op jit(solution)/shard_map/ppermute | solution.py:83
  103.9 1.8 %shard_map.93 = f32[168,1536]{1,0:T(8,128)} custom-call(s32[3]{0:T(128)S(1)} %pad_add_fusion.where_ref, f32[168,1536]{1,0:T(8,128)S(1)} %shard_map.90.after_ref.base_ref, f32[168,768]{1,0:T(8,128)S(1)} %shard_map.87.a_ref.after_ref.keep_ref, f32[168,768]{1,0:T(8,128)S(1)} %shard_map.86.after_ref.give_ref, ...), custom_call_target="tpu_custom_call" | custom-call | flops 516096 | bytes 4000000 | tf_op jit(solution)/shard_map/pallas_call | solution.py:46
  (52 shorter events, 21.3 us)
Async XLA Ops:
  5.0 10.6 %collective-permute-start.2 = (bf16[176,1536]{1,0:T(8,128)(2,1)S(1)}, bf16[176,1536]{1,0:T(8,128)(2,1)S(1)}, u32[]{:S(2)}, u32[]{:S(2)}) collective-permute-start(bf16[176,1536]{1,0:T(8,128)(2,1)S(1)} %get-tuple-element.44.refs_1_), channel_id=1, source_target_pairs={{0,4},{1,5},{2,6},{3,7},{4,8},{5,9},{6,10},{7,11},{8,12},{9,13},{1... | collective-permute-start | bytes 1622024 | tf_op jit(solution)/shard_map/ppermute | solution.py:83
  7.5 7.4 %collective-permute-start = (f32[168,768]{1,0:T(8,128)S(1)}, f32[168,768]{1,0:T(8,128)S(1)}, u32[]{:S(2)}, u32[]{:S(2)}) collective-permute-start(f32[168,768]{1,0:T(8,128)S(1)} %get-tuple-element.36.after_ref.give_ref), channel_id=1, source_target_pairs={{0,16},{1,17},{2,18},{3,19},{4,20},{5,21},{6,22},{7,23},{8,24},{9,... | collective-permute-start | bytes 1548296 | tf_op jit(solution)/shard_map/ppermute | solution.py:83
  8.2 17.8 %collective-permute-start.3 = (bf16[176,1536]{1,0:T(8,128)(2,1)S(1)}, bf16[176,1536]{1,0:T(8,128)(2,1)S(1)}, u32[]{:S(2)}, u32[]{:S(2)}) collective-permute-start(bf16[176,1536]{1,0:T(8,128)(2,1)S(1)} %get-tuple-element.44.refs_1_), channel_id=1, source_target_pairs={{0,12},{1,13},{2,14},{3,15},{4,0},{5,1},{6,2},{7,3},{8,4},{9,5},{1... | collective-permute-start | bytes 1622024 | tf_op jit(solution)/shard_map/ppermute | solution.py:83
  14.8 11.3 %collective-permute-start.4 = (bf16[176,1536]{1,0:T(8,128)(2,1)S(1)}, bf16[176,1536]{1,0:T(8,128)(2,1)S(1)}, u32[]{:S(2)}, u32[]{:S(2)}) collective-permute-start(bf16[176,1536]{1,0:T(8,128)(2,1)S(1)} %get-tuple-element.44.refs_1_), channel_id=1, source_target_pairs={{0,8},{1,9},{2,10},{3,11},{4,12},{5,13},{6,14},{7,15},{8,0},{9,1},... | collective-permute-start | bytes 1622024 | tf_op jit(solution)/shard_map/ppermute | solution.py:83
  17.3 14.7 %collective-permute-start.5 = (bf16[344,768]{1,0:T(8,128)(2,1)S(1)}, bf16[344,768]{1,0:T(8,128)(2,1)S(1)}, u32[]{:S(2)}, u32[]{:S(2)}) collective-permute-start(bf16[344,768]{1,0:T(8,128)(2,1)S(1)} %get-tuple-element.43.refs_0_.refs_2_), channel_id=1, source_target_pairs={{0,1},{1,2},{2,3},{3,0},{4,5},{5,6},{6,7},{7,4},{8,9},{9,10},{10,1... | collective-permute-start | bytes 1585160 | tf_op jit(solution)/shard_map/ppermute | solution.py:83
  18.7 13.3 %collective-permute-start.6 = (bf16[344,768]{1,0:T(8,128)(2,1)S(1)}, bf16[344,768]{1,0:T(8,128)(2,1)S(1)}, u32[]{:S(2)}, u32[]{:S(2)}) collective-permute-start(bf16[344,768]{1,0:T(8,128)(2,1)S(1)} %get-tuple-element.43.refs_0_.refs_2_), channel_id=1, source_target_pairs={{0,3},{1,0},{2,1},{3,2},{4,7},{5,4},{6,5},{7,6},{8,11},{9,8},{10,9... | collective-permute-start | bytes 1585160 | tf_op jit(solution)/shard_map/ppermute | solution.py:83
  27.8 8.4 %collective-permute-start.9 = (bf16[344,768]{1,0:T(8,128)(2,1)S(1)}, bf16[344,768]{1,0:T(8,128)(2,1)S(1)}, u32[]{:S(2)}, u32[]{:S(2)}) collective-permute-start(bf16[344,768]{1,0:T(8,128)(2,1)S(1)} %get-tuple-element.46.refs_3_), channel_id=1, source_target_pairs={{0,3},{1,0},{2,1},{3,2},{4,7},{5,4},{6,5},{7,6},{8,11},{9,8},{10,9... | collective-permute-start | bytes 1585160 | tf_op jit(solution)/shard_map/ppermute | solution.py:83
  27.9 9.8 %collective-permute-start.1 = (f32[168,768]{1,0:T(8,128)S(1)}, f32[168,768]{1,0:T(8,128)S(1)}, u32[]{:S(2)}, u32[]{:S(2)}) collective-permute-start(f32[168,768]{1,0:T(8,128)S(1)} %get-tuple-element.40.refs_0_), channel_id=1, source_target_pairs={{0,32},{1,33},{2,34},{3,35},{4,36},{5,37},{6,38},{7,39},{8,40},{9,... | collective-permute-start | bytes 1548296 | tf_op jit(solution)/shard_map/ppermute | solution.py:83
  28.5 10.1 %collective-permute-start.8 = (bf16[344,768]{1,0:T(8,128)(2,1)S(1)}, bf16[344,768]{1,0:T(8,128)(2,1)S(1)}, u32[]{:S(2)}, u32[]{:S(2)}) collective-permute-start(bf16[344,768]{1,0:T(8,128)(2,1)S(1)} %get-tuple-element.46.refs_3_), channel_id=1, source_target_pairs={{0,1},{1,2},{2,3},{3,0},{4,5},{5,6},{6,7},{7,4},{8,9},{9,10},{10,1... | collective-permute-start | bytes 1585160 | tf_op jit(solution)/shard_map/ppermute | solution.py:83
  36.3 8.4 %collective-permute-start.10 = (bf16[344,768]{1,0:T(8,128)(2,1)S(1)}, bf16[344,768]{1,0:T(8,128)(2,1)S(1)}, u32[]{:S(2)}, u32[]{:S(2)}) collective-permute-start(bf16[344,768]{1,0:T(8,128)(2,1)S(1)} %collective-permute-done.5.refs_3_), channel_id=1, source_target_pairs={{0,1},{1,2},{2,3},{3,0},{4,5},{5,6},{6,7},{7,4},{8,9},{9,10},{10,1... | collective-permute-start | bytes 1585160 | tf_op jit(solution)/shard_map/ppermute | solution.py:83
  37.3 8.4 %collective-permute-start.11 = (bf16[344,768]{1,0:T(8,128)(2,1)S(1)}, bf16[344,768]{1,0:T(8,128)(2,1)S(1)}, u32[]{:S(2)}, u32[]{:S(2)}) collective-permute-start(bf16[344,768]{1,0:T(8,128)(2,1)S(1)} %collective-permute-done.9.refs_5_), channel_id=1, source_target_pairs={{0,3},{1,0},{2,1},{3,2},{4,7},{5,4},{6,5},{7,6},{8,11},{9,8},{10,9... | collective-permute-start | bytes 1585160 | tf_op jit(solution)/shard_map/ppermute | solution.py:83
  38.6 15.2 %slice-start = ((s8[4718592]{0:T(1024)(128)(4,1)}), s8[4194304]{0:T(1024)(128)(4,1)S(1)}, s32[]{:S(2)}) async-start(s8[4718592]{0:T(1024)(128)(4,1)} %bitcast.12), calls=%async_computation | async-start | bytes 8388608
  45.6 8.1 %slice-start.1 = ((s8[4718592]{0:T(1024)(128)(4,1)}), s8[524288]{0:T(1024)(128)(4,1)S(1)}, s32[]{:S(2)}) async-start(s8[4718592]{0:T(1024)(128)(4,1)} %bitcast.12), calls=%async_computation.1 | async-start | bytes 1048576
  47.9 6.9 %collective-permute-start.12 = (bf16[168,384]{1,0:T(8,128)(2,1)S(1)}, bf16[168,384]{1,0:T(8,128)(2,1)S(1)}, u32[]{:S(2)}, u32[]{:S(2)}) collective-permute-start(bf16[168,384]{1,0:T(8,128)(2,1)S(1)} %get-tuple-element.56.refs_0_), channel_id=1, source_target_pairs={{0,12},{1,13},{2,14},{3,15},{4,0},{5,1},{6,2},{7,3},{8,4},{9,5},{1... | collective-permute-start | bytes 387080 | tf_op jit(solution)/shard_map/ppermute | solution.py:83
  51.4 6.4 %collective-permute-start.13 = (bf16[168,384]{1,0:T(8,128)(2,1)S(1)}, bf16[168,384]{1,0:T(8,128)(2,1)S(1)}, u32[]{:S(2)}, u32[]{:S(2)}) collective-permute-start(bf16[168,384]{1,0:T(8,128)(2,1)S(1)} %get-tuple-element.57), channel_id=1, source_target_pairs={{0,4},{1,5},{2,6},{3,7},{4,8},{5,9},{6,10},{7,11},{8,12},{9,13},{1... | collective-permute-start | bytes 387080 | tf_op jit(solution)/shard_map/ppermute | solution.py:83
  51.4 6.4 %collective-permute-start.14 = (bf16[168,384]{1,0:T(8,128)(2,1)S(1)}, bf16[168,384]{1,0:T(8,128)(2,1)S(1)}, u32[]{:S(2)}, u32[]{:S(2)}) collective-permute-start(bf16[168,384]{1,0:T(8,128)(2,1)S(1)} %get-tuple-element.58), channel_id=1, source_target_pairs={{0,8},{1,9},{2,10},{3,11},{4,12},{5,13},{6,14},{7,15},{8,0},{9,1},... | collective-permute-start | bytes 387080 | tf_op jit(solution)/shard_map/ppermute | solution.py:83
  58.9 24.0 %copy-start = (f32[168,1536]{1,0:T(8,128)S(1)}, f32[168,1536]{1,0:T(8,128)}, u32[]{:S(2)}) copy-start(f32[168,1536]{1,0:T(8,128)} %base_ref.1) | copy-start | bytes 3096580
  58.9 6.9 %collective-permute-start.15 = (f32[168,768]{1,0:T(8,128)S(1)}, f32[168,768]{1,0:T(8,128)S(1)}, u32[]{:S(2)}, u32[]{:S(2)}) collective-permute-start(f32[168,768]{1,0:T(8,128)S(1)} %shard_map.86.after_ref.give_ref), channel_id=1, source_target_pairs={{0,16},{1,17},{2,18},{3,19},{4,20},{5,21},{6,22},{7,23},{8,24},{9,... | collective-permute-start | bytes 1548296 | tf_op jit(solution)/shard_map/ppermute | solution.py:83
  63.4 16.2 %collective-permute-start.7 = (f32[168,768]{1,0:T(8,128)S(1)}, f32[168,768]{1,0:T(8,128)S(1)}, u32[]{:S(2)}, u32[]{:S(2)}) collective-permute-start(f32[168,768]{1,0:T(8,128)S(1)} %get-tuple-element.51.refs_0_), channel_id=1, source_target_pairs={{0,96},{1,97},{2,98},{3,99},{4,100},{5,101},{6,102},{7,103},{8,104... | collective-permute-start | bytes 1548296 | tf_op jit(solution)/shard_map/ppermute | solution.py:83
  80.3 2.6 %collective-permute-start.16 = (f32[168,768]{1,0:T(8,128)S(1)}, f32[168,768]{1,0:T(8,128)S(1)}, u32[]{:S(2)}, u32[]{:S(2)}) collective-permute-start(f32[168,768]{1,0:T(8,128)S(1)} %shard_map.89), channel_id=1, source_target_pairs={{0,16},{1,17},{2,18},{3,19},{4,20},{5,21},{6,22},{7,23},{8,24},{9,... | collective-permute-start | bytes 1548296 | tf_op jit(solution)/shard_map/ppermute | solution.py:83
  81.4 7.7 %collective-permute-start.17 = (bf16[168,768]{1,0:T(8,128)(2,1)S(1)}, bf16[168,768]{1,0:T(8,128)(2,1)S(1)}, u32[]{:S(2)}, u32[]{:S(2)}) collective-permute-start(bf16[168,768]{1,0:T(8,128)(2,1)S(1)} %get-tuple-element.60.after_ref), channel_id=1, source_target_pairs={{0,32},{1,33},{2,34},{3,35},{4,36},{5,37},{6,38},{7,39},{8,40},{9,... | collective-permute-start | bytes 774152 | tf_op jit(solution)/shard_map/ppermute | solution.py:83
  89.9 9.9 %collective-permute-start.18 = (bf16[168,768]{1,0:T(8,128)(2,1)S(1)}, bf16[168,768]{1,0:T(8,128)(2,1)S(1)}, u32[]{:S(2)}, u32[]{:S(2)}) collective-permute-start(bf16[168,768]{1,0:T(8,128)(2,1)S(1)} %get-tuple-element.62), channel_id=1, source_target_pairs={{0,96},{1,97},{2,98},{3,99},{4,100},{5,101},{6,102},{7,103},{8,104... | collective-permute-start | bytes 774152 | tf_op jit(solution)/shard_map/ppermute | solution.py:83
  100.5 3.4 %collective-permute-start.19 = (f32[168,768]{1,0:T(8,128)S(1)}, f32[168,768]{1,0:T(8,128)S(1)}, u32[]{:S(2)}, u32[]{:S(2)}) collective-permute-start(f32[168,768]{1,0:T(8,128)S(1)} %shard_map.92), channel_id=1, source_target_pairs={{0,16},{1,17},{2,18},{3,19},{4,20},{5,21},{6,22},{7,23},{8,24},{9,... | collective-permute-start | bytes 1548296 | tf_op jit(solution)/shard_map/ppermute | solution.py:83

commit v2 on v1

--- a/solution.py
+++ b/solution.py
@@ -20,6 +20,7 @@
 PAIRPACK = PAIR + 8
 QROWS = 4 * ROWS
 HALF = D // 2
+QUART = D // 4
 BIG = 131072.0
 AXES = ("tm", "ctx")
 
@@ -393,20 +394,40 @@
     )[0]
 
 
-def add_kernel(a_ref, b_ref, after_ref, out_ref, wire_ref):
+def add_kernel(n_parts, a_ref, b_ref, after_ref, *outs):
     total = a_ref[...] + b_ref[...].astype(F32)
-    out_ref[...] = total
-    wire_ref[...] = total.astype(wire_ref.dtype)
-
-
-def add_up(a, b, wire, after):
-    return call(
-        add_kernel,
+    if len(outs) > n_parts:
+        outs[0][...] = total
+    wide = total.shape[1] // n_parts
+    for i, wire_ref in enumerate(outs[-n_parts:]):
+        wire_ref[...] = total[:, i * wide : (i + 1) * wide].astype(wire_ref.dtype)
+
+
+def add_up(a, b, wire, after, n_parts=1, keep=False):
+    wide = a.shape[1]
+    outs = [shaped(ROWS, wide // n_parts, kind=wire)] * n_parts
+    return call(
+        functools.partial(add_kernel, n_parts),
         (a, b, after),
         [VM, VM, ANY],
-        [shaped(ROWS, HALF), shaped(ROWS, HALF, kind=wire)],
-        (ROWS * HALF, 2000000, 0),
-    )
+        ([shaped(ROWS, wide)] if keep else []) + outs,
+        (ROWS * wide, 2000000, 0),
+    )
+
+
+def pair_kernel(part, both_ref, got_ref, after_ref, wire_ref):
+    total = both_ref[:, pl.ds(part * QUART, QUART)] + got_ref[...].astype(F32)
+    wire_ref[...] = total.astype(wire_ref.dtype)
+
+
+def pair_up(part, both, got, after):
+    return call(
+        functools.partial(pair_kernel, part),
+        (both, got, after),
+        [VM, VM, ANY],
+        [shaped(ROWS, QUART, kind=BF16)],
+        (ROWS * QUART, 1000000, 0),
+    )[0]
 
 
 def before_sum(where_ref, got_ref, far_ref):
@@ -415,38 +436,78 @@
     return near + jnp.where(chip >= 2, far_ref[...].astype(F32), 0.0)
 
 
-def back_kernel(where_ref, after_ref, keep_ref, got_ref, far_ref, out_ref):
-    extra = jnp.where(where_ref[1] == 0, keep_ref[...], 0.0)
+def back_kernel(col0, where_ref, after_ref, keep_ref, got_ref, far_ref, out_ref):
+    mine = keep_ref[:, pl.ds(col0, got_ref.shape[1])]
+    extra = jnp.where(where_ref[1] == 0, mine, 0.0)
     out_ref[...] = before_sum(where_ref, got_ref, far_ref) + extra
 
 
-def back_sum(where, after, keep, got, far):
-    return call(
-        back_kernel,
+def back_sum(where, after, keep, got, far, col0=0):
+    return call(
+        functools.partial(back_kernel, col0),
         (where, after, keep, got, far),
         [SM, ANY] + [VM] * 3,
-        [shaped(ROWS, HALF)],
+        [shaped(*got.shape)],
         (ROWS * HALF, 2000000, 0),
     )[0]
 
 
-def join_kernel(where_ref, base_ref, keep_ref, give_ref, beside_ref, got_ref, far_ref, back_ref, out_ref):
+def base_kernel(where_ref, after_ref, anchor_ref, keep_ref, give_ref, beside_ref, got_ref, far_ref, back_ref, out_ref):
     core = where_ref[1]
     mine = pl.ds(pl.multiple_of(core * HALF, 128), HALF)
     other = pl.ds(pl.multiple_of((1 - core) * HALF, 128), HALF)
     own = before_sum(where_ref, got_ref, far_ref) + jnp.where(core == 1, beside_ref[...], 0.0)
-    out_ref[:, mine] = base_ref[:, mine] + (keep_ref[...] + own)
-    out_ref[:, other] = base_ref[:, other] + (give_ref[...] + back_ref[...])
-
-
-def join(where, base, keep, give, beside, got, far, back):
-    return call(
-        join_kernel,
-        (where, base, keep, give, beside, got, far, back),
-        [SM] + [VM] * 7,
+    out_ref[:, mine] = anchor_ref[:, mine] + (keep_ref[...] + own)
+    out_ref[:, other] = anchor_ref[:, other] + (give_ref[...] + back_ref[...])
+
+
+def base_sum(where, after, *terms):
+    return call(
+        base_kernel,
+        (where, after, *terms),
+        [SM, ANY] + [VM] * 7,
         [shaped(ROWS, D)],
         (ROWS * D * 2, 4000000, 0),
     )[0]
+
+
+def final_kernel(own, where_ref, *refs):
+    core = where_ref[1]
+    if own:
+        _, base_ref, keep_ref, beside_ref, g0, g1, f0, f1, out_hbm, buf_ref, sems = refs
+    else:
+        _, base_ref, give_ref, b0, b1, out_hbm, buf_ref, sems = refs
+    half = core if own else 1 - core
+    copies = []
+    for i in range(2):
+        part = pl.ds(i * QUART, QUART)
+        at = pl.ds(pl.multiple_of(half * HALF + i * QUART, 128), QUART)
+        if own:
+            got, far = ((g0, f0), (g1, f1))[i]
+            more = before_sum(where_ref, got, far) + jnp.where(core == 1, beside_ref[:, part], 0.0)
+            term = keep_ref[:, part] + more
+        else:
+            term = give_ref[:, part] + (b0, b1)[i][...]
+        buf_ref[:, part] = base_ref[:, at] + term
+        copies.append(pltpu.make_async_copy(buf_ref.at[:, part], out_hbm.at[:, at], sems.at[i]))
+        copies[-1].start()
+    for one in copies:
+        one.wait()
+
+
+def final_sum(own, args):
+    n = len(args)
+    return pl.pallas_call(
+        functools.partial(final_kernel, own),
+        in_specs=[SM, HBM if not own else ANY] + [VM] * (n - 2),
+        out_specs=HBM,
+        out_shape=shaped(ROWS, D),
+        input_output_aliases={} if own else {1: 0},
+        scratch_shapes=[pltpu.VMEM((ROWS, HALF), F32), pltpu.SemaphoreType.DMA((2,))],
+        compiler_params=pltpu.CompilerParams(vmem_limit_bytes=24 << 20),
+        cost_estimate=pl.CostEstimate(flops=ROWS * D, bytes_accessed=2000000, transcendentals=0),
+        name="final_own" if own else "final_other",
+    )(*args)
 
 
 SWAP = pairs(lambda x, c, y, z: (x, 1 - c, y, z))
@@ -474,17 +535,16 @@
     mine, latent = normed_pack(latent, frame_row, features, mod_weight)
     from_prev = send(mine, along("a", 1))
     from_next = send(mine, along("a", -1))
+    from_far = send(mine, along("a", 2))
     lat_keep, lat_give = lat_terms(where, latent, frame_row, gap)
     lat_beside = send(lat_give, SWAP)
     gate, weight = side_terms(
         where, lat_give, frame_row, gap, features, mod_weight, qkv_weight
     )
-    mine_later, weight = tie((mine, weight))
-    from_far = send(mine_later, along("a", 2))
-    lat_both, lat_wire = add_up(lat_keep, lat_beside, F32, weight)
-    lat_got = send(lat_wire, ROUND1)
-
-    q0, kv0 = project(mine, from_prev, weight, after=(lat_wire,))
+    (lat_both,) = add_up(lat_keep, lat_beside, F32, weight)
+    lat_got = send(lat_both, ROUND1)
+
+    q0, kv0 = project(mine, from_prev, weight, after=(lat_both,))
     up0 = send(kv0, along("b", 1))
     down0 = send(kv0, along("b", -1))
     q1, kv1 = project(from_next, from_far, weight, after=(kv0,))
@@ -495,7 +555,7 @@
     state = attend([up0, down0], state=state)
     down1_later, _ = tie((down1, state[1]))
     far1 = send(down1_later, along("b", -1))
-    _, lat_wire = add_up(lat_both, lat_got, F32, state[1])
+    (lat_wire,) = add_up(lat_both, lat_got, F32, state[1])
     lat_far = send(lat_wire, ROUND2)
     state = attend([up1, down1], state=state, after=(lat_wire,))
     a1, a2, a3 = attend([far0, far1], state=state, last=(ROWS, 3 * ROWS))
@@ -508,15 +568,25 @@
     give = out_rest(False, where, part, part, pieces, out_weight, gate)
     beside = send(give, SWAP)
     keep = out_rest(True, where, give, part, pieces, out_weight, gate)
-    both, wire = add_up(keep, beside, BF16, keep)
-    got = send(wire, ROUND1)
-    lat_sum = back_sum(where, wire, lat_keep, lat_got, lat_far)
+    both, wire0, wire1 = add_up(keep, beside, BF16, keep, n_parts=2, keep=True)
+    got0 = send(wire0, ROUND1)
+    got1 = send(wire1, ROUND1)
+    lat_sum = back_sum(where, wire0, lat_keep, lat_got, lat_far)
     lat_back = send(lat_sum, SWAP)
-    base = join(where, anchor, lat_keep, lat_give, lat_beside, lat_got, lat_far, lat_back)
-    _, wire = add_up(both, got, BF16, base)
-    far = send(wire, ROUND2)
-    back = send(back_sum(where, far, keep, got, far), SWAP)
-    return join(where, base, keep, give, beside, got, far, back)[None]
+    pair0 = pair_up(0, both, got0, lat_sum)
+    far0 = send(pair0, ROUND2)
+    pair1 = pair_up(1, both, got1, pair0)
+    far1 = send(pair1, ROUND2)
+    base = base_sum(
+        where, pair1, anchor, lat_keep, lat_give, lat_beside, lat_got, lat_far, lat_back
+    )
+    sum0 = back_sum(where, base, keep, got0, far0)
+    back0 = send(sum0, SWAP)
+    sum1 = back_sum(where, sum0, keep, got1, far1, QUART)
+    back1 = send(sum1, SWAP)
+    out = final_sum(True, (where, sum1, base, keep, beside, got0, got1, far0, far1))
+    out = final_sum(False, (where, out, base, give, back0, back1))
+    return out[None]
 
 
 def solution(mesh):

time: 107 us -> 104 us (0.972)
  waiting for transfers between devices: 46.1 us -> 34.9 us
  starting transfers between devices: 26 us -> 33.7 us
    ppermute x20 -> x23, waiting for transfers between devices: 46.1 us -> 34.9 us  [send(): return lax.ppermute(value, AXES, route)]
    ppermute x20 -> x23, starting transfers between devices: 26 us -> 33.7 us  [send(): return lax.ppermute(value, AXES, route)]
    pallas_call x21 -> x22, Pallas kernels: 31.7 us -> 28.9 us  [run_kernel(): pl.pallas_call(kernel, in_specs=specs, out_specs=[VM] * len(outs) if out_...]
    pallas_call x0 -> x2, Pallas kernels: none -> 2.81 us  [final_sum(): pl.pallas_call(functools.partial(final_kernel, own), in_specs=[SM, HBM if...]
  transfers between devices with their start and end apart: 20 -> 23, of which waited for: 11 -> 10; matrix products, arithmetic and copies ran while one was open for 0% -> 0% of each run, Pallas kernels for 20% -> 22%
where the time goes in v2:
time: 104 us; the launch traced here: 102 us
  waiting for transfers between devices  34.9 us (34%)
  starting transfers between devices  33.7 us (32%)
  Pallas kernels  31.7 us (30%)
    ppermute x23, waiting for transfers between devices, send(): return lax.ppermute(value, AXES, route)  34.9 us
    ppermute x23, starting transfers between devices, send(): return lax.ppermute(value, AXES, route)  33.7 us
    pallas_call x22, Pallas kernels, run_kernel(): pl.pallas_call(kernel, in_specs=specs, out_specs=[VM] * len(outs) if out_...  28.9 us
    pallas_call x2, Pallas kernels, final_sum(): pl.pallas_call(functools.partial(final_kernel, own), in_specs=[SM, HBM if...  2.81 us
  transfers between devices with their start and end apart: 23, of which 10 were waited for; matrix products, arithmetic and copies ran while one was open for 0% of the time, Pallas kernels for 22%

profile of v2, /device:TPU:15, one launch (start us, length us, event | category | flops | bytes accessed | tf_op | source)
XLA Modules:
  0.0 102.3 jit_solution(10795679774878315595)
XLA Ops:
  1.5 3.4 %shard_map.73 = (bf16[176,1536]{1,0:T(8,128)(2,1)S(1)}, f32[168,1536]{1,0:T(8,128)S(1)}) custom-call(f32[168,1536]{1,0:T(8,128)} %bitcast.17, s32[1,256]{1,0:T(1,128)S(1)} %bitcast.14, bf16[16,256]{1,0:T(8,128)(2,1)S(1)} %pad_maximum_fusion.feat_ref, bf16[256,4608]{1,0:T(8,128)(2,1)} %mod_hbm.3), custom_call_target="tpu_custom_call" | custom-call | flops 30000000 | bytes 4000000 | tf_op jit(solution)/shard_map/pallas_call | solution.py:47
  5.0 1.7 %collective-permute-start.1 = (bf16[176,1536]{1,0:T(8,128)(2,1)S(1)}, bf16[176,1536]{1,0:T(8,128)(2,1)S(1)}, u32[]{:S(2)}, u32[]{:S(2)}) collective-permute-start(bf16[176,1536]{1,0:T(8,128)(2,1)S(1)} %get-tuple-element.33.refs_1_), channel_id=1, source_target_pairs={{0,4},{1,5},{2,6},{3,7},{4,8},{5,9},{6,10},{7,11},{8,12},{9,13},{1... | collective-permute-start | bytes 1622024 | tf_op jit(solution)/shard_map/ppermute | solution.py:84
  8.2 3.8 %collective-permute-start.2 = (bf16[176,1536]{1,0:T(8,128)(2,1)S(1)}, bf16[176,1536]{1,0:T(8,128)(2,1)S(1)}, u32[]{:S(2)}, u32[]{:S(2)}) collective-permute-start(bf16[176,1536]{1,0:T(8,128)(2,1)S(1)} %get-tuple-element.33.refs_1_), channel_id=1, source_target_pairs={{0,12},{1,13},{2,14},{3,15},{4,0},{5,1},{6,2},{7,3},{8,4},{9,5},{1... | collective-permute-start | bytes 1622024 | tf_op jit(solution)/shard_map/ppermute | solution.py:84
  12.0 2.8 %shard_map.75 = (f32[168,1536]{1,0:T(8,128)S(1)}, bf16[1536,1152]{1,0:T(8,128)(2,1)S(1)}) custom-call(s32[3]{0:T(128)S(1)} %pad_add_fusion.where_ref, f32[168,768]{1,0:T(8,128)S(1)} %get-tuple-element.31.after_ref.give_ref, s32[1,256]{1,0:T(1,128)S(1)} %bitcast.16, f32[1,128]{1,0:T(1,128)S(1)} %pad_bitcast_fusion.gap_ref, ...), custom_call_target="tpu_custom_call" | custom-call | flops 30000000 | bytes 6000000 | tf_op jit(solution)/shard_map/pallas_call | solution.py:47
  15.5 1.8 %shard_map.77 = (bf16[336,384]{1,0:T(8,128)(2,1)S(1)}, bf16[344,768]{1,0:T(8,128)(2,1)S(1)}) custom-call(f32[168,768]{1,0:T(8,128)S(1)} %shard_map.76.refs_0_.a_ref, bf16[176,1536]{1,0:T(8,128)(2,1)S(1)} %get-tuple-element.33.refs_1_, bf16[176,1536]{1,0:T(8,128)(2,1)S(1)} %collective-permute-done.1.refs_2_, ...), custom_call_target="tpu_custom_call" | custom-call | flops 1189085184 | bytes 5000000 | tf_op jit(solution)/shard_map/pallas_call | solution.py:47
  17.3 1.5 %collective-permute-start.5 = (bf16[344,768]{1,0:T(8,128)(2,1)S(1)}, bf16[344,768]{1,0:T(8,128)(2,1)S(1)}, u32[]{:S(2)}, u32[]{:S(2)}) collective-permute-start(bf16[344,768]{1,0:T(8,128)(2,1)S(1)} %get-tuple-element.35.refs_0_.refs_2_), channel_id=1, source_target_pairs={{0,1},{1,2},{2,3},{3,0},{4,5},{5,6},{6,7},{7,4},{8,9},{9,10},{10,1... | collective-permute-start | bytes 1585160 | tf_op jit(solution)/shard_map/ppermute | solution.py:84
  18.9 7.2 %collective-permute-done.2.refs_1_ = bf16[176,1536]{1,0:T(8,128)(2,1)S(1)} collective-permute-done((bf16[176,1536]{1,0:T(8,128)(2,1)S(1)}, bf16[176,1536]{1,0:T(8,128)(2,1)S(1)}, u32[]{:S(2)}, u32[]{:S(2)}) %collective-permute-start.2) | collective-permute-done | bytes 540704 | tf_op jit(solution)/shard_map/ppermute | solution.py:84
  26.1 1.8 %shard_map.78 = (bf16[336,384]{1,0:T(8,128)(2,1)S(1)}, bf16[344,768]{1,0:T(8,128)(2,1)S(1)}) custom-call(bf16[344,768]{1,0:T(8,128)(2,1)S(1)} %get-tuple-element.35.refs_0_.refs_2_, bf16[176,1536]{1,0:T(8,128)(2,1)S(1)} %collective-permute-done.2.refs_1_, bf16[176,1536]{1,0:T(8,128)(2,1)S(1)} %collective-permute-done.3.refs_2_, ...), custom_call_target="tpu_custom_call" | custom-call | flops 1189085184 | bytes 5000000 | tf_op jit(solution)/shard_map/pallas_call | solution.py:47
  29.9 2.1 %shard_map.79 = (f32[672,384]{1,0:T(8,128)S(1)}, f32[672,128]{1,0:T(8,128)S(1)}, bf16[672,768]{1,0:T(8,128)(2,1)S(1)}) custom-call(bf16[336,384]{1,0:T(8,128)(2,1)S(1)} %get-tuple-element.34.refs_0_, bf16[336,384]{1,0:T(8,128)(2,1)S(1)} %get-tuple-element.36.refs_1_, bf16[344,768]{1,0:T(8,128)(2,1)S(1)} %get-tuple-element.35.refs_0_.refs_2_, ...), custom_call_target="tpu_custom_call" | custom-call | flops 1387266048 | bytes 2000000 | tf_op jit(solution)/shard_map/pallas_call | solution.py:47
  32.0 3.3 %shard_map.80 = (f32[672,384]{1,0:T(8,128)S(1)}, f32[672,128]{1,0:T(8,128)S(1)}) custom-call(bf16[672,768]{1,0:T(8,128)(2,1)S(1)} %get-tuple-element.38.refs_0_.refs_1_, f32[672,384]{1,0:T(8,128)S(1)} %get-tuple-element.39.refs_1_, f32[672,128]{1,0:T(8,128)S(1)} %get-tuple-element.40.refs_2_, bf16[344,768]{1,0:T(8,128)(2,1)S(1)} %collective-permute-done.5.refs_3_, ...), custom_call_target="tpu_custom_call" | custom-call | flops 1387266048 | bytes 2000000 | tf_op jit(solution)/shard_map/pallas_call | solution.py:47
  36.3 1.5 %collective-permute-start.10 = (bf16[344,768]{1,0:T(8,128)(2,1)S(1)}, bf16[344,768]{1,0:T(8,128)(2,1)S(1)}, u32[]{:S(2)}, u32[]{:S(2)}) collective-permute-start(bf16[344,768]{1,0:T(8,128)(2,1)S(1)} %collective-permute-done.8.refs_5_), channel_id=1, source_target_pairs={{0,3},{1,0},{2,1},{3,2},{4,7},{5,4},{6,5},{7,6},{8,11},{9,8},{10,9... | collective-permute-start | bytes 1585160 | tf_op jit(solution)/shard_map/ppermute | solution.py:84
  37.8 3.3 %shard_map.82 = (f32[672,384]{1,0:T(8,128)S(1)}, f32[672,128]{1,0:T(8,128)S(1)}) custom-call(f32[168,768]{1,0:T(8,128)S(1)} %shard_map.81.refs_0_, bf16[672,768]{1,0:T(8,128)(2,1)S(1)} %get-tuple-element.38.refs_0_.refs_1_, f32[672,384]{1,0:T(8,128)S(1)} %get-tuple-element.41.after_ref.refs_2_, f32[672,128]{1,0:T(8,128)S(1)} %get-tuple-element.42.refs_3_, ...), custom_call_target="tpu_custom_call" | custom-call | flops 1387266048 | bytes 2000000 | tf_op jit(solution)/shard_map/pallas_call | solution.py:47
  41.1 3.5 %collective-permute-done.9.refs_3_.refs_4_ = bf16[344,768]{1,0:T(8,128)(2,1)S(1)} collective-permute-done((bf16[344,768]{1,0:T(8,128)(2,1)S(1)}, bf16[344,768]{1,0:T(8,128)(2,1)S(1)}, u32[]{:S(2)}, u32[]{:S(2)}) %collective-permute-start.9) | collective-permute-done | bytes 528416 | tf_op jit(solution)/shard_map/ppermute | solution.py:84
  44.7 2.3 %shard_map.83 = (bf16[168,384]{1,0:T(8,128)(2,1)S(1)}, bf16[168,384]{1,0:T(8,128)(2,1)S(1)}, bf16[168,384]{1,0:T(8,128)(2,1)S(1)}) custom-call(bf16[672,768]{1,0:T(8,128)(2,1)S(1)} %get-tuple-element.38.refs_0_.refs_1_, f32[672,384]{1,0:T(8,128)S(1)} %get-tuple-element.43.refs_1_.refs_2_, f32[672,128]{1,0:T(8,128)S(1)} %get-tuple-element.44.refs_2_.refs_3_, ...), custom_call_target="tpu_custom_call" | custom-call | flops 1040449536 | bytes 2000000 | tf_op jit(solution)/shard_map/pallas_call | solution.py:47
  46.9 3.5 %collective-permute-start.11 = (bf16[168,384]{1,0:T(8,128)(2,1)S(1)}, bf16[168,384]{1,0:T(8,128)(2,1)S(1)}, u32[]{:S(2)}, u32[]{:S(2)}) collective-permute-start(bf16[168,384]{1,0:T(8,128)(2,1)S(1)} %get-tuple-element.46.refs_0_), channel_id=1, source_target_pairs={{0,12},{1,13},{2,14},{3,15},{4,0},{5,1},{6,2},{7,3},{8,4},{9,5},{1... | collective-permute-start | bytes 387080 | tf_op jit(solution)/shard_map/ppermute | solution.py:84
  50.4 2.9 %collective-permute-start.13 = (bf16[168,384]{1,0:T(8,128)(2,1)S(1)}, bf16[168,384]{1,0:T(8,128)(2,1)S(1)}, u32[]{:S(2)}, u32[]{:S(2)}) collective-permute-start(bf16[168,384]{1,0:T(8,128)(2,1)S(1)} %get-tuple-element.48), channel_id=1, source_target_pairs={{0,8},{1,9},{2,10},{3,11},{4,12},{5,13},{6,14},{7,15},{8,0},{9,1},... | collective-permute-start | bytes 387080 | tf_op jit(solution)/shard_map/ppermute | solution.py:84
  55.5 1.6 %collective-permute-done.13.a3 = bf16[168,384]{1,0:T(8,128)(2,1)S(1)} collective-permute-done((bf16[168,384]{1,0:T(8,128)(2,1)S(1)}, bf16[168,384]{1,0:T(8,128)(2,1)S(1)}, u32[]{:S(2)}, u32[]{:S(2)}) %collective-permute-start.13) | collective-permute-done | bytes 129056 | tf_op jit(solution)/shard_map/ppermute | solution.py:84
  58.2 5.2 %collective-permute-start.14 = (f32[168,768]{1,0:T(8,128)S(1)}, f32[168,768]{1,0:T(8,128)S(1)}, u32[]{:S(2)}, u32[]{:S(2)}) collective-permute-start(f32[168,768]{1,0:T(8,128)S(1)} %shard_map.86.after_ref.refs_2_), channel_id=1, source_target_pairs={{0,16},{1,17},{2,18},{3,19},{4,20},{5,21},{6,22},{7,23},{8,24},{9,... | collective-permute-start | bytes 1548296 | tf_op jit(solution)/shard_map/ppermute | solution.py:84
  65.9 13.8 %collective-permute-done.17.far_ref = f32[168,768]{1,0:T(8,128)S(1)} collective-permute-done((f32[168,768]{1,0:T(8,128)S(1)}, f32[168,768]{1,0:T(8,128)S(1)}, u32[]{:S(2)}, u32[]{:S(2)}) %collective-permute-start.17) | collective-permute-done | bytes 516128 | tf_op jit(solution)/shard_map/ppermute | solution.py:84
  81.4 1.5 %collective-permute-start.15 = (bf16[168,384]{1,0:T(8,128)(2,1)S(1)}, bf16[168,384]{1,0:T(8,128)(2,1)S(1)}, u32[]{:S(2)}, u32[]{:S(2)}) collective-permute-start(bf16[168,384]{1,0:T(8,128)(2,1)S(1)} %get-tuple-element.51), channel_id=1, source_target_pairs={{0,32},{1,33},{2,34},{3,35},{4,36},{5,37},{6,38},{7,39},{8,40},{9,... | collective-permute-start | bytes 387080 | tf_op jit(solution)/shard_map/ppermute | solution.py:84
  82.8 3.5 %collective-permute-done.16.got_ref.refs_4_ = bf16[168,384]{1,0:T(8,128)(2,1)S(1)} collective-permute-done((bf16[168,384]{1,0:T(8,128)(2,1)S(1)}, bf16[168,384]{1,0:T(8,128)(2,1)S(1)}, u32[]{:S(2)}, u32[]{:S(2)}) %collective-permute-start.16) | collective-permute-done | bytes 129056 | tf_op jit(solution)/shard_map/ppermute | solution.py:84
  87.6 1.4 %collective-permute-done.15.got_ref.refs_5_ = bf16[168,384]{1,0:T(8,128)(2,1)S(1)} collective-permute-done((bf16[168,384]{1,0:T(8,128)(2,1)S(1)}, bf16[168,384]{1,0:T(8,128)(2,1)S(1)}, u32[]{:S(2)}, u32[]{:S(2)}) %collective-permute-start.15) | collective-permute-done | bytes 129056 | tf_op jit(solution)/shard_map/ppermute | solution.py:84
  91.3 2.0 %collective-permute-done.19.far_ref.refs_6_ = bf16[168,384]{1,0:T(8,128)(2,1)S(1)} collective-permute-done((bf16[168,384]{1,0:T(8,128)(2,1)S(1)}, bf16[168,384]{1,0:T(8,128)(2,1)S(1)}, u32[]{:S(2)}, u32[]{:S(2)}) %collective-permute-start.19) | collective-permute-done | bytes 129056 | tf_op jit(solution)/shard_map/ppermute | solution.py:84
  93.8 3.3 %collective-permute-start.21 = (f32[168,384]{1,0:T(8,128)S(1)}, f32[168,384]{1,0:T(8,128)S(1)}, u32[]{:S(2)}, u32[]{:S(2)}) collective-permute-start(f32[168,384]{1,0:T(8,128)S(1)} %shard_map.93.after_ref), channel_id=1, source_target_pairs={{0,16},{1,17},{2,18},{3,19},{4,20},{5,21},{6,22},{7,23},{8,24},{9,... | collective-permute-start | bytes 774152 | tf_op jit(solution)/shard_map/ppermute | solution.py:84
  (61 shorter events, 23.3 us)
Async XLA Ops:
  5.0 10.6 %collective-permute-start.1 = (bf16[176,1536]{1,0:T(8,128)(2,1)S(1)}, bf16[176,1536]{1,0:T(8,128)(2,1)S(1)}, u32[]{:S(2)}, u32[]{:S(2)}) collective-permute-start(bf16[176,1536]{1,0:T(8,128)(2,1)S(1)} %get-tuple-element.33.refs_1_), channel_id=1, source_target_pairs={{0,4},{1,5},{2,6},{3,7},{4,8},{5,9},{6,10},{7,11},{8,12},{9,13},{1... | collective-permute-start | bytes 1622024 | tf_op jit(solution)/shard_map/ppermute | solution.py:84
  7.5 7.3 %collective-permute-start = (f32[168,768]{1,0:T(8,128)S(1)}, f32[168,768]{1,0:T(8,128)S(1)}, u32[]{:S(2)}, u32[]{:S(2)}) collective-permute-start(f32[168,768]{1,0:T(8,128)S(1)} %get-tuple-element.31.after_ref.give_ref), channel_id=1, source_target_pairs={{0,16},{1,17},{2,18},{3,19},{4,20},{5,21},{6,22},{7,23},{8,24},{9,... | collective-permute-start | bytes 1548296 | tf_op jit(solution)/shard_map/ppermute | solution.py:84
  8.2 17.8 %collective-permute-start.2 = (bf16[176,1536]{1,0:T(8,128)(2,1)S(1)}, bf16[176,1536]{1,0:T(8,128)(2,1)S(1)}, u32[]{:S(2)}, u32[]{:S(2)}) collective-permute-start(bf16[176,1536]{1,0:T(8,128)(2,1)S(1)} %get-tuple-element.33.refs_1_), channel_id=1, source_target_pairs={{0,12},{1,13},{2,14},{3,15},{4,0},{5,1},{6,2},{7,3},{8,4},{9,5},{1... | collective-permute-start | bytes 1622024 | tf_op jit(solution)/shard_map/ppermute | solution.py:84
  12.0 14.1 %collective-permute-start.3 = (bf16[176,1536]{1,0:T(8,128)(2,1)S(1)}, bf16[176,1536]{1,0:T(8,128)(2,1)S(1)}, u32[]{:S(2)}, u32[]{:S(2)}) collective-permute-start(bf16[176,1536]{1,0:T(8,128)(2,1)S(1)} %get-tuple-element.33.refs_1_), channel_id=1, source_target_pairs={{0,8},{1,9},{2,10},{3,11},{4,12},{5,13},{6,14},{7,15},{8,0},{9,1},... | collective-permute-start | bytes 1622024 | tf_op jit(solution)/shard_map/ppermute | solution.py:84
  17.3 14.7 %collective-permute-start.5 = (bf16[344,768]{1,0:T(8,128)(2,1)S(1)}, bf16[344,768]{1,0:T(8,128)(2,1)S(1)}, u32[]{:S(2)}, u32[]{:S(2)}) collective-permute-start(bf16[344,768]{1,0:T(8,128)(2,1)S(1)} %get-tuple-element.35.refs_0_.refs_2_), channel_id=1, source_target_pairs={{0,1},{1,2},{2,3},{3,0},{4,5},{5,6},{6,7},{7,4},{8,9},{9,10},{10,1... | collective-permute-start | bytes 1585160 | tf_op jit(solution)/shard_map/ppermute | solution.py:84
  18.8 13.2 %collective-permute-start.6 = (bf16[344,768]{1,0:T(8,128)(2,1)S(1)}, bf16[344,768]{1,0:T(8,128)(2,1)S(1)}, u32[]{:S(2)}, u32[]{:S(2)}) collective-permute-start(bf16[344,768]{1,0:T(8,128)(2,1)S(1)} %get-tuple-element.35.refs_0_.refs_2_), channel_id=1, source_target_pairs={{0,3},{1,0},{2,1},{3,2},{4,7},{5,4},{6,5},{7,6},{8,11},{9,8},{10,9... | collective-permute-start | bytes 1585160 | tf_op jit(solution)/shard_map/ppermute | solution.py:84
  27.8 8.4 %collective-permute-start.8 = (bf16[344,768]{1,0:T(8,128)(2,1)S(1)}, bf16[344,768]{1,0:T(8,128)(2,1)S(1)}, u32[]{:S(2)}, u32[]{:S(2)}) collective-permute-start(bf16[344,768]{1,0:T(8,128)(2,1)S(1)} %get-tuple-element.37.refs_3_), channel_id=1, source_target_pairs={{0,3},{1,0},{2,1},{3,2},{4,7},{5,4},{6,5},{7,6},{8,11},{9,8},{10,9... | collective-permute-start | bytes 1585160 | tf_op jit(solution)/shard_map/ppermute | solution.py:84
  27.9 9.8 %collective-permute-start.4 = (f32[168,768]{1,0:T(8,128)S(1)}, f32[168,768]{1,0:T(8,128)S(1)}, u32[]{:S(2)}, u32[]{:S(2)}) collective-permute-start(f32[168,768]{1,0:T(8,128)S(1)} %shard_map.76.refs_0_.a_ref), channel_id=1, source_target_pairs={{0,32},{1,33},{2,34},{3,35},{4,36},{5,37},{6,38},{7,39},{8,40},{9,... | collective-permute-start | bytes 1548296 | tf_op jit(solution)/shard_map/ppermute | solution.py:84
  28.5 9.3 %collective-permute-start.7 = (bf16[344,768]{1,0:T(8,128)(2,1)S(1)}, bf16[344,768]{1,0:T(8,128)(2,1)S(1)}, u32[]{:S(2)}, u32[]{:S(2)}) collective-permute-start(bf16[344,768]{1,0:T(8,128)(2,1)S(1)} %get-tuple-element.37.refs_3_), channel_id=1, source_target_pairs={{0,1},{1,2},{2,3},{3,0},{4,5},{5,6},{6,7},{7,4},{8,9},{9,10},{10,1... | collective-permute-start | bytes 1585160 | tf_op jit(solution)/shard_map/ppermute | solution.py:84
  36.3 8.4 %collective-permute-start.9 = (bf16[344,768]{1,0:T(8,128)(2,1)S(1)}, bf16[344,768]{1,0:T(8,128)(2,1)S(1)}, u32[]{:S(2)}, u32[]{:S(2)}) collective-permute-start(bf16[344,768]{1,0:T(8,128)(2,1)S(1)} %collective-permute-done.5.refs_3_), channel_id=1, source_target_pairs={{0,1},{1,2},{2,3},{3,0},{4,5},{5,6},{6,7},{7,4},{8,9},{9,10},{10,1... | collective-permute-start | bytes 1585160 | tf_op jit(solution)/shard_map/ppermute | solution.py:84
  36.3 8.4 %collective-permute-start.10 = (bf16[344,768]{1,0:T(8,128)(2,1)S(1)}, bf16[344,768]{1,0:T(8,128)(2,1)S(1)}, u32[]{:S(2)}, u32[]{:S(2)}) collective-permute-start(bf16[344,768]{1,0:T(8,128)(2,1)S(1)} %collective-permute-done.8.refs_5_), channel_id=1, source_target_pairs={{0,3},{1,0},{2,1},{3,2},{4,7},{5,4},{6,5},{7,6},{8,11},{9,8},{10,9... | collective-permute-start | bytes 1585160 | tf_op jit(solution)/shard_map/ppermute | solution.py:84
  46.9 8.5 %collective-permute-start.11 = (bf16[168,384]{1,0:T(8,128)(2,1)S(1)}, bf16[168,384]{1,0:T(8,128)(2,1)S(1)}, u32[]{:S(2)}, u32[]{:S(2)}) collective-permute-start(bf16[168,384]{1,0:T(8,128)(2,1)S(1)} %get-tuple-element.46.refs_0_), channel_id=1, source_target_pairs={{0,12},{1,13},{2,14},{3,15},{4,0},{5,1},{6,2},{7,3},{8,4},{9,5},{1... | collective-permute-start | bytes 387080 | tf_op jit(solution)/shard_map/ppermute | solution.py:84
  50.4 5.1 %collective-permute-start.12 = (bf16[168,384]{1,0:T(8,128)(2,1)S(1)}, bf16[168,384]{1,0:T(8,128)(2,1)S(1)}, u32[]{:S(2)}, u32[]{:S(2)}) collective-permute-start(bf16[168,384]{1,0:T(8,128)(2,1)S(1)} %get-tuple-element.47), channel_id=1, source_target_pairs={{0,4},{1,5},{2,6},{3,7},{4,8},{5,9},{6,10},{7,11},{8,12},{9,13},{1... | collective-permute-start | bytes 387080 | tf_op jit(solution)/shard_map/ppermute | solution.py:84
  50.4 6.6 %collective-permute-start.13 = (bf16[168,384]{1,0:T(8,128)(2,1)S(1)}, bf16[168,384]{1,0:T(8,128)(2,1)S(1)}, u32[]{:S(2)}, u32[]{:S(2)}) collective-permute-start(bf16[168,384]{1,0:T(8,128)(2,1)S(1)} %get-tuple-element.48), channel_id=1, source_target_pairs={{0,8},{1,9},{2,10},{3,11},{4,12},{5,13},{6,14},{7,15},{8,0},{9,1},... | collective-permute-start | bytes 387080 | tf_op jit(solution)/shard_map/ppermute | solution.py:84
  58.2 7.6 %collective-permute-start.14 = (f32[168,768]{1,0:T(8,128)S(1)}, f32[168,768]{1,0:T(8,128)S(1)}, u32[]{:S(2)}, u32[]{:S(2)}) collective-permute-start(f32[168,768]{1,0:T(8,128)S(1)} %shard_map.86.after_ref.refs_2_), channel_id=1, source_target_pairs={{0,16},{1,17},{2,18},{3,19},{4,20},{5,21},{6,22},{7,23},{8,24},{9,... | collective-permute-start | bytes 1548296 | tf_op jit(solution)/shard_map/ppermute | solution.py:84
  63.4 16.4 %collective-permute-start.17 = (f32[168,768]{1,0:T(8,128)S(1)}, f32[168,768]{1,0:T(8,128)S(1)}, u32[]{:S(2)}, u32[]{:S(2)}) collective-permute-start(f32[168,768]{1,0:T(8,128)S(1)} %shard_map.81.refs_0_), channel_id=1, source_target_pairs={{0,96},{1,97},{2,98},{3,99},{4,100},{5,101},{6,102},{7,103},{8,104... | collective-permute-start | bytes 1548296 | tf_op jit(solution)/shard_map/ppermute | solution.py:84
  65.8 24.6 %copy-start = (f32[168,1536]{1,0:T(8,128)S(1)}, f32[168,1536]{1,0:T(8,128)}, u32[]{:S(2)}) copy-start(f32[168,1536]{1,0:T(8,128)} %anchor_ref.1) | copy-start | bytes 3096580
  80.4 10.0 %collective-permute-start.18 = (f32[168,768]{1,0:T(8,128)S(1)}, f32[168,768]{1,0:T(8,128)S(1)}, u32[]{:S(2)}, u32[]{:S(2)}) collective-permute-start(f32[168,768]{1,0:T(8,128)S(1)} %shard_map.89.after_ref), channel_id=1, source_target_pairs={{0,16},{1,17},{2,18},{3,19},{4,20},{5,21},{6,22},{7,23},{8,24},{9,... | collective-permute-start | bytes 1548296 | tf_op jit(solution)/shard_map/ppermute | solution.py:84
  81.4 4.9 %collective-permute-start.16 = (bf16[168,384]{1,0:T(8,128)(2,1)S(1)}, bf16[168,384]{1,0:T(8,128)(2,1)S(1)}, u32[]{:S(2)}, u32[]{:S(2)}) collective-permute-start(bf16[168,384]{1,0:T(8,128)(2,1)S(1)} %get-tuple-element.52.after_ref), channel_id=1, source_target_pairs={{0,32},{1,33},{2,34},{3,35},{4,36},{5,37},{6,38},{7,39},{8,40},{9,... | collective-permute-start | bytes 387080 | tf_op jit(solution)/shard_map/ppermute | solution.py:84
  81.4 7.7 %collective-permute-start.15 = (bf16[168,384]{1,0:T(8,128)(2,1)S(1)}, bf16[168,384]{1,0:T(8,128)(2,1)S(1)}, u32[]{:S(2)}, u32[]{:S(2)}) collective-permute-start(bf16[168,384]{1,0:T(8,128)(2,1)S(1)} %get-tuple-element.51), channel_id=1, source_target_pairs={{0,32},{1,33},{2,34},{3,35},{4,36},{5,37},{6,38},{7,39},{8,40},{9,... | collective-permute-start | bytes 387080 | tf_op jit(solution)/shard_map/ppermute | solution.py:84
  86.3 6.9 %collective-permute-start.19 = (bf16[168,384]{1,0:T(8,128)(2,1)S(1)}, bf16[168,384]{1,0:T(8,128)(2,1)S(1)}, u32[]{:S(2)}, u32[]{:S(2)}) collective-permute-start(bf16[168,384]{1,0:T(8,128)(2,1)S(1)} %shard_map.90.after_ref), channel_id=1, source_target_pairs={{0,96},{1,97},{2,98},{3,99},{4,100},{5,101},{6,102},{7,103},{8,104... | collective-permute-start | bytes 387080 | tf_op jit(solution)/shard_map/ppermute | solution.py:84
  89.1 8.3 %collective-permute-start.20 = (bf16[168,384]{1,0:T(8,128)(2,1)S(1)}, bf16[168,384]{1,0:T(8,128)(2,1)S(1)}, u32[]{:S(2)}, u32[]{:S(2)}) collective-permute-start(bf16[168,384]{1,0:T(8,128)(2,1)S(1)} %shard_map.91.after_ref), channel_id=1, source_target_pairs={{0,96},{1,97},{2,98},{3,99},{4,100},{5,101},{6,102},{7,103},{8,104... | collective-permute-start | bytes 387080 | tf_op jit(solution)/shard_map/ppermute | solution.py:84
  93.8 6.9 %collective-permute-start.21 = (f32[168,384]{1,0:T(8,128)S(1)}, f32[168,384]{1,0:T(8,128)S(1)}, u32[]{:S(2)}, u32[]{:S(2)}) collective-permute-start(f32[168,384]{1,0:T(8,128)S(1)} %shard_map.93.after_ref), channel_id=1, source_target_pairs={{0,16},{1,17},{2,18},{3,19},{4,20},{5,21},{6,22},{7,23},{8,24},{9,... | collective-permute-start | bytes 774152 | tf_op jit(solution)/shard_map/ppermute | solution.py:84
  98.0 2.8 %collective-permute-start.22 = (f32[168,384]{1,0:T(8,128)S(1)}, f32[168,384]{1,0:T(8,128)S(1)}, u32[]{:S(2)}, u32[]{:S(2)}) collective-permute-start(f32[168,384]{1,0:T(8,128)S(1)} %shard_map.94.refs_0_), channel_id=1, source_target_pairs={{0,16},{1,17},{2,18},{3,19},{4,20},{5,21},{6,22},{7,23},{8,24},{9,... | collective-permute-start | bytes 774152 | tf_op jit(solution)/shard_map/ppermute | solution.py:84
  (2 other events, 26.4 us)

commit v3 on v2

--- a/solution.py
+++ b/solution.py
@@ -109,57 +109,72 @@
 
 
 def ones_by_frame(frame_row, rows):
-    level = lax.broadcasted_iota(jnp.int32, (128, 256), 0)
-    here = jnp.broadcast_to(frame_row, (128, 256))
+    level = lax.broadcasted_iota(jnp.int32, (128, ROWS), 0)
+    here = jnp.broadcast_to(frame_row, (128, ROWS))
     hit = jnp.where(jnp.logical_and(level % NF == here, level < rows), 1.0, 0.0)
-    return hit.T[:ROWS]
+    return hit.T
 
 
 def pick_rows(ones, table):
     return jnp.dot(ones[:, : 3 * NF], split3(table), preferred_element_type=F32)
 
 
-def norm_kernel(latent_hbm, frame_ref, feat_ref, mod_hbm, out_ref, lat_ref, mod_ref, picked_ref, sems):
-    copies = [
-        pltpu.make_async_copy(mod_hbm.at[:, pl.ds(i * D, D)], mod_ref.at[i], sems.at[i])
-        for i in range(2)
-    ]
-    copies.append(pltpu.make_async_copy(latent_hbm, lat_ref, sems.at[2]))
+def norm_kernel(
+    latent_hbm, frame_hbm, feat_ref, mod_hbm, out_ref, lat_ref, frame_ref, mod_ref, picked_ref, unit_ref, sems
+):
+    copies = [pltpu.make_async_copy(frame_hbm, frame_ref, sems.at[0])]
+    for i in range(2):
+        rows = pl.ds(i * (ROWS // 2 + 4), (88, 80)[i])
+        copies.append(
+            pltpu.make_async_copy(latent_hbm.at[rows, :], lat_ref.at[rows, :], sems.at[1 + i])
+        )
+    for i in range(4):
+        cols = pl.ds(i * HALF, HALF)
+        copies.append(pltpu.make_async_copy(mod_hbm.at[:, cols], mod_ref.at[:, cols], sems.at[3 + i]))
     for one in copies:
         one.start()
+    copies[0].wait()
     ones = ones_by_frame(frame_ref[...], 3 * NF).astype(BF16)
-    for half in range(2):
-        copies[half].wait()
-        table = jnp.dot(feat_ref[...], mod_ref[half], preferred_element_type=F32)
-        picked_ref[:, pl.ds(half * D, D)] = pick_rows(ones, table)
-    copies[2].wait()
-
-    def block(i, carry):
-        rows = pl.ds(pl.multiple_of(i * 24, 8), 24)
+    out_ref[ROWS:, :] = jnp.zeros((PACK - ROWS, D), BF16)
+    out_ref[ROWS:, :ROWS] = jnp.broadcast_to(frame_ref[...], (8, ROWS)).astype(F32).astype(BF16)
+
+    def normal(i, carry):
+        rows = pl.ds(pl.multiple_of(i * 8, 8), 8)
         latent = lat_ref[rows, :]
         center = latent - jnp.mean(latent, axis=-1, keepdims=True)
         spread = jnp.mean(center * center, axis=-1, keepdims=True)
-        normal = center * lax.rsqrt(spread + norm_eps)
-        out = normal * (1.0 + picked_ref[rows, D:]) + picked_ref[rows, :D]
-        out_ref[rows, :] = out.astype(BF16)
+        unit_ref[rows, :] = center * lax.rsqrt(spread + norm_eps)
         return carry
 
-    lax.fori_loop(0, ROWS // 24, block, 0)
-    out_ref[ROWS:, :] = jnp.zeros((PACK - ROWS, D), BF16)
-    out_ref[ROWS:, :256] = jnp.broadcast_to(frame_ref[...], (8, 256)).astype(F32).astype(BF16)
+    copies[1].wait()
+    lax.fori_loop(0, 11, normal, 0, unroll=True)
+    copies[2].wait()
+    lax.fori_loop(11, 21, normal, 0, unroll=True)
+    for i in range(4):
+        cols = pl.ds(i * HALF, HALF)
+        copies[3 + i].wait()
+        table = jnp.dot(feat_ref[...], mod_ref[:, cols], preferred_element_type=F32)
+        picked = pick_rows(ones, table)
+        if i < 2:
+            picked_ref[:, cols] = picked
+        else:
+            cols = pl.ds((i - 2) * HALF, HALF)
+            out = unit_ref[:, cols] * (1.0 + picked) + picked_ref[:, cols]
+            out_ref[:ROWS, cols] = out.astype(BF16)
 
 
 def normed_pack(latent, frame_row, features, mod_weight):
     return call(
         norm_kernel,
         (latent, frame_row, features, mod_weight),
-        [HBM, VM, VM, HBM],
-        [shaped(PACK, D, kind=BF16), shaped(ROWS, D)],
+        [HBM, HBM, VM, HBM],
+        [shaped(PACK, D, kind=BF16), shaped(ROWS, D), shaped(1, ROWS, kind=jnp.int32)],
         (30000000, 4000000, 0),
         [
-            pltpu.VMEM((2, 256, D), BF16),
-            pltpu.VMEM((ROWS, 2 * D), F32),
-            pltpu.SemaphoreType.DMA((3,)),
+            pltpu.VMEM((256, 2 * D), BF16),
+            pltpu.VMEM((ROWS, D), F32),
+            pltpu.VMEM((ROWS, D), F32),
+            pltpu.SemaphoreType.DMA((7,)),
         ],
     )
 
@@ -299,10 +314,17 @@
                 key_ref[at, pl.ds(h * 256 + HD, HD)] = block
 
         lanes_to_rows(kv_ref, put, lambda level, here: jnp.where(level == here, 1.0, 0.0))
+    used, whole_keys = n_kv * PAIR, key_ref.shape[0]
+    extra = pl.ds(used, whole_keys - used)
+    column = lax.broadcasted_iota(jnp.int32, (whole_keys - used, HD), 1)
+    last_frame = jnp.where(column == NF, 1.0, 0.0).astype(BF16)
+    for h in range(3):
+        key_ref[extra, pl.ds(h * 256, HD)] = jnp.zeros((whole_keys - used, HD), BF16)
+        key_ref[extra, pl.ds(h * 256 + HD, HD)] = last_frame
+    val_ref[extra, :] = jnp.zeros((whole_keys - used, WIDE), BF16)
 
     scale = HD**-0.5 * math.log2(math.e)
     rows = pl.ds(row0, nrows)
-    dens = []
     for h in range(3):
         cols = pl.ds(h * HD, HD)
         wide = pl.ds(h * 256, 256)
@@ -311,21 +333,20 @@
             preferred_element_type=F32,
         )
         weights = jnp.exp2(scores * scale)
-        den = jnp.sum(weights, axis=1, keepdims=True)
+        den = weights[:, :HD]
+        for i in range(1, whole_keys // HD):
+            den = den + weights[:, i * HD : (i + 1) * HD]
         num = jnp.dot(weights.astype(BF16), val_ref[:, cols], preferred_element_type=F32)
         if not first:
             num = num + num_in[rows, cols]
-            den = den + den_in[rows, h : h + 1]
+            den = den + den_in[rows, cols]
         if last:
-            done = (num / den).astype(BF16)
+            done = (num / jnp.sum(den, axis=1, keepdims=True)).astype(BF16)
             for i, out_ref in enumerate(outs):
                 out_ref[:, cols] = done[i * ROWS : (i + 1) * ROWS]
         else:
             num_ref[:, cols] = num
-            dens.append(den)
-    if not last:
-        lane = lax.broadcasted_iota(jnp.int32, (QROWS, HD), 1)
-        den_ref[...] = jnp.where(lane == 0, dens[0], jnp.where(lane == 1, dens[1], dens[2]))
+            den_ref[:, cols] = den
 
 
 def attend(kvs, queries=None, state=None, last=None, after=()):
@@ -334,7 +355,7 @@
     row0, nrows = (0, QROWS) if last is None else last
     args = (list(queries) if first else list(state)) + list(kvs)
     if last is None:
-        outs = [shaped(QROWS, WIDE), shaped(QROWS, HD)]
+        outs = [shaped(QROWS, WIDE), shaped(QROWS, WIDE)]
         if first:
             outs.append(shaped(QROWS, 768, kind=BF16))
     else:
@@ -346,8 +367,8 @@
         outs,
         (4 * nrows * PAIR * n_kv * WIDE * 2, 2000000, nrows * PAIR * 3 * n_kv),
         [
-            pltpu.VMEM((n_kv * PAIR, 768), BF16),
-            pltpu.VMEM((n_kv * PAIR, WIDE), BF16),
+            pltpu.VMEM((-(-n_kv * PAIR // HD) * HD, 768), BF16),
+            pltpu.VMEM((-(-n_kv * PAIR // HD) * HD, WIDE), BF16),
         ],
     )
     if last is not None:
@@ -436,39 +457,43 @@
     return near + jnp.where(chip >= 2, far_ref[...].astype(F32), 0.0)
 
 
-def back_kernel(col0, where_ref, after_ref, keep_ref, got_ref, far_ref, out_ref):
-    mine = keep_ref[:, pl.ds(col0, got_ref.shape[1])]
-    extra = jnp.where(where_ref[1] == 0, mine, 0.0)
+def back_kernel(col0, where_ref, keep_ref, got_ref, far_ref, lat_ref, out_ref):
+    cols = pl.ds(col0, got_ref.shape[1])
+    extra = jnp.where(where_ref[1] == 0, keep_ref[:, cols], 0.0) + lat_ref[:, cols]
     out_ref[...] = before_sum(where_ref, got_ref, far_ref) + extra
 
 
-def back_sum(where, after, keep, got, far, col0=0):
-    return call(
-        functools.partial(back_kernel, col0),
-        (where, after, keep, got, far),
-        [SM, ANY] + [VM] * 3,
+def back_sum(where, after, keep, got, far, lat, col0=0):
+    return call(
+        lambda _, *refs: back_kernel(col0, *refs),
+        (after, where, keep, got, far, lat),
+        [ANY, SM] + [VM] * 4,
         [shaped(*got.shape)],
         (ROWS * HALF, 2000000, 0),
     )[0]
 
 
-def base_kernel(where_ref, after_ref, anchor_ref, keep_ref, give_ref, beside_ref, got_ref, far_ref, back_ref, out_ref):
+def base_kernel(
+    where_ref, after_ref, anchor_ref, keep_ref, give_ref, beside_ref, got_ref, far_ref, own_ref, other_ref, back_ref
+):
     core = where_ref[1]
     mine = pl.ds(pl.multiple_of(core * HALF, 128), HALF)
     other = pl.ds(pl.multiple_of((1 - core) * HALF, 128), HALF)
-    own = before_sum(where_ref, got_ref, far_ref) + jnp.where(core == 1, beside_ref[...], 0.0)
-    out_ref[:, mine] = anchor_ref[:, mine] + (keep_ref[...] + own)
-    out_ref[:, other] = anchor_ref[:, other] + (give_ref[...] + back_ref[...])
+    before = before_sum(where_ref, got_ref, far_ref)
+    own = before + jnp.where(core == 1, beside_ref[...], 0.0)
+    own_ref[...] = anchor_ref[:, mine] + (keep_ref[...] + own)
+    other_ref[...] = anchor_ref[:, other] + give_ref[...]
+    back_ref[...] = before + jnp.where(core == 0, keep_ref[...], 0.0)
 
 
 def base_sum(where, after, *terms):
     return call(
         base_kernel,
         (where, after, *terms),
-        [SM, ANY] + [VM] * 7,
-        [shaped(ROWS, D)],
+        [SM, ANY] + [VM] * 6,
+        [shaped(ROWS, HALF)] * 3,
         (ROWS * D * 2, 4000000, 0),
-    )[0]
+    )
 
 
 def final_kernel(own, where_ref, *refs):
@@ -488,7 +513,7 @@
             term = keep_ref[:, part] + more
         else:
             term = give_ref[:, part] + (b0, b1)[i][...]
-        buf_ref[:, part] = base_ref[:, at] + term
+        buf_ref[:, part] = base_ref[:, part] + term
         copies.append(pltpu.make_async_copy(buf_ref.at[:, part], out_hbm.at[:, at], sems.at[i]))
         copies[-1].start()
     for one in copies:
@@ -529,10 +554,10 @@
     latent = held(iterate[0])
     features, gap = frame_features(noise_steps[0])
     gap = jnp.pad(gap, (0, 128 - NF))[None, :]
-    frame_row = jnp.pad(frame_index, (0, 256 - ROWS))[None, :]
+    frame_row = held(frame_index[None, :])
 
     tie = lax.optimization_barrier
-    mine, latent = normed_pack(latent, frame_row, features, mod_weight)
+    mine, latent, frame_row = normed_pack(latent, frame_row, features, mod_weight)
     from_prev = send(mine, along("a", 1))
     from_next = send(mine, along("a", -1))
     from_far = send(mine, along("a", 2))
@@ -551,14 +576,13 @@
     down1 = send(kv1, along("b", -1))
     up1 = send(kv1, along("b", 1))
     far0 = send(up0, along("b", 1))
-    state = attend([kv0, kv1], queries=(q0, q1))
-    state = attend([up0, down0], state=state)
+    state = attend([kv0, kv1, up0, down0], queries=(q0, q1))
     down1_later, _ = tie((down1, state[1]))
     far1 = send(down1_later, along("b", -1))
+    state = attend([up1, down1], state=state)
     (lat_wire,) = add_up(lat_both, lat_got, F32, state[1])
+    a1, a2, a3 = attend([far0, far1], state=state, last=(ROWS, 3 * ROWS), after=(lat_wire,))
     lat_far = send(lat_wire, ROUND2)
-    state = attend([up1, down1], state=state, after=(lat_wire,))
-    a1, a2, a3 = attend([far0, far1], state=state, last=(ROWS, 3 * ROWS))
     b3 = send(a3, along("a", -2))
     b1 = send(a1, along("a", -1))
     b2 = send(a2, along("a", 1))
@@ -571,21 +595,19 @@
     both, wire0, wire1 = add_up(keep, beside, BF16, keep, n_parts=2, keep=True)
     got0 = send(wire0, ROUND1)
     got1 = send(wire1, ROUND1)
-    lat_sum = back_sum(where, wire0, lat_keep, lat_got, lat_far)
-    lat_back = send(lat_sum, SWAP)
-    pair0 = pair_up(0, both, got0, lat_sum)
+    pair0 = pair_up(0, both, got0, wire0)
     far0 = send(pair0, ROUND2)
     pair1 = pair_up(1, both, got1, pair0)
     far1 = send(pair1, ROUND2)
-    base = base_sum(
-        where, pair1, anchor, lat_keep, lat_give, lat_beside, lat_got, lat_far, lat_back
-    )
-    sum0 = back_sum(where, base, keep, got0, far0)
+    base_own, base_other, lat_sum = base_sum(
+        where, pair1, anchor, lat_keep, lat_give, lat_beside, lat_got, lat_far
+    )
+    sum0 = back_sum(where, pair1, keep, got0, far0, lat_sum)
     back0 = send(sum0, SWAP)
-    sum1 = back_sum(where, sum0, keep, got1, far1, QUART)
+    sum1 = back_sum(where, sum0, keep, got1, far1, lat_sum, QUART)
     back1 = send(sum1, SWAP)
-    out = final_sum(True, (where, sum1, base, keep, beside, got0, got1, far0, far1))
-    out = final_sum(False, (where, out, base, give, back0, back1))
+    out = final_sum(True, (where, sum1, base_own, keep, beside, got0, got1, far0, far1))
+    out = final_sum(False, (where, out, base_other, give, back0, back1))
     return out[None]
 
 

time: 104 us -> 91.6 us (0.88)
  waiting for transfers between devices: 34.9 us -> 29.8 us
  Pallas kernels: 31.7 us -> 27.5 us
  starting transfers between devices: 33.7 us -> 31.6 us
    ppermute x23 -> x22, waiting for transfers between devices: 34.9 us -> 29.8 us  [send(): return lax.ppermute(value, AXES, route)]
    pallas_call x22 -> x20, Pallas kernels: 28.9 us -> 24.7 us  [run_kernel(): pl.pallas_call(kernel, in_specs=specs, out_specs=[VM] * len(outs) if out_...]
    ppermute x23 -> x22, starting transfers between devices: 33.7 us -> 31.6 us  [send(): return lax.ppermute(value, AXES, route)]
  transfers between devices with their start and end apart: 23 -> 22, of which waited for: 10 -> 10; matrix products, arithmetic and copies ran while one was open for 0% -> 0% of each run, Pallas kernels for 22% -> 22%
where the time goes in v3:
time: 91.6 us; the launch traced here: 90.3 us
  starting transfers between devices  31.6 us (34%)
  waiting for transfers between devices  29.8 us (33%)
  Pallas kernels  27.5 us (30%)
    ppermute x22, starting transfers between devices, send(): return lax.ppermute(value, AXES, route)  31.6 us
    ppermute x22, waiting for transfers between devices, send(): return lax.ppermute(value, AXES, route)  29.8 us
    pallas_call x20, Pallas kernels, run_kernel(): pl.pallas_call(kernel, in_specs=specs, out_specs=[VM] * len(outs) if out_...  24.7 us
    pallas_call x2, Pallas kernels, final_sum(): pl.pallas_call(functools.partial(final_kernel, own), in_specs=[SM, HBM if...  2.82 us
  transfers between devices with their start and end apart: 22, of which 10 were waited for; matrix products, arithmetic and copies ran while one was open for 0% of the time, Pallas kernels for 22%

profile of v3, /device:TPU:15, one launch (start us, length us, event | category | flops | bytes accessed | tf_op | source)
XLA Modules:
  0.0 90.3 jit_solution(8151576753081996195)
XLA Ops:
  0.8 3.1 %shard_map.73 = (bf16[176,1536]{1,0:T(8,128)(2,1)S(1)}, f32[168,1536]{1,0:T(8,128)S(1)}, s32[1,168]{1,0:T(1,128)S(1)}) custom-call(f32[168,1536]{1,0:T(8,128)} %bitcast.14, s32[1,168]{1,0:T(1,128)} %bitcast.15, bf16[16,256]{1,0:T(8,128)(2,1)S(1)} %pad_maximum_fusion.feat_ref, bf16[256,4608]{1,0:T(8,128)(2,1)} %mod_hbm.3), custom_call_target="tpu_custom_call" | custom-call | flops 30000000 | bytes 4000000 | tf_op jit(solution)/shard_map/pallas_call | solution.py:47
  4.0 1.7 %collective-permute-start.2 = (bf16[176,1536]{1,0:T(8,128)(2,1)S(1)}, bf16[176,1536]{1,0:T(8,128)(2,1)S(1)}, u32[]{:S(2)}, u32[]{:S(2)}) collective-permute-start(bf16[176,1536]{1,0:T(8,128)(2,1)S(1)} %get-tuple-element.36.refs_1_), channel_id=1, source_target_pairs={{0,4},{1,5},{2,6},{3,7},{4,8},{5,9},{6,10},{7,11},{8,12},{9,13},{1... | collective-permute-start | bytes 1622024 | tf_op jit(solution)/shard_map/ppermute | solution.py:84
  7.2 3.8 %collective-permute-start.3 = (bf16[176,1536]{1,0:T(8,128)(2,1)S(1)}, bf16[176,1536]{1,0:T(8,128)(2,1)S(1)}, u32[]{:S(2)}, u32[]{:S(2)}) collective-permute-start(bf16[176,1536]{1,0:T(8,128)(2,1)S(1)} %get-tuple-element.36.refs_1_), channel_id=1, source_target_pairs={{0,12},{1,13},{2,14},{3,15},{4,0},{5,1},{6,2},{7,3},{8,4},{9,5},{1... | collective-permute-start | bytes 1622024 | tf_op jit(solution)/shard_map/ppermute | solution.py:84
  11.0 2.8 %shard_map.75 = (f32[168,1536]{1,0:T(8,128)S(1)}, bf16[1536,1152]{1,0:T(8,128)(2,1)S(1)}) custom-call(s32[3]{0:T(128)S(1)} %pad_add_fusion.where_ref.refs_0_, f32[168,768]{1,0:T(8,128)S(1)} %get-tuple-element.34.after_ref.give_ref, s32[1,168]{1,0:T(1,128)S(1)} %get-tuple-element.32.frame_ref, f32[1,128]{1,0:T(1,128)S(1)} %pad_bitcast_fusion.gap_ref, ...), custom_call_target="tpu_custom_call" | custom-call | flops 30000000 | bytes 6000000 | tf_op jit(solution)/shard_map/pallas_call | solution.py:47
  14.5 1.8 %shard_map.77 = (bf16[336,384]{1,0:T(8,128)(2,1)S(1)}, bf16[344,768]{1,0:T(8,128)(2,1)S(1)}) custom-call(f32[168,768]{1,0:T(8,128)S(1)} %shard_map.76.refs_0_.a_ref, bf16[176,1536]{1,0:T(8,128)(2,1)S(1)} %get-tuple-element.36.refs_1_, bf16[176,1536]{1,0:T(8,128)(2,1)S(1)} %collective-permute-done.2.refs_2_, ...), custom_call_target="tpu_custom_call" | custom-call | flops 1189085184 | bytes 5000000 | tf_op jit(solution)/shard_map/pallas_call | solution.py:47
  16.3 1.5 %collective-permute-start.5 = (bf16[344,768]{1,0:T(8,128)(2,1)S(1)}, bf16[344,768]{1,0:T(8,128)(2,1)S(1)}, u32[]{:S(2)}, u32[]{:S(2)}) collective-permute-start(bf16[344,768]{1,0:T(8,128)(2,1)S(1)} %get-tuple-element.38.refs_0_.refs_2_), channel_id=1, source_target_pairs={{0,1},{1,2},{2,3},{3,0},{4,5},{5,6},{6,7},{7,4},{8,9},{9,10},{10,1... | collective-permute-start | bytes 1585160 | tf_op jit(solution)/shard_map/ppermute | solution.py:84
  17.9 7.2 %collective-permute-done.3.refs_1_ = bf16[176,1536]{1,0:T(8,128)(2,1)S(1)} collective-permute-done((bf16[176,1536]{1,0:T(8,128)(2,1)S(1)}, bf16[176,1536]{1,0:T(8,128)(2,1)S(1)}, u32[]{:S(2)}, u32[]{:S(2)}) %collective-permute-start.3) | collective-permute-done | bytes 540704 | tf_op jit(solution)/shard_map/ppermute | solution.py:84
  25.0 1.8 %shard_map.78 = (bf16[336,384]{1,0:T(8,128)(2,1)S(1)}, bf16[344,768]{1,0:T(8,128)(2,1)S(1)}) custom-call(bf16[344,768]{1,0:T(8,128)(2,1)S(1)} %get-tuple-element.38.refs_0_.refs_2_, bf16[176,1536]{1,0:T(8,128)(2,1)S(1)} %collective-permute-done.3.refs_1_, bf16[176,1536]{1,0:T(8,128)(2,1)S(1)} %collective-permute-done.4.refs_2_, ...), custom_call_target="tpu_custom_call" | custom-call | flops 1189085184 | bytes 5000000 | tf_op jit(solution)/shard_map/pallas_call | solution.py:47
  26.9 1.5 %collective-permute-start.7 = (bf16[344,768]{1,0:T(8,128)(2,1)S(1)}, bf16[344,768]{1,0:T(8,128)(2,1)S(1)}, u32[]{:S(2)}, u32[]{:S(2)}) collective-permute-start(bf16[344,768]{1,0:T(8,128)(2,1)S(1)} %get-tuple-element.40.refs_3_), channel_id=1, source_target_pairs={{0,1},{1,2},{2,3},{3,0},{4,5},{5,6},{6,7},{7,4},{8,9},{9,10},{10,1... | collective-permute-start | bytes 1585160 | tf_op jit(solution)/shard_map/ppermute | solution.py:84
  28.4 3.9 %shard_map.79 = (f32[672,384]{1,0:T(8,128)S(1)}, f32[672,384]{1,0:T(8,128)S(1)}, bf16[672,768]{1,0:T(8,128)(2,1)S(1)}) custom-call(bf16[336,384]{1,0:T(8,128)(2,1)S(1)} %get-tuple-element.37.refs_0_, bf16[336,384]{1,0:T(8,128)(2,1)S(1)} %get-tuple-element.39.refs_1_, bf16[344,768]{1,0:T(8,128)(2,1)S(1)} %get-tuple-element.38.refs_0_.refs_2_, ...), custom_call_target="tpu_custom_call" | custom-call | flops 2774532096 | bytes 2000000 | tf_op jit(solution)/shard_map/pallas_call | solution.py:47
  32.3 3.0 %collective-permute-done.8.refs_4_ = bf16[344,768]{1,0:T(8,128)(2,1)S(1)} collective-permute-done((bf16[344,768]{1,0:T(8,128)(2,1)S(1)}, bf16[344,768]{1,0:T(8,128)(2,1)S(1)}, u32[]{:S(2)}, u32[]{:S(2)}) %collective-permute-start.8) | collective-permute-done | bytes 528416 | tf_op jit(solution)/shard_map/ppermute | solution.py:84
  35.3 1.5 %collective-permute-start.10 = (bf16[344,768]{1,0:T(8,128)(2,1)S(1)}, bf16[344,768]{1,0:T(8,128)(2,1)S(1)}, u32[]{:S(2)}, u32[]{:S(2)}) collective-permute-start(bf16[344,768]{1,0:T(8,128)(2,1)S(1)} %collective-permute-done.8.refs_4_), channel_id=1, source_target_pairs={{0,3},{1,0},{2,1},{3,2},{4,7},{5,4},{6,5},{7,6},{8,11},{9,8},{10,9... | collective-permute-start | bytes 1585160 | tf_op jit(solution)/shard_map/ppermute | solution.py:84
  37.3 2.1 %shard_map.80 = (f32[672,384]{1,0:T(8,128)S(1)}, f32[672,384]{1,0:T(8,128)S(1)}) custom-call(bf16[672,768]{1,0:T(8,128)(2,1)S(1)} %get-tuple-element.41.refs_0_.refs_1_, f32[672,384]{1,0:T(8,128)S(1)} %get-tuple-element.42.refs_1_, f32[672,384]{1,0:T(8,128)S(1)} %get-tuple-element.43.refs_2_, bf16[344,768]{1,0:T(8,128)(2,1)S(1)} %collective-permute-done.7.refs_3_, ...), custom_call_target="tpu_custom_call" | custom-call | flops 1387266048 | bytes 2000000 | tf_op jit(solution)/shard_map/pallas_call | solution.py:47
  39.4 5.6 %collective-permute-done.1.b_ref.got_ref = f32[168,768]{1,0:T(8,128)S(1)} collective-permute-done((f32[168,768]{1,0:T(8,128)S(1)}, f32[168,768]{1,0:T(8,128)S(1)}, u32[]{:S(2)}, u32[]{:S(2)}) %collective-permute-start.1) | collective-permute-done | bytes 516128 | tf_op jit(solution)/shard_map/ppermute | solution.py:84
  45.1 1.7 %shard_map.82 = (bf16[168,384]{1,0:T(8,128)(2,1)S(1)}, bf16[168,384]{1,0:T(8,128)(2,1)S(1)}, bf16[168,384]{1,0:T(8,128)(2,1)S(1)}) custom-call(f32[168,768]{1,0:T(8,128)S(1)} %shard_map.81.refs_0_, bf16[672,768]{1,0:T(8,128)(2,1)S(1)} %get-tuple-element.41.refs_0_.refs_1_, f32[672,384]{1,0:T(8,128)S(1)} %get-tuple-element.44.after_ref.refs_2_, ...), custom_call_target="tpu_custom_call" | custom-call | flops 1040449536 | bytes 2000000 | tf_op jit(solution)/shard_map/pallas_call | solution.py:47
  46.8 3.8 %collective-permute-start.11 = (bf16[168,384]{1,0:T(8,128)(2,1)S(1)}, bf16[168,384]{1,0:T(8,128)(2,1)S(1)}, u32[]{:S(2)}, u32[]{:S(2)}) collective-permute-start(bf16[168,384]{1,0:T(8,128)(2,1)S(1)} %get-tuple-element.47.refs_0_), channel_id=1, source_target_pairs={{0,12},{1,13},{2,14},{3,15},{4,0},{5,1},{6,2},{7,3},{8,4},{9,5},{1... | collective-permute-start | bytes 387080 | tf_op jit(solution)/shard_map/ppermute | solution.py:84
  50.6 2.9 %collective-permute-start.13 = (bf16[168,384]{1,0:T(8,128)(2,1)S(1)}, bf16[168,384]{1,0:T(8,128)(2,1)S(1)}, u32[]{:S(2)}, u32[]{:S(2)}) collective-permute-start(bf16[168,384]{1,0:T(8,128)(2,1)S(1)} %get-tuple-element.49), channel_id=1, source_target_pairs={{0,8},{1,9},{2,10},{3,11},{4,12},{5,13},{6,14},{7,15},{8,0},{9,1},... | collective-permute-start | bytes 387080 | tf_op jit(solution)/shard_map/ppermute | solution.py:84
  55.7 1.6 %collective-permute-done.13.a3 = bf16[168,384]{1,0:T(8,128)(2,1)S(1)} collective-permute-done((bf16[168,384]{1,0:T(8,128)(2,1)S(1)}, bf16[168,384]{1,0:T(8,128)(2,1)S(1)}, u32[]{:S(2)}, u32[]{:S(2)}) %collective-permute-start.13) | collective-permute-done | bytes 129056 | tf_op jit(solution)/shard_map/ppermute | solution.py:84
  58.4 5.4 %collective-permute-start.14 = (f32[168,768]{1,0:T(8,128)S(1)}, f32[168,768]{1,0:T(8,128)S(1)}, u32[]{:S(2)}, u32[]{:S(2)}) collective-permute-start(f32[168,768]{1,0:T(8,128)S(1)} %shard_map.85.after_ref.refs_2_), channel_id=1, source_target_pairs={{0,16},{1,17},{2,18},{3,19},{4,20},{5,21},{6,22},{7,23},{8,24},{9,... | collective-permute-start | bytes 1548296 | tf_op jit(solution)/shard_map/ppermute | solution.py:84
  67.9 3.4 %collective-permute-done.16.got_ref.refs_2_.refs_4_ = bf16[168,384]{1,0:T(8,128)(2,1)S(1)} collective-permute-done((bf16[168,384]{1,0:T(8,128)(2,1)S(1)}, bf16[168,384]{1,0:T(8,128)(2,1)S(1)}, u32[]{:S(2)}, u32[]{:S(2)}) %collective-permute-start.16) | collective-permute-done | bytes 129056 | tf_op jit(solution)/shard_map/ppermute | solution.py:84
  72.6 1.4 %collective-permute-done.15.got_ref.refs_2_.refs_5_ = bf16[168,384]{1,0:T(8,128)(2,1)S(1)} collective-permute-done((bf16[168,384]{1,0:T(8,128)(2,1)S(1)}, bf16[168,384]{1,0:T(8,128)(2,1)S(1)}, u32[]{:S(2)}, u32[]{:S(2)}) %collective-permute-start.15) | collective-permute-done | bytes 129056 | tf_op jit(solution)/shard_map/ppermute | solution.py:84
  75.3 4.7 %collective-permute-done.18.far_ref = f32[168,768]{1,0:T(8,128)S(1)} collective-permute-done((f32[168,768]{1,0:T(8,128)S(1)}, f32[168,768]{1,0:T(8,128)S(1)}, u32[]{:S(2)}, u32[]{:S(2)}) %collective-permute-start.18) | collective-permute-done | bytes 516128 | tf_op jit(solution)/shard_map/ppermute | solution.py:84
  80.9 1.9 %collective-permute-done.17.refs_3_.refs_6_ = bf16[168,384]{1,0:T(8,128)(2,1)S(1)} collective-permute-done((bf16[168,384]{1,0:T(8,128)(2,1)S(1)}, bf16[168,384]{1,0:T(8,128)(2,1)S(1)}, u32[]{:S(2)}, u32[]{:S(2)}) %collective-permute-start.17) | collective-permute-done | bytes 129056 | tf_op jit(solution)/shard_map/ppermute | solution.py:84
  83.4 1.7 %collective-permute-start.20 = (f32[168,384]{1,0:T(8,128)S(1)}, f32[168,384]{1,0:T(8,128)S(1)}, u32[]{:S(2)}, u32[]{:S(2)}) collective-permute-start(f32[168,384]{1,0:T(8,128)S(1)} %shard_map.91._), channel_id=1, source_target_pairs={{0,16},{1,17},{2,18},{3,19},{4,20},{5,21},{6,22},{7,23},{8,24},{9,... | collective-permute-start | bytes 774152 | tf_op jit(solution)/shard_map/ppermute | solution.py:84
  (56 shorter events, 20.2 us)
Async XLA Ops:
  4.0 10.6 %collective-permute-start.2 = (bf16[176,1536]{1,0:T(8,128)(2,1)S(1)}, bf16[176,1536]{1,0:T(8,128)(2,1)S(1)}, u32[]{:S(2)}, u32[]{:S(2)}) collective-permute-start(bf16[176,1536]{1,0:T(8,128)(2,1)S(1)} %get-tuple-element.36.refs_1_), channel_id=1, source_target_pairs={{0,4},{1,5},{2,6},{3,7},{4,8},{5,9},{6,10},{7,11},{8,12},{9,13},{1... | collective-permute-start | bytes 1622024 | tf_op jit(solution)/shard_map/ppermute | solution.py:84
  6.5 7.3 %collective-permute-start = (f32[168,768]{1,0:T(8,128)S(1)}, f32[168,768]{1,0:T(8,128)S(1)}, u32[]{:S(2)}, u32[]{:S(2)}) collective-permute-start(f32[168,768]{1,0:T(8,128)S(1)} %get-tuple-element.34.after_ref.give_ref), channel_id=1, source_target_pairs={{0,16},{1,17},{2,18},{3,19},{4,20},{5,21},{6,22},{7,23},{8,24},{9,... | collective-permute-start | bytes 1548296 | tf_op jit(solution)/shard_map/ppermute | solution.py:84
  7.2 17.8 %collective-permute-start.3 = (bf16[176,1536]{1,0:T(8,128)(2,1)S(1)}, bf16[176,1536]{1,0:T(8,128)(2,1)S(1)}, u32[]{:S(2)}, u32[]{:S(2)}) collective-permute-start(bf16[176,1536]{1,0:T(8,128)(2,1)S(1)} %get-tuple-element.36.refs_1_), channel_id=1, source_target_pairs={{0,12},{1,13},{2,14},{3,15},{4,0},{5,1},{6,2},{7,3},{8,4},{9,5},{1... | collective-permute-start | bytes 1622024 | tf_op jit(solution)/shard_map/ppermute | solution.py:84
  11.0 14.1 %collective-permute-start.4 = (bf16[176,1536]{1,0:T(8,128)(2,1)S(1)}, bf16[176,1536]{1,0:T(8,128)(2,1)S(1)}, u32[]{:S(2)}, u32[]{:S(2)}) collective-permute-start(bf16[176,1536]{1,0:T(8,128)(2,1)S(1)} %get-tuple-element.36.refs_1_), channel_id=1, source_target_pairs={{0,8},{1,9},{2,10},{3,11},{4,12},{5,13},{6,14},{7,15},{8,0},{9,1},... | collective-permute-start | bytes 1622024 | tf_op jit(solution)/shard_map/ppermute | solution.py:84
  16.3 12.0 %collective-permute-start.5 = (bf16[344,768]{1,0:T(8,128)(2,1)S(1)}, bf16[344,768]{1,0:T(8,128)(2,1)S(1)}, u32[]{:S(2)}, u32[]{:S(2)}) collective-permute-start(bf16[344,768]{1,0:T(8,128)(2,1)S(1)} %get-tuple-element.38.refs_0_.refs_2_), channel_id=1, source_target_pairs={{0,1},{1,2},{2,3},{3,0},{4,5},{5,6},{6,7},{7,4},{8,9},{9,10},{10,1... | collective-permute-start | bytes 1585160 | tf_op jit(solution)/shard_map/ppermute | solution.py:84
  17.8 10.5 %collective-permute-start.6 = (bf16[344,768]{1,0:T(8,128)(2,1)S(1)}, bf16[344,768]{1,0:T(8,128)(2,1)S(1)}, u32[]{:S(2)}, u32[]{:S(2)}) collective-permute-start(bf16[344,768]{1,0:T(8,128)(2,1)S(1)} %get-tuple-element.38.refs_0_.refs_2_), channel_id=1, source_target_pairs={{0,3},{1,0},{2,1},{3,2},{4,7},{5,4},{6,5},{7,6},{8,11},{9,8},{10,9... | collective-permute-start | bytes 1585160 | tf_op jit(solution)/shard_map/ppermute | solution.py:84
  26.8 8.4 %collective-permute-start.8 = (bf16[344,768]{1,0:T(8,128)(2,1)S(1)}, bf16[344,768]{1,0:T(8,128)(2,1)S(1)}, u32[]{:S(2)}, u32[]{:S(2)}) collective-permute-start(bf16[344,768]{1,0:T(8,128)(2,1)S(1)} %get-tuple-element.40.refs_3_), channel_id=1, source_target_pairs={{0,3},{1,0},{2,1},{3,2},{4,7},{5,4},{6,5},{7,6},{8,11},{9,8},{10,9... | collective-permute-start | bytes 1585160 | tf_op jit(solution)/shard_map/ppermute | solution.py:84
  26.9 10.4 %collective-permute-start.7 = (bf16[344,768]{1,0:T(8,128)(2,1)S(1)}, bf16[344,768]{1,0:T(8,128)(2,1)S(1)}, u32[]{:S(2)}, u32[]{:S(2)}) collective-permute-start(bf16[344,768]{1,0:T(8,128)(2,1)S(1)} %get-tuple-element.40.refs_3_), channel_id=1, source_target_pairs={{0,1},{1,2},{2,3},{3,0},{4,5},{5,6},{6,7},{7,4},{8,9},{9,10},{10,1... | collective-permute-start | bytes 1585160 | tf_op jit(solution)/shard_map/ppermute | solution.py:84
  35.3 9.8 %collective-permute-start.9 = (bf16[344,768]{1,0:T(8,128)(2,1)S(1)}, bf16[344,768]{1,0:T(8,128)(2,1)S(1)}, u32[]{:S(2)}, u32[]{:S(2)}) collective-permute-start(bf16[344,768]{1,0:T(8,128)(2,1)S(1)} %collective-permute-done.5.refs_4_), channel_id=1, source_target_pairs={{0,1},{1,2},{2,3},{3,0},{4,5},{5,6},{6,7},{7,4},{8,9},{9,10},{10,1... | collective-permute-start | bytes 1585160 | tf_op jit(solution)/shard_map/ppermute | solution.py:84
  35.3 9.8 %collective-permute-start.10 = (bf16[344,768]{1,0:T(8,128)(2,1)S(1)}, bf16[344,768]{1,0:T(8,128)(2,1)S(1)}, u32[]{:S(2)}, u32[]{:S(2)}) collective-permute-start(bf16[344,768]{1,0:T(8,128)(2,1)S(1)} %collective-permute-done.8.refs_4_), channel_id=1, source_target_pairs={{0,3},{1,0},{2,1},{3,2},{4,7},{5,4},{6,5},{7,6},{8,11},{9,8},{10,9... | collective-permute-start | bytes 1585160 | tf_op jit(solution)/shard_map/ppermute | solution.py:84
  36.7 8.2 %collective-permute-start.1 = (f32[168,768]{1,0:T(8,128)S(1)}, f32[168,768]{1,0:T(8,128)S(1)}, u32[]{:S(2)}, u32[]{:S(2)}) collective-permute-start(f32[168,768]{1,0:T(8,128)S(1)} %shard_map.76.refs_0_.a_ref), channel_id=1, source_target_pairs={{0,32},{1,33},{2,34},{3,35},{4,36},{5,37},{6,38},{7,39},{8,40},{9,... | collective-permute-start | bytes 1548296 | tf_op jit(solution)/shard_map/ppermute | solution.py:84
  45.0 9.6 %slice-start = ((s8[4718592]{0:T(1024)(128)(4,1)}), s8[4194304]{0:T(1024)(128)(4,1)S(1)}, s32[]{:S(2)}) async-start(s8[4718592]{0:T(1024)(128)(4,1)} %bitcast.12), calls=%async_computation | async-start | bytes 8388608
  46.8 8.9 %collective-permute-start.11 = (bf16[168,384]{1,0:T(8,128)(2,1)S(1)}, bf16[168,384]{1,0:T(8,128)(2,1)S(1)}, u32[]{:S(2)}, u32[]{:S(2)}) collective-permute-start(bf16[168,384]{1,0:T(8,128)(2,1)S(1)} %get-tuple-element.47.refs_0_), channel_id=1, source_target_pairs={{0,12},{1,13},{2,14},{3,15},{4,0},{5,1},{6,2},{7,3},{8,4},{9,5},{1... | collective-permute-start | bytes 387080 | tf_op jit(solution)/shard_map/ppermute | solution.py:84
  50.6 5.1 %collective-permute-start.12 = (bf16[168,384]{1,0:T(8,128)(2,1)S(1)}, bf16[168,384]{1,0:T(8,128)(2,1)S(1)}, u32[]{:S(2)}, u32[]{:S(2)}) collective-permute-start(bf16[168,384]{1,0:T(8,128)(2,1)S(1)} %get-tuple-element.48), channel_id=1, source_target_pairs={{0,4},{1,5},{2,6},{3,7},{4,8},{5,9},{6,10},{7,11},{8,12},{9,13},{1... | collective-permute-start | bytes 387080 | tf_op jit(solution)/shard_map/ppermute | solution.py:84
  50.6 6.6 %collective-permute-start.13 = (bf16[168,384]{1,0:T(8,128)(2,1)S(1)}, bf16[168,384]{1,0:T(8,128)(2,1)S(1)}, u32[]{:S(2)}, u32[]{:S(2)}) collective-permute-start(bf16[168,384]{1,0:T(8,128)(2,1)S(1)} %get-tuple-element.49), channel_id=1, source_target_pairs={{0,8},{1,9},{2,10},{3,11},{4,12},{5,13},{6,14},{7,15},{8,0},{9,1},... | collective-permute-start | bytes 387080 | tf_op jit(solution)/shard_map/ppermute | solution.py:84
  58.4 21.6 %copy-start = (f32[168,1536]{1,0:T(8,128)S(1)}, f32[168,1536]{1,0:T(8,128)}, u32[]{:S(2)}) copy-start(f32[168,1536]{1,0:T(8,128)} %anchor_ref.1) | copy-start | bytes 3096580
  58.4 7.8 %collective-permute-start.14 = (f32[168,768]{1,0:T(8,128)S(1)}, f32[168,768]{1,0:T(8,128)S(1)}, u32[]{:S(2)}, u32[]{:S(2)}) collective-permute-start(f32[168,768]{1,0:T(8,128)S(1)} %shard_map.85.after_ref.refs_2_), channel_id=1, source_target_pairs={{0,16},{1,17},{2,18},{3,19},{4,20},{5,21},{6,22},{7,23},{8,24},{9,... | collective-permute-start | bytes 1548296 | tf_op jit(solution)/shard_map/ppermute | solution.py:84
  63.8 16.2 %collective-permute-start.18 = (f32[168,768]{1,0:T(8,128)S(1)}, f32[168,768]{1,0:T(8,128)S(1)}, u32[]{:S(2)}, u32[]{:S(2)}) collective-permute-start(f32[168,768]{1,0:T(8,128)S(1)} %shard_map.81.refs_0_), channel_id=1, source_target_pairs={{0,96},{1,97},{2,98},{3,99},{4,100},{5,101},{6,102},{7,103},{8,104... | collective-permute-start | bytes 1548296 | tf_op jit(solution)/shard_map/ppermute | solution.py:84
  66.3 4.9 %collective-permute-start.16 = (bf16[168,384]{1,0:T(8,128)(2,1)S(1)}, bf16[168,384]{1,0:T(8,128)(2,1)S(1)}, u32[]{:S(2)}, u32[]{:S(2)}) collective-permute-start(bf16[168,384]{1,0:T(8,128)(2,1)S(1)} %get-tuple-element.53.after_ref), channel_id=1, source_target_pairs={{0,32},{1,33},{2,34},{3,35},{4,36},{5,37},{6,38},{7,39},{8,40},{9,... | collective-permute-start | bytes 387080 | tf_op jit(solution)/shard_map/ppermute | solution.py:84
  66.9 7.1 %collective-permute-start.15 = (bf16[168,384]{1,0:T(8,128)(2,1)S(1)}, bf16[168,384]{1,0:T(8,128)(2,1)S(1)}, u32[]{:S(2)}, u32[]{:S(2)}) collective-permute-start(bf16[168,384]{1,0:T(8,128)(2,1)S(1)} %get-tuple-element.52), channel_id=1, source_target_pairs={{0,32},{1,33},{2,34},{3,35},{4,36},{5,37},{6,38},{7,39},{8,40},{9,... | collective-permute-start | bytes 387080 | tf_op jit(solution)/shard_map/ppermute | solution.py:84
  71.3 11.5 %collective-permute-start.17 = (bf16[168,384]{1,0:T(8,128)(2,1)S(1)}, bf16[168,384]{1,0:T(8,128)(2,1)S(1)}, u32[]{:S(2)}, u32[]{:S(2)}) collective-permute-start(bf16[168,384]{1,0:T(8,128)(2,1)S(1)} %shard_map.88.after_ref), channel_id=1, source_target_pairs={{0,96},{1,97},{2,98},{3,99},{4,100},{5,101},{6,102},{7,103},{8,104... | collective-permute-start | bytes 387080 | tf_op jit(solution)/shard_map/ppermute | solution.py:84
  74.0 11.5 %collective-permute-start.19 = (bf16[168,384]{1,0:T(8,128)(2,1)S(1)}, bf16[168,384]{1,0:T(8,128)(2,1)S(1)}, u32[]{:S(2)}, u32[]{:S(2)}) collective-permute-start(bf16[168,384]{1,0:T(8,128)(2,1)S(1)} %shard_map.89.after_ref._), channel_id=1, source_target_pairs={{0,96},{1,97},{2,98},{3,99},{4,100},{5,101},{6,102},{7,103},{8,104... | collective-permute-start | bytes 387080 | tf_op jit(solution)/shard_map/ppermute | solution.py:84
  83.4 5.3 %collective-permute-start.20 = (f32[168,384]{1,0:T(8,128)S(1)}, f32[168,384]{1,0:T(8,128)S(1)}, u32[]{:S(2)}, u32[]{:S(2)}) collective-permute-start(f32[168,384]{1,0:T(8,128)S(1)} %shard_map.91._), channel_id=1, source_target_pairs={{0,16},{1,17},{2,18},{3,19},{4,20},{5,21},{6,22},{7,23},{8,24},{9,... | collective-permute-start | bytes 774152 | tf_op jit(solution)/shard_map/ppermute | solution.py:84
  86.2 2.5 %collective-permute-start.21 = (f32[168,384]{1,0:T(8,128)S(1)}, f32[168,384]{1,0:T(8,128)S(1)}, u32[]{:S(2)}, u32[]{:S(2)}) collective-permute-start(f32[168,384]{1,0:T(8,128)S(1)} %shard_map.92.refs_0_), channel_id=1, source_target_pairs={{0,16},{1,17},{2,18},{3,19},{4,20},{5,21},{6,22},{7,23},{8,24},{9,... | collective-permute-start | bytes 774152 | tf_op jit(solution)/shard_map/ppermute | solution.py:84
  (1 other events, 9.6 us)

commit v4 on v3

--- a/solution.py
+++ b/solution.py
@@ -89,15 +89,14 @@
     return shift_factor * fraction / (1.0 + (shift_factor - 1.0) * fraction)
 
 
-def frame_features(steps_row):
-    level_float = steps_row.astype(F32)
-    upper = noise_level(level_float + 1.0)
-    lower = noise_level(level_float)
-    half_freq = 128
-    rates = jnp.exp(-math.log(10000.0) * jnp.arange(half_freq, dtype=F32) / half_freq)
-    angles = (1000.0 * upper)[:, None] * rates[None, :]
-    features = jnp.concatenate([jnp.cos(angles), jnp.sin(angles)], axis=1).astype(BF16)
-    return features, upper - lower
+def frame_features(steps_ref, rates_ref, feat_ref, gap_ref):
+    level_row = steps_ref[...].astype(F32)
+    gap_ref[...] = jnp.zeros((1, 128), F32)
+    gap_ref[:, :NF] = noise_level(level_row + 1.0) - noise_level(level_row)
+    level = jnp.broadcast_to(level_row, (128, NF)).T
+    angles = (1000.0 * noise_level(level + 1.0)) * rates_ref[...]
+    feat_ref[:, :128] = jnp.cos(angles).astype(BF16)
+    feat_ref[:, 128:] = jnp.sin(angles).astype(BF16)
 
 
 def split3(value):
@@ -120,8 +119,24 @@
 
 
 def norm_kernel(
-    latent_hbm, frame_hbm, feat_ref, mod_hbm, out_ref, lat_ref, frame_ref, mod_ref, picked_ref, unit_ref, sems
+    latent_hbm,
+    frame_hbm,
+    steps_hbm,
+    rates_ref,
+    mod_hbm,
+    out_ref,
+    lat_ref,
+    frame_ref,
+    feat_ref,
+    gap_ref,
+    mod_ref,
+    picked_ref,
+    unit_ref,
+    steps_ref,
+    sems,
 ):
+    steps = pltpu.make_async_copy(steps_hbm, steps_ref, sems.at[7])
+    steps.start()
     copies = [pltpu.make_async_copy(frame_hbm, frame_ref, sems.at[0])]
     for i in range(2):
         rows = pl.ds(i * (ROWS // 2 + 4), (88, 80)[i])
@@ -138,6 +153,9 @@
     out_ref[ROWS:, :] = jnp.zeros((PACK - ROWS, D), BF16)
     out_ref[ROWS:, :ROWS] = jnp.broadcast_to(frame_ref[...], (8, ROWS)).astype(F32).astype(BF16)
 
+    steps.wait()
+    frame_features(steps_ref, rates_ref, feat_ref, gap_ref)
+
     def normal(i, carry):
         rows = pl.ds(pl.multiple_of(i * 8, 8), 8)
         latent = lat_ref[rows, :]
@@ -163,18 +181,25 @@
             out_ref[:ROWS, cols] = out.astype(BF16)
 
 
-def normed_pack(latent, frame_row, features, mod_weight):
+def normed_pack(latent, frame_row, steps_row, rates, mod_weight):
     return call(
         norm_kernel,
-        (latent, frame_row, features, mod_weight),
-        [HBM, HBM, VM, HBM],
-        [shaped(PACK, D, kind=BF16), shaped(ROWS, D), shaped(1, ROWS, kind=jnp.int32)],
+        (latent, frame_row, steps_row, rates, mod_weight),
+        [HBM, HBM, HBM, VM, HBM],
+        [
+            shaped(PACK, D, kind=BF16),
+            shaped(ROWS, D),
+            shaped(1, ROWS, kind=jnp.int32),
+            shaped(NF, 256, kind=BF16),
+            shaped(1, 128),
+        ],
         (30000000, 4000000, 0),
         [
             pltpu.VMEM((256, 2 * D), BF16),
             pltpu.VMEM((ROWS, D), F32),
             pltpu.VMEM((ROWS, D), F32),
-            pltpu.SemaphoreType.DMA((7,)),
+            pltpu.VMEM((1, NF), jnp.int32),
+            pltpu.SemaphoreType.DMA((8,)),
         ],
     )
 
@@ -552,12 +577,13 @@
     place = jnp.where(core == 0, ctx // 4, ctx % 4)
     where = jnp.stack([place, core, chip]).astype(jnp.int32)
     latent = held(iterate[0])
-    features, gap = frame_features(noise_steps[0])
-    gap = jnp.pad(gap, (0, 128 - NF))[None, :]
+    rates = jnp.exp(-math.log(10000.0) * jnp.arange(128, dtype=F32) / 128)[None, :]
     frame_row = held(frame_index[None, :])
 
     tie = lax.optimization_barrier
-    mine, latent, frame_row = normed_pack(latent, frame_row, features, mod_weight)
+    mine, latent, frame_row, features, gap = normed_pack(
+        latent, frame_row, held(noise_steps), rates, mod_weight
+    )
     from_prev = send(mine, along("a", 1))
     from_next = send(mine, along("a", -1))
     from_far = send(mine, along("a", 2))

time: 91.6 us -> 90.8 us (level)
  transfers between devices with their start and end apart: 22 -> 22, of which waited for: 10 -> 10; matrix products, arithmetic and copies ran while one was open for 0% -> 0% of each run, Pallas kernels for 22% -> 23%
where the time goes in v4:
time: 90.8 us; the launch traced here: 89.5 us
  starting transfers between devices  31.6 us (35%)
  waiting for transfers between devices  29.8 us (33%)
  Pallas kernels  27.6 us (30%)
    ppermute x22, starting transfers between devices, send(): return lax.ppermute(value, AXES, route)  31.6 us
    ppermute x22, waiting for transfers between devices, send(): return lax.ppermute(value, AXES, route)  29.8 us
    pallas_call x20, Pallas kernels, run_kernel(): pl.pallas_call(kernel, in_specs=specs, out_specs=[VM] * len(outs) if out_...  24.8 us
    pallas_call x2, Pallas kernels, final_sum(): pl.pallas_call(functools.partial(final_kernel, own), in_specs=[SM, HBM if...  2.82 us
  transfers between devices with their start and end apart: 22, of which 10 were waited for; matrix products, arithmetic and copies ran while one was open for 0% of the time, Pallas kernels for 23%

profile of v4, /device:TPU:15, one launch (start us, length us, event | category | flops | bytes accessed | tf_op | source)
XLA Modules:
  0.0 89.5 jit_solution(5794000244654159929)
XLA Ops:
  0.0 3.1 %shard_map.73 = (bf16[176,1536]{1,0:T(8,128)(2,1)S(1)}, f32[168,1536]{1,0:T(8,128)S(1)}, s32[1,168]{1,0:T(1,128)S(1)}, bf16[16,256]{1,0:T(8,128)(2,1)S(1)}, f32[1,128]{1,0:T(1,128)S(1)}) custom-call(f32[168,1536]{1,0:T(8,128)} %bitcast.8, s32[1,168]{1,0:T(1,128)} %bitcast.9, s32[1,16]{1,0:T(1,128)} %steps_hbm.1, ...), custom_call_target="tpu_custom_call" | custom-call | flops 30000000 | bytes 4000000 | tf_op jit(solution)/shard_map/pallas_call | solution.py:47
  3.2 1.7 %collective-permute-start.2 = (bf16[176,1536]{1,0:T(8,128)(2,1)S(1)}, bf16[176,1536]{1,0:T(8,128)(2,1)S(1)}, u32[]{:S(2)}, u32[]{:S(2)}) collective-permute-start(bf16[176,1536]{1,0:T(8,128)(2,1)S(1)} %get-tuple-element.40.refs_1_), channel_id=1, source_target_pairs={{0,4},{1,5},{2,6},{3,7},{4,8},{5,9},{6,10},{7,11},{8,12},{9,13},{1... | collective-permute-start | bytes 1622024 | tf_op jit(solution)/shard_map/ppermute | solution.py:84
  6.4 3.8 %collective-permute-start.3 = (bf16[176,1536]{1,0:T(8,128)(2,1)S(1)}, bf16[176,1536]{1,0:T(8,128)(2,1)S(1)}, u32[]{:S(2)}, u32[]{:S(2)}) collective-permute-start(bf16[176,1536]{1,0:T(8,128)(2,1)S(1)} %get-tuple-element.40.refs_1_), channel_id=1, source_target_pairs={{0,12},{1,13},{2,14},{3,15},{4,0},{5,1},{6,2},{7,3},{8,4},{9,5},{1... | collective-permute-start | bytes 1622024 | tf_op jit(solution)/shard_map/ppermute | solution.py:84
  10.2 2.8 %shard_map.75 = (f32[168,1536]{1,0:T(8,128)S(1)}, bf16[1536,1152]{1,0:T(8,128)(2,1)S(1)}) custom-call(s32[3]{0:T(128)S(1)} %pad_add_fusion.where_ref.refs_0_, f32[168,768]{1,0:T(8,128)S(1)} %get-tuple-element.37.after_ref.give_ref, s32[1,168]{1,0:T(1,128)S(1)} %get-tuple-element.34.frame_ref, f32[1,128]{1,0:T(1,128)S(1)} %get-tuple-element.35.gap_ref, ...), custom_call_target="tpu_custom_call" | custom-call | flops 30000000 | bytes 6000000 | tf_op jit(solution)/shard_map/pallas_call | solution.py:47
  13.7 1.8 %shard_map.77 = (bf16[336,384]{1,0:T(8,128)(2,1)S(1)}, bf16[344,768]{1,0:T(8,128)(2,1)S(1)}) custom-call(f32[168,768]{1,0:T(8,128)S(1)} %shard_map.76.refs_0_.a_ref, bf16[176,1536]{1,0:T(8,128)(2,1)S(1)} %get-tuple-element.40.refs_1_, bf16[176,1536]{1,0:T(8,128)(2,1)S(1)} %collective-permute-done.2.refs_2_, ...), custom_call_target="tpu_custom_call" | custom-call | flops 1189085184 | bytes 5000000 | tf_op jit(solution)/shard_map/pallas_call | solution.py:47
  15.5 1.5 %collective-permute-start.5 = (bf16[344,768]{1,0:T(8,128)(2,1)S(1)}, bf16[344,768]{1,0:T(8,128)(2,1)S(1)}, u32[]{:S(2)}, u32[]{:S(2)}) collective-permute-start(bf16[344,768]{1,0:T(8,128)(2,1)S(1)} %get-tuple-element.42.refs_0_.refs_2_), channel_id=1, source_target_pairs={{0,1},{1,2},{2,3},{3,0},{4,5},{5,6},{6,7},{7,4},{8,9},{9,10},{10,1... | collective-permute-start | bytes 1585160 | tf_op jit(solution)/shard_map/ppermute | solution.py:84
  17.1 7.2 %collective-permute-done.3.refs_1_ = bf16[176,1536]{1,0:T(8,128)(2,1)S(1)} collective-permute-done((bf16[176,1536]{1,0:T(8,128)(2,1)S(1)}, bf16[176,1536]{1,0:T(8,128)(2,1)S(1)}, u32[]{:S(2)}, u32[]{:S(2)}) %collective-permute-start.3) | collective-permute-done | bytes 540704 | tf_op jit(solution)/shard_map/ppermute | solution.py:84
  24.2 1.8 %shard_map.78 = (bf16[336,384]{1,0:T(8,128)(2,1)S(1)}, bf16[344,768]{1,0:T(8,128)(2,1)S(1)}) custom-call(bf16[344,768]{1,0:T(8,128)(2,1)S(1)} %get-tuple-element.42.refs_0_.refs_2_, bf16[176,1536]{1,0:T(8,128)(2,1)S(1)} %collective-permute-done.3.refs_1_, bf16[176,1536]{1,0:T(8,128)(2,1)S(1)} %collective-permute-done.4.refs_2_, ...), custom_call_target="tpu_custom_call" | custom-call | flops 1189085184 | bytes 5000000 | tf_op jit(solution)/shard_map/pallas_call | solution.py:47
  26.1 1.5 %collective-permute-start.7 = (bf16[344,768]{1,0:T(8,128)(2,1)S(1)}, bf16[344,768]{1,0:T(8,128)(2,1)S(1)}, u32[]{:S(2)}, u32[]{:S(2)}) collective-permute-start(bf16[344,768]{1,0:T(8,128)(2,1)S(1)} %get-tuple-element.44.refs_3_), channel_id=1, source_target_pairs={{0,1},{1,2},{2,3},{3,0},{4,5},{5,6},{6,7},{7,4},{8,9},{9,10},{10,1... | collective-permute-start | bytes 1585160 | tf_op jit(solution)/shard_map/ppermute | solution.py:84
  27.6 3.9 %shard_map.79 = (f32[672,384]{1,0:T(8,128)S(1)}, f32[672,384]{1,0:T(8,128)S(1)}, bf16[672,768]{1,0:T(8,128)(2,1)S(1)}) custom-call(bf16[336,384]{1,0:T(8,128)(2,1)S(1)} %get-tuple-element.41.refs_0_, bf16[336,384]{1,0:T(8,128)(2,1)S(1)} %get-tuple-element.43.refs_1_, bf16[344,768]{1,0:T(8,128)(2,1)S(1)} %get-tuple-element.42.refs_0_.refs_2_, ...), custom_call_target="tpu_custom_call" | custom-call | flops 2774532096 | bytes 2000000 | tf_op jit(solution)/shard_map/pallas_call | solution.py:47
  31.5 3.0 %collective-permute-done.8.refs_4_ = bf16[344,768]{1,0:T(8,128)(2,1)S(1)} collective-permute-done((bf16[344,768]{1,0:T(8,128)(2,1)S(1)}, bf16[344,768]{1,0:T(8,128)(2,1)S(1)}, u32[]{:S(2)}, u32[]{:S(2)}) %collective-permute-start.8) | collective-permute-done | bytes 528416 | tf_op jit(solution)/shard_map/ppermute | solution.py:84
  34.5 1.5 %collective-permute-start.10 = (bf16[344,768]{1,0:T(8,128)(2,1)S(1)}, bf16[344,768]{1,0:T(8,128)(2,1)S(1)}, u32[]{:S(2)}, u32[]{:S(2)}) collective-permute-start(bf16[344,768]{1,0:T(8,128)(2,1)S(1)} %collective-permute-done.8.refs_4_), channel_id=1, source_target_pairs={{0,3},{1,0},{2,1},{3,2},{4,7},{5,4},{6,5},{7,6},{8,11},{9,8},{10,9... | collective-permute-start | bytes 1585160 | tf_op jit(solution)/shard_map/ppermute | solution.py:84
  36.5 2.1 %shard_map.80 = (f32[672,384]{1,0:T(8,128)S(1)}, f32[672,384]{1,0:T(8,128)S(1)}) custom-call(bf16[672,768]{1,0:T(8,128)(2,1)S(1)} %get-tuple-element.45.refs_0_.refs_1_, f32[672,384]{1,0:T(8,128)S(1)} %get-tuple-element.46.refs_1_, f32[672,384]{1,0:T(8,128)S(1)} %get-tuple-element.47.refs_2_, bf16[344,768]{1,0:T(8,128)(2,1)S(1)} %collective-permute-done.7.refs_3_, ...), custom_call_target="tpu_custom_call" | custom-call | flops 1387266048 | bytes 2000000 | tf_op jit(solution)/shard_map/pallas_call | solution.py:47
  38.6 5.6 %collective-permute-done.1.b_ref.got_ref = f32[168,768]{1,0:T(8,128)S(1)} collective-permute-done((f32[168,768]{1,0:T(8,128)S(1)}, f32[168,768]{1,0:T(8,128)S(1)}, u32[]{:S(2)}, u32[]{:S(2)}) %collective-permute-start.1) | collective-permute-done | bytes 516128 | tf_op jit(solution)/shard_map/ppermute | solution.py:84
  44.3 1.7 %shard_map.82 = (bf16[168,384]{1,0:T(8,128)(2,1)S(1)}, bf16[168,384]{1,0:T(8,128)(2,1)S(1)}, bf16[168,384]{1,0:T(8,128)(2,1)S(1)}) custom-call(f32[168,768]{1,0:T(8,128)S(1)} %shard_map.81.refs_0_, bf16[672,768]{1,0:T(8,128)(2,1)S(1)} %get-tuple-element.45.refs_0_.refs_1_, f32[672,384]{1,0:T(8,128)S(1)} %get-tuple-element.48.after_ref.refs_2_, ...), custom_call_target="tpu_custom_call" | custom-call | flops 1040449536 | bytes 2000000 | tf_op jit(solution)/shard_map/pallas_call | solution.py:47
  46.0 3.8 %collective-permute-start.11 = (bf16[168,384]{1,0:T(8,128)(2,1)S(1)}, bf16[168,384]{1,0:T(8,128)(2,1)S(1)}, u32[]{:S(2)}, u32[]{:S(2)}) collective-permute-start(bf16[168,384]{1,0:T(8,128)(2,1)S(1)} %get-tuple-element.51.refs_0_), channel_id=1, source_target_pairs={{0,12},{1,13},{2,14},{3,15},{4,0},{5,1},{6,2},{7,3},{8,4},{9,5},{1... | collective-permute-start | bytes 387080 | tf_op jit(solution)/shard_map/ppermute | solution.py:84
  49.8 2.9 %collective-permute-start.13 = (bf16[168,384]{1,0:T(8,128)(2,1)S(1)}, bf16[168,384]{1,0:T(8,128)(2,1)S(1)}, u32[]{:S(2)}, u32[]{:S(2)}) collective-permute-start(bf16[168,384]{1,0:T(8,128)(2,1)S(1)} %get-tuple-element.53), channel_id=1, source_target_pairs={{0,8},{1,9},{2,10},{3,11},{4,12},{5,13},{6,14},{7,15},{8,0},{9,1},... | collective-permute-start | bytes 387080 | tf_op jit(solution)/shard_map/ppermute | solution.py:84
  54.9 1.6 %collective-permute-done.13.a3 = bf16[168,384]{1,0:T(8,128)(2,1)S(1)} collective-permute-done((bf16[168,384]{1,0:T(8,128)(2,1)S(1)}, bf16[168,384]{1,0:T(8,128)(2,1)S(1)}, u32[]{:S(2)}, u32[]{:S(2)}) %collective-permute-start.13) | collective-permute-done | bytes 129056 | tf_op jit(solution)/shard_map/ppermute | solution.py:84
  57.6 5.4 %collective-permute-start.14 = (f32[168,768]{1,0:T(8,128)S(1)}, f32[168,768]{1,0:T(8,128)S(1)}, u32[]{:S(2)}, u32[]{:S(2)}) collective-permute-start(f32[168,768]{1,0:T(8,128)S(1)} %shard_map.85.after_ref.refs_2_), channel_id=1, source_target_pairs={{0,16},{1,17},{2,18},{3,19},{4,20},{5,21},{6,22},{7,23},{8,24},{9,... | collective-permute-start | bytes 1548296 | tf_op jit(solution)/shard_map/ppermute | solution.py:84
  67.1 3.4 %collective-permute-done.16.got_ref.refs_2_.refs_4_ = bf16[168,384]{1,0:T(8,128)(2,1)S(1)} collective-permute-done((bf16[168,384]{1,0:T(8,128)(2,1)S(1)}, bf16[168,384]{1,0:T(8,128)(2,1)S(1)}, u32[]{:S(2)}, u32[]{:S(2)}) %collective-permute-start.16) | collective-permute-done | bytes 129056 | tf_op jit(solution)/shard_map/ppermute | solution.py:84
  71.8 1.4 %collective-permute-done.15.got_ref.refs_2_.refs_5_ = bf16[168,384]{1,0:T(8,128)(2,1)S(1)} collective-permute-done((bf16[168,384]{1,0:T(8,128)(2,1)S(1)}, bf16[168,384]{1,0:T(8,128)(2,1)S(1)}, u32[]{:S(2)}, u32[]{:S(2)}) %collective-permute-start.15) | collective-permute-done | bytes 129056 | tf_op jit(solution)/shard_map/ppermute | solution.py:84
  74.5 4.7 %collective-permute-done.18.far_ref = f32[168,768]{1,0:T(8,128)S(1)} collective-permute-done((f32[168,768]{1,0:T(8,128)S(1)}, f32[168,768]{1,0:T(8,128)S(1)}, u32[]{:S(2)}, u32[]{:S(2)}) %collective-permute-start.18) | collective-permute-done | bytes 516128 | tf_op jit(solution)/shard_map/ppermute | solution.py:84
  80.1 1.9 %collective-permute-done.17.refs_3_.refs_6_ = bf16[168,384]{1,0:T(8,128)(2,1)S(1)} collective-permute-done((bf16[168,384]{1,0:T(8,128)(2,1)S(1)}, bf16[168,384]{1,0:T(8,128)(2,1)S(1)}, u32[]{:S(2)}, u32[]{:S(2)}) %collective-permute-start.17) | collective-permute-done | bytes 129056 | tf_op jit(solution)/shard_map/ppermute | solution.py:84
  82.6 1.7 %collective-permute-start.20 = (f32[168,384]{1,0:T(8,128)S(1)}, f32[168,384]{1,0:T(8,128)S(1)}, u32[]{:S(2)}, u32[]{:S(2)}) collective-permute-start(f32[168,384]{1,0:T(8,128)S(1)} %shard_map.91._), channel_id=1, source_target_pairs={{0,16},{1,17},{2,18},{3,19},{4,20},{5,21},{6,22},{7,23},{8,24},{9,... | collective-permute-start | bytes 774152 | tf_op jit(solution)/shard_map/ppermute | solution.py:84
  (51 shorter events, 19.4 us)
Async XLA Ops:
  3.2 10.6 %collective-permute-start.2 = (bf16[176,1536]{1,0:T(8,128)(2,1)S(1)}, bf16[176,1536]{1,0:T(8,128)(2,1)S(1)}, u32[]{:S(2)}, u32[]{:S(2)}) collective-permute-start(bf16[176,1536]{1,0:T(8,128)(2,1)S(1)} %get-tuple-element.40.refs_1_), channel_id=1, source_target_pairs={{0,4},{1,5},{2,6},{3,7},{4,8},{5,9},{6,10},{7,11},{8,12},{9,13},{1... | collective-permute-start | bytes 1622024 | tf_op jit(solution)/shard_map/ppermute | solution.py:84
  5.7 7.3 %collective-permute-start = (f32[168,768]{1,0:T(8,128)S(1)}, f32[168,768]{1,0:T(8,128)S(1)}, u32[]{:S(2)}, u32[]{:S(2)}) collective-permute-start(f32[168,768]{1,0:T(8,128)S(1)} %get-tuple-element.37.after_ref.give_ref), channel_id=1, source_target_pairs={{0,16},{1,17},{2,18},{3,19},{4,20},{5,21},{6,22},{7,23},{8,24},{9,... | collective-permute-start | bytes 1548296 | tf_op jit(solution)/shard_map/ppermute | solution.py:84
  6.4 17.8 %collective-permute-start.3 = (bf16[176,1536]{1,0:T(8,128)(2,1)S(1)}, bf16[176,1536]{1,0:T(8,128)(2,1)S(1)}, u32[]{:S(2)}, u32[]{:S(2)}) collective-permute-start(bf16[176,1536]{1,0:T(8,128)(2,1)S(1)} %get-tuple-element.40.refs_1_), channel_id=1, source_target_pairs={{0,12},{1,13},{2,14},{3,15},{4,0},{5,1},{6,2},{7,3},{8,4},{9,5},{1... | collective-permute-start | bytes 1622024 | tf_op jit(solution)/shard_map/ppermute | solution.py:84
  10.2 14.1 %collective-permute-start.4 = (bf16[176,1536]{1,0:T(8,128)(2,1)S(1)}, bf16[176,1536]{1,0:T(8,128)(2,1)S(1)}, u32[]{:S(2)}, u32[]{:S(2)}) collective-permute-start(bf16[176,1536]{1,0:T(8,128)(2,1)S(1)} %get-tuple-element.40.refs_1_), channel_id=1, source_target_pairs={{0,8},{1,9},{2,10},{3,11},{4,12},{5,13},{6,14},{7,15},{8,0},{9,1},... | collective-permute-start | bytes 1622024 | tf_op jit(solution)/shard_map/ppermute | solution.py:84
  15.5 12.0 %collective-permute-start.5 = (bf16[344,768]{1,0:T(8,128)(2,1)S(1)}, bf16[344,768]{1,0:T(8,128)(2,1)S(1)}, u32[]{:S(2)}, u32[]{:S(2)}) collective-permute-start(bf16[344,768]{1,0:T(8,128)(2,1)S(1)} %get-tuple-element.42.refs_0_.refs_2_), channel_id=1, source_target_pairs={{0,1},{1,2},{2,3},{3,0},{4,5},{5,6},{6,7},{7,4},{8,9},{9,10},{10,1... | collective-permute-start | bytes 1585160 | tf_op jit(solution)/shard_map/ppermute | solution.py:84
  17.0 10.5 %collective-permute-start.6 = (bf16[344,768]{1,0:T(8,128)(2,1)S(1)}, bf16[344,768]{1,0:T(8,128)(2,1)S(1)}, u32[]{:S(2)}, u32[]{:S(2)}) collective-permute-start(bf16[344,768]{1,0:T(8,128)(2,1)S(1)} %get-tuple-element.42.refs_0_.refs_2_), channel_id=1, source_target_pairs={{0,3},{1,0},{2,1},{3,2},{4,7},{5,4},{6,5},{7,6},{8,11},{9,8},{10,9... | collective-permute-start | bytes 1585160 | tf_op jit(solution)/shard_map/ppermute | solution.py:84
  26.0 8.4 %collective-permute-start.8 = (bf16[344,768]{1,0:T(8,128)(2,1)S(1)}, bf16[344,768]{1,0:T(8,128)(2,1)S(1)}, u32[]{:S(2)}, u32[]{:S(2)}) collective-permute-start(bf16[344,768]{1,0:T(8,128)(2,1)S(1)} %get-tuple-element.44.refs_3_), channel_id=1, source_target_pairs={{0,3},{1,0},{2,1},{3,2},{4,7},{5,4},{6,5},{7,6},{8,11},{9,8},{10,9... | collective-permute-start | bytes 1585160 | tf_op jit(solution)/shard_map/ppermute | solution.py:84
  26.1 10.4 %collective-permute-start.7 = (bf16[344,768]{1,0:T(8,128)(2,1)S(1)}, bf16[344,768]{1,0:T(8,128)(2,1)S(1)}, u32[]{:S(2)}, u32[]{:S(2)}) collective-permute-start(bf16[344,768]{1,0:T(8,128)(2,1)S(1)} %get-tuple-element.44.refs_3_), channel_id=1, source_target_pairs={{0,1},{1,2},{2,3},{3,0},{4,5},{5,6},{6,7},{7,4},{8,9},{9,10},{10,1... | collective-permute-start | bytes 1585160 | tf_op jit(solution)/shard_map/ppermute | solution.py:84
  34.5 9.8 %collective-permute-start.9 = (bf16[344,768]{1,0:T(8,128)(2,1)S(1)}, bf16[344,768]{1,0:T(8,128)(2,1)S(1)}, u32[]{:S(2)}, u32[]{:S(2)}) collective-permute-start(bf16[344,768]{1,0:T(8,128)(2,1)S(1)} %collective-permute-done.5.refs_4_), channel_id=1, source_target_pairs={{0,1},{1,2},{2,3},{3,0},{4,5},{5,6},{6,7},{7,4},{8,9},{9,10},{10,1... | collective-permute-start | bytes 1585160 | tf_op jit(solution)/shard_map/ppermute | solution.py:84
  34.5 9.8 %collective-permute-start.10 = (bf16[344,768]{1,0:T(8,128)(2,1)S(1)}, bf16[344,768]{1,0:T(8,128)(2,1)S(1)}, u32[]{:S(2)}, u32[]{:S(2)}) collective-permute-start(bf16[344,768]{1,0:T(8,128)(2,1)S(1)} %collective-permute-done.8.refs_4_), channel_id=1, source_target_pairs={{0,3},{1,0},{2,1},{3,2},{4,7},{5,4},{6,5},{7,6},{8,11},{9,8},{10,9... | collective-permute-start | bytes 1585160 | tf_op jit(solution)/shard_map/ppermute | solution.py:84
  35.9 8.2 %collective-permute-start.1 = (f32[168,768]{1,0:T(8,128)S(1)}, f32[168,768]{1,0:T(8,128)S(1)}, u32[]{:S(2)}, u32[]{:S(2)}) collective-permute-start(f32[168,768]{1,0:T(8,128)S(1)} %shard_map.76.refs_0_.a_ref), channel_id=1, source_target_pairs={{0,32},{1,33},{2,34},{3,35},{4,36},{5,37},{6,38},{7,39},{8,40},{9,... | collective-permute-start | bytes 1548296 | tf_op jit(solution)/shard_map/ppermute | solution.py:84
  44.2 9.6 %slice-start = ((s8[4718592]{0:T(1024)(128)(4,1)}), s8[4194304]{0:T(1024)(128)(4,1)S(1)}, s32[]{:S(2)}) async-start(s8[4718592]{0:T(1024)(128)(4,1)} %bitcast.6), calls=%async_computation | async-start | bytes 8388608
  46.0 8.9 %collective-permute-start.11 = (bf16[168,384]{1,0:T(8,128)(2,1)S(1)}, bf16[168,384]{1,0:T(8,128)(2,1)S(1)}, u32[]{:S(2)}, u32[]{:S(2)}) collective-permute-start(bf16[168,384]{1,0:T(8,128)(2,1)S(1)} %get-tuple-element.51.refs_0_), channel_id=1, source_target_pairs={{0,12},{1,13},{2,14},{3,15},{4,0},{5,1},{6,2},{7,3},{8,4},{9,5},{1... | collective-permute-start | bytes 387080 | tf_op jit(solution)/shard_map/ppermute | solution.py:84
  49.8 5.1 %collective-permute-start.12 = (bf16[168,384]{1,0:T(8,128)(2,1)S(1)}, bf16[168,384]{1,0:T(8,128)(2,1)S(1)}, u32[]{:S(2)}, u32[]{:S(2)}) collective-permute-start(bf16[168,384]{1,0:T(8,128)(2,1)S(1)} %get-tuple-element.52), channel_id=1, source_target_pairs={{0,4},{1,5},{2,6},{3,7},{4,8},{5,9},{6,10},{7,11},{8,12},{9,13},{1... | collective-permute-start | bytes 387080 | tf_op jit(solution)/shard_map/ppermute | solution.py:84
  49.8 6.6 %collective-permute-start.13 = (bf16[168,384]{1,0:T(8,128)(2,1)S(1)}, bf16[168,384]{1,0:T(8,128)(2,1)S(1)}, u32[]{:S(2)}, u32[]{:S(2)}) collective-permute-start(bf16[168,384]{1,0:T(8,128)(2,1)S(1)} %get-tuple-element.53), channel_id=1, source_target_pairs={{0,8},{1,9},{2,10},{3,11},{4,12},{5,13},{6,14},{7,15},{8,0},{9,1},... | collective-permute-start | bytes 387080 | tf_op jit(solution)/shard_map/ppermute | solution.py:84
  57.6 21.6 %copy-start = (f32[168,1536]{1,0:T(8,128)S(1)}, f32[168,1536]{1,0:T(8,128)}, u32[]{:S(2)}) copy-start(f32[168,1536]{1,0:T(8,128)} %anchor_ref.1) | copy-start | bytes 3096580
  57.6 7.8 %collective-permute-start.14 = (f32[168,768]{1,0:T(8,128)S(1)}, f32[168,768]{1,0:T(8,128)S(1)}, u32[]{:S(2)}, u32[]{:S(2)}) collective-permute-start(f32[168,768]{1,0:T(8,128)S(1)} %shard_map.85.after_ref.refs_2_), channel_id=1, source_target_pairs={{0,16},{1,17},{2,18},{3,19},{4,20},{5,21},{6,22},{7,23},{8,24},{9,... | collective-permute-start | bytes 1548296 | tf_op jit(solution)/shard_map/ppermute | solution.py:84
  63.0 16.2 %collective-permute-start.18 = (f32[168,768]{1,0:T(8,128)S(1)}, f32[168,768]{1,0:T(8,128)S(1)}, u32[]{:S(2)}, u32[]{:S(2)}) collective-permute-start(f32[168,768]{1,0:T(8,128)S(1)} %shard_map.81.refs_0_), channel_id=1, source_target_pairs={{0,96},{1,97},{2,98},{3,99},{4,100},{5,101},{6,102},{7,103},{8,104... | collective-permute-start | bytes 1548296 | tf_op jit(solution)/shard_map/ppermute | solution.py:84
  65.5 4.9 %collective-permute-start.16 = (bf16[168,384]{1,0:T(8,128)(2,1)S(1)}, bf16[168,384]{1,0:T(8,128)(2,1)S(1)}, u32[]{:S(2)}, u32[]{:S(2)}) collective-permute-start(bf16[168,384]{1,0:T(8,128)(2,1)S(1)} %get-tuple-element.57.after_ref), channel_id=1, source_target_pairs={{0,32},{1,33},{2,34},{3,35},{4,36},{5,37},{6,38},{7,39},{8,40},{9,... | collective-permute-start | bytes 387080 | tf_op jit(solution)/shard_map/ppermute | solution.py:84
  66.1 7.1 %collective-permute-start.15 = (bf16[168,384]{1,0:T(8,128)(2,1)S(1)}, bf16[168,384]{1,0:T(8,128)(2,1)S(1)}, u32[]{:S(2)}, u32[]{:S(2)}) collective-permute-start(bf16[168,384]{1,0:T(8,128)(2,1)S(1)} %get-tuple-element.56), channel_id=1, source_target_pairs={{0,32},{1,33},{2,34},{3,35},{4,36},{5,37},{6,38},{7,39},{8,40},{9,... | collective-permute-start | bytes 387080 | tf_op jit(solution)/shard_map/ppermute | solution.py:84
  70.5 11.5 %collective-permute-start.17 = (bf16[168,384]{1,0:T(8,128)(2,1)S(1)}, bf16[168,384]{1,0:T(8,128)(2,1)S(1)}, u32[]{:S(2)}, u32[]{:S(2)}) collective-permute-start(bf16[168,384]{1,0:T(8,128)(2,1)S(1)} %shard_map.88.after_ref), channel_id=1, source_target_pairs={{0,96},{1,97},{2,98},{3,99},{4,100},{5,101},{6,102},{7,103},{8,104... | collective-permute-start | bytes 387080 | tf_op jit(solution)/shard_map/ppermute | solution.py:84
  73.2 11.5 %collective-permute-start.19 = (bf16[168,384]{1,0:T(8,128)(2,1)S(1)}, bf16[168,384]{1,0:T(8,128)(2,1)S(1)}, u32[]{:S(2)}, u32[]{:S(2)}) collective-permute-start(bf16[168,384]{1,0:T(8,128)(2,1)S(1)} %shard_map.89.after_ref._), channel_id=1, source_target_pairs={{0,96},{1,97},{2,98},{3,99},{4,100},{5,101},{6,102},{7,103},{8,104... | collective-permute-start | bytes 387080 | tf_op jit(solution)/shard_map/ppermute | solution.py:84
  82.6 5.3 %collective-permute-start.20 = (f32[168,384]{1,0:T(8,128)S(1)}, f32[168,384]{1,0:T(8,128)S(1)}, u32[]{:S(2)}, u32[]{:S(2)}) collective-permute-start(f32[168,384]{1,0:T(8,128)S(1)} %shard_map.91._), channel_id=1, source_target_pairs={{0,16},{1,17},{2,18},{3,19},{4,20},{5,21},{6,22},{7,23},{8,24},{9,... | collective-permute-start | bytes 774152 | tf_op jit(solution)/shard_map/ppermute | solution.py:84
  85.4 2.5 %collective-permute-start.21 = (f32[168,384]{1,0:T(8,128)S(1)}, f32[168,384]{1,0:T(8,128)S(1)}, u32[]{:S(2)}, u32[]{:S(2)}) collective-permute-start(f32[168,384]{1,0:T(8,128)S(1)} %shard_map.92.refs_0_), channel_id=1, source_target_pairs={{0,16},{1,17},{2,18},{3,19},{4,20},{5,21},{6,22},{7,23},{8,24},{9,... | collective-permute-start | bytes 774152 | tf_op jit(solution)/shard_map/ppermute | solution.py:84
  (1 other events, 9.6 us)

commit v5 on v4

--- a/solution.py
+++ b/solution.py
@@ -76,6 +76,18 @@
         if (c == 0) == (ring == "a"):
             return (x, c, y + step, z)
         return (x, c, y, z + step)
+
+    return pairs(move)
+
+
+def exchange(ring, kind):
+    def partner(p):
+        return p ^ 1 if kind == 1 else 3 - p
+
+    def move(x, c, y, z):
+        if (c == 0) == (ring == "a"):
+            return (x, c, partner(y), z)
+        return (x, c, y, partner(z))
 
     return pairs(move)
 
@@ -401,12 +413,12 @@
     return (got[2] if first else state[0], got[0], got[1])
 
 
-def out_rows(where_ref, step):
-    return pl.ds(pl.multiple_of(lax.rem(where_ref[0] + step, 4) * WIDE, 128), WIDE)
+def out_rows(group):
+    return pl.ds(pl.multiple_of(group * WIDE, 128), WIDE)
 
 
 def out_first_kernel(where_ref, a_ref, w_ref, part_ref):
-    part_ref[...] = jnp.dot(a_ref[...], w_ref[out_rows(where_ref, 0), :], preferred_element_type=F32)
+    part_ref[...] = jnp.dot(a_ref[...], w_ref[out_rows(where_ref[0]), :], preferred_element_type=F32)
 
 
 def out_first(where, piece, out_weight):
@@ -424,8 +436,10 @@
     half = core if own else 1 - core
     cols = pl.ds(pl.multiple_of(half * HALF, 128), HALF)
     branch = part_ref[:, cols]
-    for piece, step in ((a1, 1), (a2, 3), (a3, 2)):
-        weight = w_ref[out_rows(where_ref, step), cols]
+    place = where_ref[0]
+    near = place + 1 - 2 * lax.rem(place, 2)
+    for piece, group in ((a1, near), (a2, 3 - place), (a3, lax.rem(place + 2, 4))):
+        weight = w_ref[out_rows(group), cols]
         branch = branch + jnp.dot(piece[...], weight, preferred_element_type=F32)
     term_ref[...] = gate_ref[:, cols] * branch
 
@@ -562,7 +576,7 @@
 
 SWAP = pairs(lambda x, c, y, z: (x, 1 - c, y, z))
 ROUND1 = pairs(lambda x, c, y, z: (x ^ 1, c, y, z))
-ROUND2 = pairs(lambda x, c, y, z: (3 - x, c, y, z) if x < 2 else None)
+ROUND2 = pairs(lambda x, c, y, z: (3 - x, c, y, z))
 
 
 def held(x):
@@ -584,8 +598,8 @@
     mine, latent, frame_row, features, gap = normed_pack(
         latent, frame_row, held(noise_steps), rates, mod_weight
     )
-    from_prev = send(mine, along("a", 1))
-    from_next = send(mine, along("a", -1))
+    from_prev = send(mine, exchange("a", 1))
+    from_next = send(mine, exchange("a", 2))
     from_far = send(mine, along("a", 2))
     lat_keep, lat_give = lat_terms(where, latent, frame_row, gap)
     lat_beside = send(lat_give, SWAP)
@@ -596,22 +610,22 @@
     lat_got = send(lat_both, ROUND1)
 
     q0, kv0 = project(mine, from_prev, weight, after=(lat_both,))
-    up0 = send(kv0, along("b", 1))
-    down0 = send(kv0, along("b", -1))
+    up0 = send(kv0, exchange("b", 1))
+    down0 = send(kv0, exchange("b", 2))
     q1, kv1 = project(from_next, from_far, weight, after=(kv0,))
-    down1 = send(kv1, along("b", -1))
-    up1 = send(kv1, along("b", 1))
-    far0 = send(up0, along("b", 1))
+    down1 = send(kv1, exchange("b", 2))
+    up1 = send(kv1, exchange("b", 1))
+    far0 = send(up0, exchange("b", 2))
     state = attend([kv0, kv1, up0, down0], queries=(q0, q1))
     down1_later, _ = tie((down1, state[1]))
-    far1 = send(down1_later, along("b", -1))
+    far1 = send(down1_later, exchange("b", 1))
     state = attend([up1, down1], state=state)
     (lat_wire,) = add_up(lat_both, lat_got, F32, state[1])
     a1, a2, a3 = attend([far0, far1], state=state, last=(ROWS, 3 * ROWS), after=(lat_wire,))
     lat_far = send(lat_wire, ROUND2)
-    b3 = send(a3, along("a", -2))
-    b1 = send(a1, along("a", -1))
-    b2 = send(a2, along("a", 1))
+    b3 = send(a3, along("a", 2))
+    b1 = send(a1, exchange("a", 1))
+    b2 = send(a2, exchange("a", 2))
     (a0,) = attend([far0, far1], state=state, last=(0, ROWS), after=(a1,))
     part = out_first(where, a0, out_weight)
     pieces = (b1, b2, b3)

time: 90.8 us -> 90 us (level)
  the two profiles are of different devices: /device:TPU:15 before, /device:TPU:1 now
where the time goes in v5:
time: 90 us; the launch traced here: 89.9 us
  starting transfers between devices  32.2 us (36%)
  waiting for transfers between devices  29.6 us (33%)
  Pallas kernels  27.6 us (31%)
    ppermute x22, starting transfers between devices, send(): return lax.ppermute(value, AXES, route)  32.2 us
    ppermute x22, waiting for transfers between devices, send(): return lax.ppermute(value, AXES, route)  29.6 us
    pallas_call x20, Pallas kernels, run_kernel(): pl.pallas_call(kernel, in_specs=specs, out_specs=[VM] * len(outs) if out_...  24.7 us
    pallas_call x2, Pallas kernels, final_sum(): pl.pallas_call(functools.partial(final_kernel, own), in_specs=[SM, HBM if...  2.82 us
  transfers between devices with their start and end apart: 22, of which 10 were waited for; matrix products, arithmetic and copies ran while one was open for 0% of the time, Pallas kernels for 22%

profile of v5, /device:TPU:1, one launch (start us, length us, event | category | flops | bytes accessed | tf_op | source)
XLA Modules:
  0.0 89.9 jit_solution(8504767234068449322)
XLA Ops:
  0.0 3.1 %shard_map.73 = (bf16[176,1536]{1,0:T(8,128)(2,1)S(1)}, f32[168,1536]{1,0:T(8,128)S(1)}, s32[1,168]{1,0:T(1,128)S(1)}, bf16[16,256]{1,0:T(8,128)(2,1)S(1)}, f32[1,128]{1,0:T(1,128)S(1)}) custom-call(f32[168,1536]{1,0:T(8,128)} %bitcast.8, s32[1,168]{1,0:T(1,128)} %bitcast.9, s32[1,16]{1,0:T(1,128)} %steps_hbm.1, ...), custom_call_target="tpu_custom_call" | custom-call | flops 30000000 | bytes 4000000 | tf_op jit(solution)/shard_map/pallas_call | solution.py:47
  3.2 2.5 %collective-permute-start.2 = (bf16[176,1536]{1,0:T(8,128)(2,1)S(1)}, bf16[176,1536]{1,0:T(8,128)(2,1)S(1)}, u32[]{:S(2)}, u32[]{:S(2)}) collective-permute-start(bf16[176,1536]{1,0:T(8,128)(2,1)S(1)} %get-tuple-element.40.refs_1_), channel_id=1, source_target_pairs={{0,4},{1,5},{2,6},{3,7},{4,0},{5,1},{6,2},{7,3},{8,12},{9,13},{10,... | collective-permute-start | bytes 1622024 | tf_op jit(solution)/shard_map/ppermute | solution.py:96
  7.2 3.8 %collective-permute-start.3 = (bf16[176,1536]{1,0:T(8,128)(2,1)S(1)}, bf16[176,1536]{1,0:T(8,128)(2,1)S(1)}, u32[]{:S(2)}, u32[]{:S(2)}) collective-permute-start(bf16[176,1536]{1,0:T(8,128)(2,1)S(1)} %get-tuple-element.40.refs_1_), channel_id=1, source_target_pairs={{0,12},{1,13},{2,14},{3,15},{4,8},{5,9},{6,10},{7,11},{8,4},{9,5},... | collective-permute-start | bytes 1622024 | tf_op jit(solution)/shard_map/ppermute | solution.py:96
  11.0 2.8 %shard_map.75 = (f32[168,1536]{1,0:T(8,128)S(1)}, bf16[1536,1152]{1,0:T(8,128)(2,1)S(1)}) custom-call(s32[3]{0:T(128)S(1)} %pad_add_fusion.where_ref.refs_0_, f32[168,768]{1,0:T(8,128)S(1)} %get-tuple-element.37.after_ref.give_ref, s32[1,168]{1,0:T(1,128)S(1)} %get-tuple-element.34.frame_ref, f32[1,128]{1,0:T(1,128)S(1)} %get-tuple-element.35.gap_ref, ...), custom_call_target="tpu_custom_call" | custom-call | flops 30000000 | bytes 6000000 | tf_op jit(solution)/shard_map/pallas_call | solution.py:47
  13.9 1.8 %shard_map.77 = (bf16[336,384]{1,0:T(8,128)(2,1)S(1)}, bf16[344,768]{1,0:T(8,128)(2,1)S(1)}) custom-call(f32[168,768]{1,0:T(8,128)S(1)} %shard_map.76.refs_0_.a_ref, bf16[176,1536]{1,0:T(8,128)(2,1)S(1)} %get-tuple-element.40.refs_1_, bf16[176,1536]{1,0:T(8,128)(2,1)S(1)} %collective-permute-done.2.refs_2_, ...), custom_call_target="tpu_custom_call" | custom-call | flops 1189085184 | bytes 5000000 | tf_op jit(solution)/shard_map/pallas_call | solution.py:47
  16.2 2.5 %collective-permute-start.6 = (bf16[344,768]{1,0:T(8,128)(2,1)S(1)}, bf16[344,768]{1,0:T(8,128)(2,1)S(1)}, u32[]{:S(2)}, u32[]{:S(2)}) collective-permute-start(bf16[344,768]{1,0:T(8,128)(2,1)S(1)} %get-tuple-element.42.refs_0_.refs_2_), channel_id=1, source_target_pairs={{0,3},{1,2},{2,1},{3,0},{4,7},{5,6},{6,5},{7,4},{8,11},{9,10},{10,... | collective-permute-start | bytes 1585160 | tf_op jit(solution)/shard_map/ppermute | solution.py:96
  18.7 6.7 %collective-permute-done.3.refs_1_ = bf16[176,1536]{1,0:T(8,128)(2,1)S(1)} collective-permute-done((bf16[176,1536]{1,0:T(8,128)(2,1)S(1)}, bf16[176,1536]{1,0:T(8,128)(2,1)S(1)}, u32[]{:S(2)}, u32[]{:S(2)}) %collective-permute-start.3) | collective-permute-done | bytes 540704 | tf_op jit(solution)/shard_map/ppermute | solution.py:96
  25.4 1.8 %shard_map.78 = (bf16[336,384]{1,0:T(8,128)(2,1)S(1)}, bf16[344,768]{1,0:T(8,128)(2,1)S(1)}) custom-call(bf16[344,768]{1,0:T(8,128)(2,1)S(1)} %get-tuple-element.42.refs_0_.refs_2_, bf16[176,1536]{1,0:T(8,128)(2,1)S(1)} %collective-permute-done.3.refs_1_, bf16[176,1536]{1,0:T(8,128)(2,1)S(1)} %collective-permute-done.4.refs_2_, ...), custom_call_target="tpu_custom_call" | custom-call | flops 1189085184 | bytes 5000000 | tf_op jit(solution)/shard_map/pallas_call | solution.py:47
  29.2 3.9 %shard_map.79 = (f32[672,384]{1,0:T(8,128)S(1)}, f32[672,384]{1,0:T(8,128)S(1)}, bf16[672,768]{1,0:T(8,128)(2,1)S(1)}) custom-call(bf16[336,384]{1,0:T(8,128)(2,1)S(1)} %get-tuple-element.41.refs_0_, bf16[336,384]{1,0:T(8,128)(2,1)S(1)} %get-tuple-element.43.refs_1_, bf16[344,768]{1,0:T(8,128)(2,1)S(1)} %get-tuple-element.42.refs_0_.refs_2_, ...), custom_call_target="tpu_custom_call" | custom-call | flops 2774532096 | bytes 2000000 | tf_op jit(solution)/shard_map/pallas_call | solution.py:47
  33.2 3.6 %collective-permute-done.8.refs_4_ = bf16[344,768]{1,0:T(8,128)(2,1)S(1)} collective-permute-done((bf16[344,768]{1,0:T(8,128)(2,1)S(1)}, bf16[344,768]{1,0:T(8,128)(2,1)S(1)}, u32[]{:S(2)}, u32[]{:S(2)}) %collective-permute-start.8) | collective-permute-done | bytes 528416 | tf_op jit(solution)/shard_map/ppermute | solution.py:96
  39.1 2.1 %shard_map.80 = (f32[672,384]{1,0:T(8,128)S(1)}, f32[672,384]{1,0:T(8,128)S(1)}) custom-call(bf16[672,768]{1,0:T(8,128)(2,1)S(1)} %get-tuple-element.45.refs_0_.refs_1_, f32[672,384]{1,0:T(8,128)S(1)} %get-tuple-element.46.refs_1_, f32[672,384]{1,0:T(8,128)S(1)} %get-tuple-element.47.refs_2_, bf16[344,768]{1,0:T(8,128)(2,1)S(1)} %collective-permute-done.7.refs_3_, ...), custom_call_target="tpu_custom_call" | custom-call | flops 1387266048 | bytes 2000000 | tf_op jit(solution)/shard_map/pallas_call | solution.py:47
  41.2 6.6 %collective-permute-done.1.b_ref.got_ref = f32[168,768]{1,0:T(8,128)S(1)} collective-permute-done((f32[168,768]{1,0:T(8,128)S(1)}, f32[168,768]{1,0:T(8,128)S(1)}, u32[]{:S(2)}, u32[]{:S(2)}) %collective-permute-start.1) | collective-permute-done | bytes 516128 | tf_op jit(solution)/shard_map/ppermute | solution.py:96
  47.9 1.7 %shard_map.82 = (bf16[168,384]{1,0:T(8,128)(2,1)S(1)}, bf16[168,384]{1,0:T(8,128)(2,1)S(1)}, bf16[168,384]{1,0:T(8,128)(2,1)S(1)}) custom-call(f32[168,768]{1,0:T(8,128)S(1)} %shard_map.81.refs_0_, bf16[672,768]{1,0:T(8,128)(2,1)S(1)} %get-tuple-element.45.refs_0_.refs_1_, f32[672,384]{1,0:T(8,128)S(1)} %get-tuple-element.48.after_ref.refs_2_, ...), custom_call_target="tpu_custom_call" | custom-call | flops 1040449536 | bytes 2000000 | tf_op jit(solution)/shard_map/pallas_call | solution.py:47
  49.7 6.3 %collective-permute-start.12 = (bf16[168,384]{1,0:T(8,128)(2,1)S(1)}, bf16[168,384]{1,0:T(8,128)(2,1)S(1)}, u32[]{:S(2)}, u32[]{:S(2)}) collective-permute-start(bf16[168,384]{1,0:T(8,128)(2,1)S(1)} %get-tuple-element.52), channel_id=1, source_target_pairs={{0,12},{1,13},{2,14},{3,15},{4,8},{5,9},{6,10},{7,11},{8,4},{9,5},... | collective-permute-start | bytes 387080 | tf_op jit(solution)/shard_map/ppermute | solution.py:96
  59.3 2.0 %collective-permute-done.13.a3 = bf16[168,384]{1,0:T(8,128)(2,1)S(1)} collective-permute-done((bf16[168,384]{1,0:T(8,128)(2,1)S(1)}, bf16[168,384]{1,0:T(8,128)(2,1)S(1)}, u32[]{:S(2)}, u32[]{:S(2)}) %collective-permute-start.13) | collective-permute-done | bytes 129056 | tf_op jit(solution)/shard_map/ppermute | solution.py:96
  62.5 2.7 %collective-permute-start.14 = (f32[168,768]{1,0:T(8,128)S(1)}, f32[168,768]{1,0:T(8,128)S(1)}, u32[]{:S(2)}, u32[]{:S(2)}) collective-permute-start(f32[168,768]{1,0:T(8,128)S(1)} %shard_map.85.after_ref.refs_2_), channel_id=1, source_target_pairs={{0,16},{1,17},{2,18},{3,19},{4,20},{5,21},{6,22},{7,23},{8,24},{9,... | collective-permute-start | bytes 1548296 | tf_op jit(solution)/shard_map/ppermute | solution.py:96
  65.2 2.5 %collective-permute-start.18 = (f32[168,768]{1,0:T(8,128)S(1)}, f32[168,768]{1,0:T(8,128)S(1)}, u32[]{:S(2)}, u32[]{:S(2)}) collective-permute-start(f32[168,768]{1,0:T(8,128)S(1)} %shard_map.81.refs_0_), channel_id=1, source_target_pairs={{0,96},{1,97},{2,98},{3,99},{4,100},{5,101},{6,102},{7,103},{8,104... | collective-permute-start | bytes 1548296 | tf_op jit(solution)/shard_map/ppermute | solution.py:96
  69.0 1.5 %collective-permute-start.15 = (bf16[168,384]{1,0:T(8,128)(2,1)S(1)}, bf16[168,384]{1,0:T(8,128)(2,1)S(1)}, u32[]{:S(2)}, u32[]{:S(2)}) collective-permute-start(bf16[168,384]{1,0:T(8,128)(2,1)S(1)} %get-tuple-element.56), channel_id=1, source_target_pairs={{0,32},{1,33},{2,34},{3,35},{4,36},{5,37},{6,38},{7,39},{8,40},{9,... | collective-permute-start | bytes 387080 | tf_op jit(solution)/shard_map/ppermute | solution.py:96
  70.5 3.2 %collective-permute-done.16.got_ref.refs_2_.refs_4_ = bf16[168,384]{1,0:T(8,128)(2,1)S(1)} collective-permute-done((bf16[168,384]{1,0:T(8,128)(2,1)S(1)}, bf16[168,384]{1,0:T(8,128)(2,1)S(1)}, u32[]{:S(2)}, u32[]{:S(2)}) %collective-permute-start.16) | collective-permute-done | bytes 129056 | tf_op jit(solution)/shard_map/ppermute | solution.py:96
  74.2 2.3 %collective-permute-done.15.got_ref.refs_2_.refs_5_ = bf16[168,384]{1,0:T(8,128)(2,1)S(1)} collective-permute-done((bf16[168,384]{1,0:T(8,128)(2,1)S(1)}, bf16[168,384]{1,0:T(8,128)(2,1)S(1)}, u32[]{:S(2)}, u32[]{:S(2)}) %collective-permute-start.15) | collective-permute-done | bytes 129056 | tf_op jit(solution)/shard_map/ppermute | solution.py:96
  76.9 2.7 %collective-permute-done.18.far_ref = f32[168,768]{1,0:T(8,128)S(1)} collective-permute-done((f32[168,768]{1,0:T(8,128)S(1)}, f32[168,768]{1,0:T(8,128)S(1)}, u32[]{:S(2)}, u32[]{:S(2)}) %collective-permute-start.18) | collective-permute-done | bytes 516128 | tf_op jit(solution)/shard_map/ppermute | solution.py:96
  80.5 1.9 %collective-permute-done.17.refs_3_.refs_6_ = bf16[168,384]{1,0:T(8,128)(2,1)S(1)} collective-permute-done((bf16[168,384]{1,0:T(8,128)(2,1)S(1)}, bf16[168,384]{1,0:T(8,128)(2,1)S(1)}, u32[]{:S(2)}, u32[]{:S(2)}) %collective-permute-start.17) | collective-permute-done | bytes 129056 | tf_op jit(solution)/shard_map/ppermute | solution.py:96
  83.1 1.6 %collective-permute-start.20 = (f32[168,384]{1,0:T(8,128)S(1)}, f32[168,384]{1,0:T(8,128)S(1)}, u32[]{:S(2)}, u32[]{:S(2)}) collective-permute-start(f32[168,384]{1,0:T(8,128)S(1)} %shard_map.91._), channel_id=1, source_target_pairs={{0,16},{1,17},{2,18},{3,19},{4,20},{5,21},{6,22},{7,23},{8,24},{9,... | collective-permute-start | bytes 774152 | tf_op jit(solution)/shard_map/ppermute | solution.py:96
  86.8 1.4 %final_own.1.refs_0_ = f32[168,1536]{1,0:T(8,128)} custom-call(s32[3]{0:T(128)S(1)} %pad_add_fusion.where_ref.refs_0_, f32[168,384]{1,0:T(8,128)S(1)} %shard_map.92.refs_0_, f32[168,768]{1,0:T(8,128)S(1)} %get-tuple-element.59.refs_1_, f32[168,768]{1,0:T(8,128)S(1)} %shard_map.86.a_ref.after_ref.refs_1_.refs_2_, ...), custom_call_target="tpu_custom_call" | custom-call | flops 258048 | bytes 2000000 | tf_op jit(solution)/shard_map/final_own/pallas_call | solution.py:564
  (51 shorter events, 18.4 us)
Async XLA Ops:
  3.2 10.7 %collective-permute-start.2 = (bf16[176,1536]{1,0:T(8,128)(2,1)S(1)}, bf16[176,1536]{1,0:T(8,128)(2,1)S(1)}, u32[]{:S(2)}, u32[]{:S(2)}) collective-permute-start(bf16[176,1536]{1,0:T(8,128)(2,1)S(1)} %get-tuple-element.40.refs_1_), channel_id=1, source_target_pairs={{0,4},{1,5},{2,6},{3,7},{4,0},{5,1},{6,2},{7,3},{8,12},{9,13},{10,... | collective-permute-start | bytes 1622024 | tf_op jit(solution)/shard_map/ppermute | solution.py:96
  6.5 7.3 %collective-permute-start = (f32[168,768]{1,0:T(8,128)S(1)}, f32[168,768]{1,0:T(8,128)S(1)}, u32[]{:S(2)}, u32[]{:S(2)}) collective-permute-start(f32[168,768]{1,0:T(8,128)S(1)} %get-tuple-element.37.after_ref.give_ref), channel_id=1, source_target_pairs={{0,16},{1,17},{2,18},{3,19},{4,20},{5,21},{6,22},{7,23},{8,24},{9,... | collective-permute-start | bytes 1548296 | tf_op jit(solution)/shard_map/ppermute | solution.py:96
  7.2 18.1 %collective-permute-start.3 = (bf16[176,1536]{1,0:T(8,128)(2,1)S(1)}, bf16[176,1536]{1,0:T(8,128)(2,1)S(1)}, u32[]{:S(2)}, u32[]{:S(2)}) collective-permute-start(bf16[176,1536]{1,0:T(8,128)(2,1)S(1)} %get-tuple-element.40.refs_1_), channel_id=1, source_target_pairs={{0,12},{1,13},{2,14},{3,15},{4,8},{5,9},{6,10},{7,11},{8,4},{9,5},... | collective-permute-start | bytes 1622024 | tf_op jit(solution)/shard_map/ppermute | solution.py:96
  11.0 14.4 %collective-permute-start.4 = (bf16[176,1536]{1,0:T(8,128)(2,1)S(1)}, bf16[176,1536]{1,0:T(8,128)(2,1)S(1)}, u32[]{:S(2)}, u32[]{:S(2)}) collective-permute-start(bf16[176,1536]{1,0:T(8,128)(2,1)S(1)} %get-tuple-element.40.refs_1_), channel_id=1, source_target_pairs={{0,8},{1,9},{2,10},{3,11},{4,12},{5,13},{6,14},{7,15},{8,0},{9,1},... | collective-permute-start | bytes 1622024 | tf_op jit(solution)/shard_map/ppermute | solution.py:96
  15.7 13.5 %collective-permute-start.5 = (bf16[344,768]{1,0:T(8,128)(2,1)S(1)}, bf16[344,768]{1,0:T(8,128)(2,1)S(1)}, u32[]{:S(2)}, u32[]{:S(2)}) collective-permute-start(bf16[344,768]{1,0:T(8,128)(2,1)S(1)} %get-tuple-element.42.refs_0_.refs_2_), channel_id=1, source_target_pairs={{0,1},{1,0},{2,3},{3,2},{4,5},{5,4},{6,7},{7,6},{8,9},{9,8},{10,11... | collective-permute-start | bytes 1585160 | tf_op jit(solution)/shard_map/ppermute | solution.py:96
  16.2 13.0 %collective-permute-start.6 = (bf16[344,768]{1,0:T(8,128)(2,1)S(1)}, bf16[344,768]{1,0:T(8,128)(2,1)S(1)}, u32[]{:S(2)}, u32[]{:S(2)}) collective-permute-start(bf16[344,768]{1,0:T(8,128)(2,1)S(1)} %get-tuple-element.42.refs_0_.refs_2_), channel_id=1, source_target_pairs={{0,3},{1,2},{2,1},{3,0},{4,7},{5,6},{6,5},{7,4},{8,11},{9,10},{10,... | collective-permute-start | bytes 1585160 | tf_op jit(solution)/shard_map/ppermute | solution.py:96
  27.1 9.7 %collective-permute-start.8 = (bf16[344,768]{1,0:T(8,128)(2,1)S(1)}, bf16[344,768]{1,0:T(8,128)(2,1)S(1)}, u32[]{:S(2)}, u32[]{:S(2)}) collective-permute-start(bf16[344,768]{1,0:T(8,128)(2,1)S(1)} %get-tuple-element.44.refs_3_), channel_id=1, source_target_pairs={{0,3},{1,2},{2,1},{3,0},{4,7},{5,6},{6,5},{7,4},{8,11},{9,10},{10,... | collective-permute-start | bytes 1585160 | tf_op jit(solution)/shard_map/ppermute | solution.py:96
  28.3 10.8 %collective-permute-start.7 = (bf16[344,768]{1,0:T(8,128)(2,1)S(1)}, bf16[344,768]{1,0:T(8,128)(2,1)S(1)}, u32[]{:S(2)}, u32[]{:S(2)}) collective-permute-start(bf16[344,768]{1,0:T(8,128)(2,1)S(1)} %get-tuple-element.44.refs_3_), channel_id=1, source_target_pairs={{0,1},{1,0},{2,3},{3,2},{4,5},{5,4},{6,7},{7,6},{8,9},{9,8},{10,11... | collective-permute-start | bytes 1585160 | tf_op jit(solution)/shard_map/ppermute | solution.py:96
  36.8 11.1 %collective-permute-start.9 = (bf16[344,768]{1,0:T(8,128)(2,1)S(1)}, bf16[344,768]{1,0:T(8,128)(2,1)S(1)}, u32[]{:S(2)}, u32[]{:S(2)}) collective-permute-start(bf16[344,768]{1,0:T(8,128)(2,1)S(1)} %collective-permute-done.5.refs_4_), channel_id=1, source_target_pairs={{0,3},{1,2},{2,1},{3,0},{4,7},{5,6},{6,5},{7,4},{8,11},{9,10},{10,... | collective-permute-start | bytes 1585160 | tf_op jit(solution)/shard_map/ppermute | solution.py:96
  37.9 10.0 %collective-permute-start.10 = (bf16[344,768]{1,0:T(8,128)(2,1)S(1)}, bf16[344,768]{1,0:T(8,128)(2,1)S(1)}, u32[]{:S(2)}, u32[]{:S(2)}) collective-permute-start(bf16[344,768]{1,0:T(8,128)(2,1)S(1)} %collective-permute-done.8.refs_4_), channel_id=1, source_target_pairs={{0,1},{1,0},{2,3},{3,2},{4,5},{5,4},{6,7},{7,6},{8,9},{9,8},{10,11... | collective-permute-start | bytes 1585160 | tf_op jit(solution)/shard_map/ppermute | solution.py:96
  37.9 9.9 %collective-permute-start.1 = (f32[168,768]{1,0:T(8,128)S(1)}, f32[168,768]{1,0:T(8,128)S(1)}, u32[]{:S(2)}, u32[]{:S(2)}) collective-permute-start(f32[168,768]{1,0:T(8,128)S(1)} %shard_map.76.refs_0_.a_ref), channel_id=1, source_target_pairs={{0,32},{1,33},{2,34},{3,35},{4,36},{5,37},{6,38},{7,39},{8,40},{9,... | collective-permute-start | bytes 1548296 | tf_op jit(solution)/shard_map/ppermute | solution.py:96
  47.9 10.4 %slice-start = ((s8[4718592]{0:T(1024)(128)(4,1)}), s8[4194304]{0:T(1024)(128)(4,1)S(1)}, s32[]{:S(2)}) async-start(s8[4718592]{0:T(1024)(128)(4,1)} %bitcast.6), calls=%async_computation | async-start | bytes 8388608
  49.6 9.6 %collective-permute-start.11 = (bf16[168,384]{1,0:T(8,128)(2,1)S(1)}, bf16[168,384]{1,0:T(8,128)(2,1)S(1)}, u32[]{:S(2)}, u32[]{:S(2)}) collective-permute-start(bf16[168,384]{1,0:T(8,128)(2,1)S(1)} %get-tuple-element.51.refs_0_), channel_id=1, source_target_pairs={{0,4},{1,5},{2,6},{3,7},{4,0},{5,1},{6,2},{7,3},{8,12},{9,13},{10,... | collective-permute-start | bytes 387080 | tf_op jit(solution)/shard_map/ppermute | solution.py:96
  49.7 9.6 %collective-permute-start.12 = (bf16[168,384]{1,0:T(8,128)(2,1)S(1)}, bf16[168,384]{1,0:T(8,128)(2,1)S(1)}, u32[]{:S(2)}, u32[]{:S(2)}) collective-permute-start(bf16[168,384]{1,0:T(8,128)(2,1)S(1)} %get-tuple-element.52), channel_id=1, source_target_pairs={{0,12},{1,13},{2,14},{3,15},{4,8},{5,9},{6,10},{7,11},{8,4},{9,5},... | collective-permute-start | bytes 387080 | tf_op jit(solution)/shard_map/ppermute | solution.py:96
  56.0 5.3 %collective-permute-start.13 = (bf16[168,384]{1,0:T(8,128)(2,1)S(1)}, bf16[168,384]{1,0:T(8,128)(2,1)S(1)}, u32[]{:S(2)}, u32[]{:S(2)}) collective-permute-start(bf16[168,384]{1,0:T(8,128)(2,1)S(1)} %get-tuple-element.53), channel_id=1, source_target_pairs={{0,8},{1,9},{2,10},{3,11},{4,12},{5,13},{6,14},{7,15},{8,0},{9,1},... | collective-permute-start | bytes 387080 | tf_op jit(solution)/shard_map/ppermute | solution.py:96
  62.5 17.2 %copy-start = (f32[168,1536]{1,0:T(8,128)S(1)}, f32[168,1536]{1,0:T(8,128)}, u32[]{:S(2)}) copy-start(f32[168,1536]{1,0:T(8,128)} %anchor_ref.1) | copy-start | bytes 3096580
  62.5 6.4 %collective-permute-start.14 = (f32[168,768]{1,0:T(8,128)S(1)}, f32[168,768]{1,0:T(8,128)S(1)}, u32[]{:S(2)}, u32[]{:S(2)}) collective-permute-start(f32[168,768]{1,0:T(8,128)S(1)} %shard_map.85.after_ref.refs_2_), channel_id=1, source_target_pairs={{0,16},{1,17},{2,18},{3,19},{4,20},{5,21},{6,22},{7,23},{8,24},{9,... | collective-permute-start | bytes 1548296 | tf_op jit(solution)/shard_map/ppermute | solution.py:96
  65.2 14.4 %collective-permute-start.18 = (f32[168,768]{1,0:T(8,128)S(1)}, f32[168,768]{1,0:T(8,128)S(1)}, u32[]{:S(2)}, u32[]{:S(2)}) collective-permute-start(f32[168,768]{1,0:T(8,128)S(1)} %shard_map.81.refs_0_), channel_id=1, source_target_pairs={{0,96},{1,97},{2,98},{3,99},{4,100},{5,101},{6,102},{7,103},{8,104... | collective-permute-start | bytes 1548296 | tf_op jit(solution)/shard_map/ppermute | solution.py:96
  69.0 4.7 %collective-permute-start.16 = (bf16[168,384]{1,0:T(8,128)(2,1)S(1)}, bf16[168,384]{1,0:T(8,128)(2,1)S(1)}, u32[]{:S(2)}, u32[]{:S(2)}) collective-permute-start(bf16[168,384]{1,0:T(8,128)(2,1)S(1)} %get-tuple-element.57.after_ref), channel_id=1, source_target_pairs={{0,32},{1,33},{2,34},{3,35},{4,36},{5,37},{6,38},{7,39},{8,40},{9,... | collective-permute-start | bytes 387080 | tf_op jit(solution)/shard_map/ppermute | solution.py:96
  69.0 7.4 %collective-permute-start.15 = (bf16[168,384]{1,0:T(8,128)(2,1)S(1)}, bf16[168,384]{1,0:T(8,128)(2,1)S(1)}, u32[]{:S(2)}, u32[]{:S(2)}) collective-permute-start(bf16[168,384]{1,0:T(8,128)(2,1)S(1)} %get-tuple-element.56), channel_id=1, source_target_pairs={{0,32},{1,33},{2,34},{3,35},{4,36},{5,37},{6,38},{7,39},{8,40},{9,... | collective-permute-start | bytes 387080 | tf_op jit(solution)/shard_map/ppermute | solution.py:96
  73.7 8.7 %collective-permute-start.17 = (bf16[168,384]{1,0:T(8,128)(2,1)S(1)}, bf16[168,384]{1,0:T(8,128)(2,1)S(1)}, u32[]{:S(2)}, u32[]{:S(2)}) collective-permute-start(bf16[168,384]{1,0:T(8,128)(2,1)S(1)} %shard_map.88.after_ref), channel_id=1, source_target_pairs={{0,96},{1,97},{2,98},{3,99},{4,100},{5,101},{6,102},{7,103},{8,104... | collective-permute-start | bytes 387080 | tf_op jit(solution)/shard_map/ppermute | solution.py:96
  76.5 8.7 %collective-permute-start.19 = (bf16[168,384]{1,0:T(8,128)(2,1)S(1)}, bf16[168,384]{1,0:T(8,128)(2,1)S(1)}, u32[]{:S(2)}, u32[]{:S(2)}) collective-permute-start(bf16[168,384]{1,0:T(8,128)(2,1)S(1)} %shard_map.89.after_ref._), channel_id=1, source_target_pairs={{0,96},{1,97},{2,98},{3,99},{4,100},{5,101},{6,102},{7,103},{8,104... | collective-permute-start | bytes 387080 | tf_op jit(solution)/shard_map/ppermute | solution.py:96
  83.1 5.2 %collective-permute-start.20 = (f32[168,384]{1,0:T(8,128)S(1)}, f32[168,384]{1,0:T(8,128)S(1)}, u32[]{:S(2)}, u32[]{:S(2)}) collective-permute-start(f32[168,384]{1,0:T(8,128)S(1)} %shard_map.91._), channel_id=1, source_target_pairs={{0,16},{1,17},{2,18},{3,19},{4,20},{5,21},{6,22},{7,23},{8,24},{9,... | collective-permute-start | bytes 774152 | tf_op jit(solution)/shard_map/ppermute | solution.py:96
  85.8 2.5 %collective-permute-start.21 = (f32[168,384]{1,0:T(8,128)S(1)}, f32[168,384]{1,0:T(8,128)S(1)}, u32[]{:S(2)}, u32[]{:S(2)}) collective-permute-start(f32[168,384]{1,0:T(8,128)S(1)} %shard_map.92.refs_0_), channel_id=1, source_target_pairs={{0,16},{1,17},{2,18},{3,19},{4,20},{5,21},{6,22},{7,23},{8,24},{9,... | collective-permute-start | bytes 774152 | tf_op jit(solution)/shard_map/ppermute | solution.py:96
  (1 other events, 10.3 us)
